TPU v7x, 32 devices: a whole 2x2x4 slice. The times are simulated.
32 devices in a mesh: groups: 2 (over x), dp: 2 (over core), tensor: 8 (over z, y).
Axes of the slice: x: 2, y: 2, z: 4, core: 2. Of those that a mesh axis runs over, the one named last changes fastest.
Arguments:
- reward_hidden: bfloat16 [32, 256, 8192], P(('groups', 'dp'), None, 'tensor'), parts along dimension 0, may hold values from -6 to 6
- reward_gain: float32 [8192], P('tensor'), may hold values from 0.5 to 1.5
- reward_head: float32 [8192], P('tensor'), may hold values from -1 to 1
- decode_inputs: bfloat16 [2, 32, 8192], P(None, ('groups', 'dp'), 'tensor'), parts along dimension 1, may hold values from -6 to 6
- attn_gain: float32 [8192], replicated, may hold values from 0.5 to 1.5
- w_query: bfloat16 [8192, 8192], P(None, 'tensor'), may hold values from -0.0625 to 0.0625
- w_keyval: bfloat16 [8192, 2048], P(None, 'tensor'), may hold values from -0.0625 to 0.0625
- w_out: bfloat16 [8192, 8192], P('tensor'), may hold values from -3 to 3
- cache_keys: bfloat16 [32, 2048, 1024], P(('groups', 'dp'), 'tensor'), parts along dimension 0, may hold values from -720 to 720
- cache_values: bfloat16 [32, 2048, 1024], P(('groups', 'dp'), 'tensor'), parts along dimension 0, may hold values from -6 to 6
- lengths: int32 [32], P('groups'), parts along dimension 0, may hold values from 512 to 2048
- slot_map: int32 [32], P('groups'), parts along dimension 0, may hold values from 0 to 15, as said below
Outputs:
- reward: float32 [32], P(('groups', 'dp')), parts along dimension 0
- decoded: bfloat16 [2, 32, 8192], P(None, ('groups', 'dp'), 'tensor'), parts along dimension 1
There are 2 independent parts, one for each index of `groups`. A program takes and returns all parts, laid end to end along the dimension named above; an argument that names none is the same for every part. Nothing has to cross between parts.
Inputs may be any that keep to these rules, and one draw needn't show every extreme that they name: `slot_map`: each aligned block of 8 slots holds exactly 4 survivors, which map to themselves; every other slot maps to a survivor, and every survivor is named by exactly one other slot.
All inputs are finite; a program needn't handle non-finite values.
Results may differ from a plain program's by a relative error of at most 0.0055.
The roundings to bfloat16 on the way count: a program that leaves them out, or rounds other values in their place, can miss the bound.
Values may be sent and summed in bfloat16 or wider, within the bound.
No kernel may reach another device: no remote copies, remote signals or barrier semaphores. Data moves between devices by JAX's collectives and lax.ppermute only.
A program may use at most 128 MiB of HBM per device.

v0:
```python
import jax
import jax.numpy as jnp
from jax import lax
from jax.sharding import PartitionSpec as P

D = 8192
QH = 64
KVH = 8
HD = 128
STEPS = 2


EPS = 1e-05
NEG = -1e30


def fold_sources(parts):
    maxima, totals, sums = parts
    top = jnp.max(maxima, axis=0)
    factor = jnp.exp(maxima - top[None])
    return (top, jnp.sum(factor * totals, axis=0), jnp.sum(factor[..., None] * sums, axis=0))


def local(
    reward_hidden,
    reward_gain,
    reward_head,
    decode_inputs,
    attn_gain,
    w_query,
    w_keyval,
    w_out,
    cache_keys,
    cache_values,
    lengths,
    slot_map,
):
    hidden = reward_hidden.astype(jnp.float32)
    squares = jnp.sum(hidden * hidden, axis=-1)
    head_dot = jnp.sum(hidden * (reward_gain * reward_head), axis=-1)
    squares, head_dot = lax.psum((squares, head_dot), "tensor")
    reward = jnp.mean(head_dot * lax.rsqrt(squares / D + EPS), axis=-1)
    rows = cache_keys.shape[0]
    width = cache_keys.shape[1]
    base = lax.axis_index("dp") * rows
    mine = lax.dynamic_slice_in_dim(slot_map, base, rows)
    every_k, every_v = (
        lax.all_gather(cache_keys, "dp", axis=0, tiled=True),
        lax.all_gather(cache_values, "dp", axis=0, tiled=True),
    )
    keys_now = jnp.take(every_k, mine, axis=0)
    values_now = jnp.take(every_v, mine, axis=0)
    live = jnp.take(lengths, mine, axis=0)
    group = QH // KVH
    heads_dev = w_query.shape[1] // HD
    keys4 = keys_now.reshape(rows, width, KVH, HD)
    values4 = values_now.reshape(rows, width, KVH, HD)
    positions = lax.axis_index("tensor") * width + jnp.arange(width)
    valid = (positions[None, :] < live[:, None])[:, None, None, :]
    head_start = lax.axis_index("tensor") * heads_dev
    kv_index = (head_start + jnp.arange(heads_dev)) // group
    scale = HD ** (-0.5)
    new_keys = []
    new_values = []
    outputs = []
    for step in range(STEPS):
        whole = lax.all_gather(decode_inputs[step], "tensor", axis=1, tiled=True).astype(
            jnp.float32
        )
        normed = (
            whole * lax.rsqrt(jnp.mean(whole * whole, axis=-1, keepdims=True) + EPS) * attn_gain
        ).astype(jnp.bfloat16)
        query_part = jnp.dot(normed, w_query, preferred_element_type=jnp.float32).astype(
            jnp.bfloat16
        )
        kv_part = jnp.dot(normed, w_keyval, preferred_element_type=jnp.float32).astype(jnp.bfloat16)
        query_all, keyval = (
            lax.all_gather(query_part, "tensor", axis=1, tiled=True),
            lax.all_gather(kv_part, "tensor", axis=1, tiled=True),
        )
        query = query_all.reshape(rows, KVH, group, HD)
        keyval = keyval.reshape(rows, 2, KVH, HD)
        new_keys.append(keyval[:, 0])
        new_values.append(keyval[:, 1])
        scores = (
            jnp.einsum("rkgd,rwkd->rkgw", query, keys4, preferred_element_type=jnp.float32) * scale
        )
        scores = jnp.where(valid, scores, NEG)
        block_max = jnp.max(scores, axis=-1)
        expo = jnp.where(valid, jnp.exp(scores - block_max[..., None]), 0.0)
        block_total = jnp.sum(expo, axis=-1).reshape(rows, QH)
        block_acc = jnp.einsum(
            "rkgw,rwkd->rkgd",
            expo.astype(jnp.bfloat16),
            values4,
            preferred_element_type=jnp.float32,
        )
        block_acc = block_acc.reshape(rows, QH, HD)
        block_max = block_max.reshape(rows, QH)
        cache_top, cache_total, cache_acc = fold_sources(
            (
                lax.all_to_all(block_max[None], "tensor", split_axis=2, concat_axis=0, tiled=True),
                lax.all_to_all(
                    block_total[None], "tensor", split_axis=2, concat_axis=0, tiled=True
                ),
                lax.all_to_all(block_acc[None], "tensor", split_axis=2, concat_axis=0, tiled=True),
            )
        )
        query_own = query_part.reshape(rows, heads_dev, HD)
        fresh_k = jnp.take(jnp.stack(new_keys, axis=1), kv_index, axis=2)
        fresh_v = jnp.take(jnp.stack(new_values, axis=1), kv_index, axis=2)
        recent = (
            jnp.einsum("rhd,rjhd->rhj", query_own, fresh_k, preferred_element_type=jnp.float32)
            * scale
        )
        recent_max = jnp.max(recent, axis=-1)
        recent_exp = jnp.exp(recent - recent_max[..., None])
        recent_total = jnp.sum(recent_exp, axis=-1)
        recent_acc = jnp.einsum(
            "rhj,rjhd->rhd",
            recent_exp.astype(jnp.bfloat16),
            fresh_v,
            preferred_element_type=jnp.float32,
        )
        top = jnp.maximum(cache_top, recent_max)
        cache_factor = jnp.exp(cache_top - top)
        recent_factor = jnp.exp(recent_max - top)
        total = cache_factor * cache_total + recent_factor * recent_total
        acc = cache_factor[..., None] * cache_acc + recent_factor[..., None] * recent_acc
        attended = (acc / total[..., None]).astype(jnp.bfloat16).reshape(rows, heads_dev * HD)
        partial_out = jnp.dot(attended, w_out, preferred_element_type=jnp.float32)
        summed = lax.psum_scatter(partial_out, "tensor", scatter_dimension=1, tiled=True)
        outputs.append(summed.astype(jnp.bfloat16))
    return (reward, jnp.stack(outputs, axis=0))


def solution(mesh):
    return jax.shard_map(
        local,
        mesh=mesh,
        in_specs=(
            P(("groups", "dp"), None, "tensor"),
            P("tensor"),
            P("tensor"),
            P(None, ("groups", "dp"), "tensor"),
            P(),
            P(None, "tensor"),
            P(None, "tensor"),
            P("tensor", None),
            P(("groups", "dp"), "tensor", None),
            P(("groups", "dp"), "tensor", None),
            P("groups"),
            P("groups"),
        ),
        out_specs=(P(("groups", "dp")), P(None, ("groups", "dp"), "tensor")),
        check_vma=False,
    )
```

profile of v0, /device:TPU:0, one launch (start us, length us, event | category | flops | bytes accessed | tf_op | source)
XLA Modules:
  0.0 486.0 jit_solution(13673014890106930044)
XLA Ops:
  8.7 32.3 %all-gather = bf16[1,8,8192]{2,1,0:T(8,128)(2,1)S(1)} all-gather(bf16[1,8,1024]{2,1,0:T(8,128)(2,1)S(1)} %get-tuple-element.26), channel_id=2, replica_groups=mesh['groups'=2,'dp'=2,'tensor'=8] {'tensor'}, dimensions={2}, use_global_device_ids=true | all-gather | bytes 147456 | tf_op jit(solution)/shard_map/all_gather | solution.py:67
  41.2 3.5 convolution_convert_fusion.3
  44.8 30.6 %all_gather.27 = bf16[8,2048]{1,0:T(8,128)(2,1)S(1)} all-gather(bf16[8,256]{1,0:T(8,128)(2,1)S(1)} %convolution_convert_fusion.3), channel_id=1, replica_groups=mesh['groups'=2,'dp'=2,'tensor'=8] {'tensor'}, dimensions={1}, use_global_device_ids=true | all-gather | bytes 36864 | tf_op jit(solution)/shard_map/all_gather | solution.py:79
  76.0 8.2 %fusion.61 = (f32[8,8]{0,1:T(8,128)S(1)}, bf16[8,1024]{1,0:T(8,128)(2,1)S(1)}) fusion(bf16[8,8,128]{2,1,0:T(8,128)(2,1)S(1)} %gather_fusion.2, pred[8]{0:T(512)(128)(4,1)S(1)} %compare_and_fusion, bf16[8192,1024]{1,0:T(8,128)(2,1)} %param.23, bf16[1,8,8192]{2,1,0:T(8,128)(2,1)S(1)} %all-gather, f32[8192]{0:T(1024)S(1)} %copy-done.2, f32[8]{0:T(128)S(1)} %add_rsqrt_fusion.1), kind=kOutput, calls=%fused_computation.78 | convolution fusion | flops 134528960 | bytes 16974120 | tf_op jit(solution)/shard_map/dot_general | solution.py:73
  84.8 30.5 %all-gather.1 = bf16[1,8,8192]{2,1,0:T(8,128)(2,1)S(1)} all-gather(bf16[1,8,1024]{2,1,0:T(8,128)(2,1)S(1)} %get-tuple-element.27), channel_id=3, replica_groups=mesh['groups'=2,'dp'=2,'tensor'=8] {'tensor'}, dimensions={2}, use_global_device_ids=true | all-gather | bytes 147456 | tf_op jit(solution)/shard_map/all_gather | solution.py:67
  118.4 30.6 %all_gather.31 = bf16[8,2048]{1,0:T(8,128)(2,1)S(1)} all-gather(bf16[8,256]{1,0:T(8,128)(2,1)S(1)} %convolution_convert_fusion.2), channel_id=1, replica_groups=mesh['groups'=2,'dp'=2,'tensor'=8] {'tensor'}, dimensions={1}, use_global_device_ids=true | all-gather | bytes 36864 | tf_op jit(solution)/shard_map/all_gather | solution.py:79
  150.3 8.1 %convolution_convert_fusion = bf16[8,1024]{1,0:T(8,128)(2,1)S(1)} fusion(bf16[8192,1024]{1,0:T(8,128)(2,1)} %param.23, bf16[1,8,8192]{2,1,0:T(8,128)(2,1)S(1)} %all-gather.1, f32[8]{0:T(128)S(1)} %add_rsqrt_fusion, f32[8192]{0:T(1024)S(1)} %copy-done.2), kind=kOutput, calls=%fused_computation.31 | convolution fusion | flops 134488064 | bytes 16957472 | tf_op jit(solution)/shard_map/dot_general | solution.py:73
  159.8 3.6 fusion.1
  163.5 37.1 %all-reduce = (f32[8,256]{1,0:T(8,128)S(1)}, f32[8,256]{1,0:T(8,128)S(1)}) all-reduce(f32[8,256]{1,0:T(8,128)S(1)} %get-tuple-element.6, f32[8,256]{1,0:T(8,128)S(1)} %get-tuple-element.4), channel_id=1, replica_groups=mesh['groups'=2,'dp'=2,'tensor'=8] {'tensor'}, use_global_device_ids=true, to_apply=%region_1.0 | all-reduce | flops 4096 | bytes 32768 | tf_op jit(solution)/shard_map/psum | solution.py:41
  200.5 30.5 %all_gather.30 = bf16[8,8192]{1,0:T(8,128)(2,1)S(1)} all-gather(bf16[8,1024]{1,0:T(8,128)(2,1)S(1)} %convolution_convert_fusion), channel_id=1, replica_groups=mesh['groups'=2,'dp'=2,'tensor'=8] {'tensor'}, dimensions={1}, use_global_device_ids=true | all-gather | bytes 147456 | tf_op jit(solution)/shard_map/all_gather | solution.py:78
  231.0 30.7 %all_gather.25 = bf16[8,8192]{1,0:T(8,128)(2,1)S(1)} all-gather(bf16[8,1024]{1,0:T(8,128)(2,1)S(1)} %get-tuple-element.43), channel_id=1, replica_groups=mesh['groups'=2,'dp'=2,'tensor'=8] {'tensor'}, dimensions={1}, use_global_device_ids=true | all-gather | bytes 147456 | tf_op jit(solution)/shard_map/all_gather | solution.py:78
  262.0 6.1 %gather_fusion.1 = bf16[8,256,1024]{2,1,0:T(8,128)(2,1)} fusion(bf16[16,256,1024]{2,1,0:T(8,128)(2,1)} %all-gather.5.cloned.1.call-done, s32[1024]{0:T(1024)S(1)} %pad_clamp_fusion.1), kind=kCustom, calls=%fused_computation.clone | custom fusion | bytes 8388640 | tf_op jit(solution)/shard_map/jit(_take)/gather | solution.py:51
  268.2 6.2 %gather_fusion.3 = bf16[8,256,1024]{2,1,0:T(8,128)(2,1)} fusion(bf16[16,256,1024]{2,1,0:T(8,128)(2,1)} %all-gather.7.cloned.1.call-done, s32[1024]{0:T(1024)S(1)} %pad_clamp_fusion.1), kind=kCustom, calls=%fused_computation.3.clone | custom fusion | bytes 8388640 | tf_op jit(solution)/shard_map/jit(_take)/gather | solution.py:52
  274.3 6.2 %select_bitcast_fusion.1 = (bf16[8,32,8,8,128]{4,3,2,1,0:T(8,128)(2,1)S(1)}, bf16[8,32,8,8,128]{4,3,2,1,0:T(8,128)(2,1)}) fusion(bf16[8,256,1024]{2,1,0:T(8,128)(2,1)} %gather_fusion.1, pred[8]{0:T(512)(128)(4,1)S(1)} %get-tuple-element.18, bf16[8,256,1024]{2,1,0:T(8,128)(2,1)} %gather_fusion.3), kind=kLoop, calls=%fused_computation.20 | loop fusion | flops 4194304 | bytes 16777224
  303.9 5.4 %all-to-all-start.5 = ((f32[1,8,64]{1,0,2:T(1,128)}), f32[1,8,64]{1,0,2:T(1,128)S(1)}, u32[]{:S(2)}, u32[]{:S(2)}) async-start(f32[1,8,64]{1,0,2:T(1,128)} %bitcast.47), calls=%async_computation.6 | async-start | bytes 65536 | tf_op jit(solution)/shard_map/all_to_all | solution.py:103
  309.4 6.6 %all-to-all-done.5 = f32[1,8,64]{1,0,2:T(1,128)S(1)} async-done(((f32[1,8,64]{1,0,2:T(1,128)}), f32[1,8,64]{1,0,2:T(1,128)S(1)}, u32[]{:S(2)}, u32[]{:S(2)}) %all-to-all-start.5) | async-done | bytes 2080 | tf_op jit(solution)/shard_map/all_to_all | solution.py:103
  319.4 6.6 %all-to-all-done.3 = f32[1,8,64]{1,0,2:T(1,128)S(1)} async-done(((f32[1,8,64]{1,0,2:T(1,128)}), f32[1,8,64]{1,0,2:T(1,128)S(1)}, u32[]{:S(2)}, u32[]{:S(2)}) %all-to-all-start.3) | async-done | bytes 2080 | tf_op jit(solution)/shard_map/all_to_all | solution.py:102
  325.9 3.4 all-to-all-start.1
  329.7 7.8 %all-to-all-done.1 = f32[1,8,64,128]{3,1,0,2:T(8,128)S(1)} async-done(((f32[1,8,64,128]{3,1,0,2:T(8,128)}), f32[1,8,64,128]{3,1,0,2:T(8,128)S(1)}, u32[]{:S(2)}, u32[]{:S(2)}) %all-to-all-start.1) | async-done | bytes 262176 | tf_op jit(solution)/shard_map/all_to_all | solution.py:106
  337.5 3.4 all-to-all-start.4
  341.1 8.8 %fusion.75 = f32[8,8192]{1,0:T(8,128)} fusion(bf16[1024,8192]{1,0:T(8,128)(2,1)} %param.25, f32[8,8,128]{2,1,0:T(8,128)S(1)} %fusion.44, bf16[8,8,128]{2,1,0:T(8,128)(2,1)S(1)} %gather_fusion.4, f32[8,8]{0,1:T(8,128)S(1)} %copy.125, f32[8,8]{0,1:T(8,128)S(1)} %copy.122, f32[8,8]{0,1:T(8,128)S(1)} %copy.121, f32[8,8]{0,1:T(8,128)S(1)} %copy.116, ...), kind=kOutput, calls=%fused_computation.96 | convolution fusion | flops 134283264 | bytes 17089544 | tf_op jit(solution)/shard_map/dot_general | solution.py:131
  350.2 8.8 %fusion.73 = f32[8,8192]{1,0:T(8,128)} fusion(bf16[1024,8192]{1,0:T(8,128)(2,1)} %param.25, f32[8,8,1,128]{3,2,1,0:T(1,128)S(1)} %fusion.63, f32[8,8,128]{2,0,1:T(8,128)S(1)} %multiply_reduce_fusion, f32[8,8]{0,1:T(8,128)S(1)} %get-tuple-element.13, f32[8,8]{0,1:T(8,128)S(1)} %get-tuple-element.15, f32[8,8]{0,1:T(8,128)S(1)} %get-tuple-element.14), kind=kOutput, calls=%fused_computation.94 | convolution fusion | flops 134258688 | bytes 17105664 | tf_op jit(solution)/shard_map/dot_general | solution.py:131
  359.6 53.8 %reduce-scatter.3.cloned.1.call-done = f32[8,1024]{1,0:T(8,128)} async-done(((f32[8,8192]{1,0:T(8,128)}), f32[8,1024]{1,0:T(8,128)}) %reduce-scatter.3.cloned.1.call-update) | async-done | bytes 32784 | tf_op jit(solution)/shard_map/reduce_scatter | solution.py:132
  414.2 63.9 %reduce-scatter.5.cloned.1.call-done = f32[8,1024]{1,0:T(8,128)} async-done(((f32[8,8192]{1,0:T(8,128)}), f32[8,1024]{1,0:T(8,128)}) %reduce-scatter.5.cloned.1.call-update) | async-done | bytes 32784 | tf_op jit(solution)/shard_map/reduce_scatter | solution.py:132
  (93 shorter events, 39.1 us)
Async XLA Ops:
  7.2 152.0 %copy-start = (s32[16]{0:T(128)S(1)}, s32[16]{0:T(128)}, u32[]{:S(2)}) copy-start(s32[16]{0:T(128)} %param.28) | copy-start | bytes 196
  7.2 1.5 copy-start.3
  7.2 34.1 %copy-start.2 = (f32[8192]{0:T(1024)S(1)}, f32[8192]{0:T(1024)}, u32[]{:S(2)}) copy-start(f32[8192]{0:T(1024)} %param.22) | copy-start | bytes 98308
  7.2 254.8 %all-gather.5.cloned.1.call-start = ((), (), s32[]{:S(2)}) async-start(), calls=%async_computation.8 | async-start | bytes 12582912 | tf_op jit(solution)/shard_map/all_gather | solution.py:48
  7.9 260.2 %all-gather.7.cloned.1.call-start = ((), (), s32[]{:S(2)}) async-start(), calls=%async_computation.9 | async-start | bytes 12582912 | tf_op jit(solution)/shard_map/all_gather | solution.py:49
  150.3 8.8 %copy-start.6 = (s32[16]{0:T(128)S(1)}, s32[16]{0:T(128)}, u32[]{:S(2)}) copy-start(s32[16]{0:T(128)} %param.29) | copy-start | bytes 196
  150.3 9.5 %copy-start.4 = (f32[1024]{0:T(1024)S(1)}, f32[1024]{0:T(1024)}, u32[]{:S(2)}) copy-start(f32[1024]{0:T(1024)} %param.19) | copy-start | bytes 12292
  150.3 9.5 %copy-start.5 = (f32[1024]{0:T(1024)S(1)}, f32[1024]{0:T(1024)}, u32[]{:S(2)}) copy-start(f32[1024]{0:T(1024)} %param.20) | copy-start | bytes 12292
  283.8 10.1 %all-to-all-start = ((f32[1,8,64]{1,0,2:T(1,128)}), f32[1,8,64]{1,0,2:T(1,128)S(1)}, u32[]{:S(2)}, u32[]{:S(2)}) async-start(f32[1,8,64]{1,0,2:T(1,128)} %bitcast.3), calls=%async_computation | async-start | bytes 65536 | tf_op jit(solution)/shard_map/all_to_all | solution.py:102
  293.9 10.0 %all-to-all-start.2 = ((f32[1,8,64]{1,0,2:T(1,128)}), f32[1,8,64]{1,0,2:T(1,128)S(1)}, u32[]{:S(2)}, u32[]{:S(2)}) async-start(f32[1,8,64]{1,0,2:T(1,128)} %bitcast.21), calls=%async_computation.2 | async-start | bytes 65536 | tf_op jit(solution)/shard_map/all_to_all | solution.py:103
  303.9 12.1 %all-to-all-start.5 = ((f32[1,8,64]{1,0,2:T(1,128)}), f32[1,8,64]{1,0,2:T(1,128)S(1)}, u32[]{:S(2)}, u32[]{:S(2)}) async-start(f32[1,8,64]{1,0,2:T(1,128)} %bitcast.47), calls=%async_computation.6 | async-start | bytes 65536 | tf_op jit(solution)/shard_map/all_to_all | solution.py:103
  316.0 10.0 %all-to-all-start.3 = ((f32[1,8,64]{1,0,2:T(1,128)}), f32[1,8,64]{1,0,2:T(1,128)S(1)}, u32[]{:S(2)}, u32[]{:S(2)}) async-start(f32[1,8,64]{1,0,2:T(1,128)} %bitcast.30), calls=%async_computation.4 | async-start | bytes 65536 | tf_op jit(solution)/shard_map/all_to_all | solution.py:102
  325.9 11.6 %all-to-all-start.1 = ((f32[1,8,64,128]{3,1,0,2:T(8,128)}), f32[1,8,64,128]{3,1,0,2:T(8,128)S(1)}, u32[]{:S(2)}, u32[]{:S(2)}) async-start(f32[1,8,64,128]{3,1,0,2:T(8,128)} %copy.118), calls=%async_computation.1 | async-start | bytes 524288 | tf_op jit(solution)/shard_map/all_to_all | solution.py:106
  337.5 12.5 %all-to-all-start.4 = ((f32[1,8,64,128]{3,1,0,2:T(8,128)}), f32[1,8,64,128]{3,1,0,2:T(8,128)S(1)}, u32[]{:S(2)}, u32[]{:S(2)}) async-start(f32[1,8,64,128]{3,1,0,2:T(8,128)} %copy.131), calls=%async_computation.5 | async-start | bytes 524288 | tf_op jit(solution)/shard_map/all_to_all | solution.py:106
  340.9 72.5 %reduce-scatter.3.cloned.1.call-start = ((), (), s32[]{:S(2)}) async-start(), calls=%async_computation.10 | async-start | bytes 294912 | tf_op jit(solution)/shard_map/reduce_scatter | solution.py:132
  349.9 128.2 %reduce-scatter.5.cloned.1.call-start = ((), (), s32[]{:S(2)}) async-start(), calls=%async_computation.11 | async-start | bytes 294912 | tf_op jit(solution)/shard_map/reduce_scatter | solution.py:132
  350.1 129.3 %copy-start.1 = (s32[16]{0:T(128)S(1)}, s32[16]{0:T(128)}, u32[]{:S(2)}) copy-start(s32[16]{0:T(128)} %param.28) | copy-start | bytes 196
Sparse Core Ops, SparseCore 0:
  9.5 22.5 all-gather.4
  33.7 21.0 all-gather.6
  350.1 63.3 reduce-scatter.2
  416.6 61.4 reduce-scatter.4
where the time goes:
time: 487 us; the launch traced here: 486 us
  blocking collectives  222 us (46%)
  waiting for transfers between devices  143 us (29%)
  matrix products  49 us (10%)
  starting transfers between devices  22.4 us (5%)
  local copies, waits for them, and re-layouts  20.7 us (4%)
  other arithmetic  14.1 us (3%)
  between operations  14.1 us (3%)
    reduce_scatter x2, waiting for transfers between devices, local(): lax.psum_scatter(partial_out, 'tensor', scatter_dimension=1, tiled=True)  118 us
    all_gather x2, blocking collectives, local(): lax.all_gather(decode_inputs[step], 'tensor', axis=1, tiled=True)  62.9 us
    all_gather x2, blocking collectives, local(): lax.all_gather(kv_part, 'tensor', axis=1, tiled=True)  61.2 us
    all_gather x2, blocking collectives, local(): lax.all_gather(query_part, 'tensor', axis=1, tiled=True)  61.2 us
    psum x1, blocking collectives, local(): squares, head_dot = lax.psum((squares, head_dot), 'tensor')  37.1 us
    dot_general x2, matrix products, local(): partial_out = jnp.dot(attended, w_out, preferred_element_type=jnp.float32)  17.6 us
    dot_general x2, matrix products, local(): jnp.dot(normed, w_query, preferred_element_type=jnp.float32)  16.2 us
  transfers between devices with their start and end apart: 10, of which 7 were waited for; matrix products, arithmetic and copies ran while one was open for 14% of the time, Pallas kernels for 0%

commit v1 on v0

v1 whole, which is shorter than its diff:
```python
import functools

import jax
import jax.numpy as jnp
from jax import lax
from jax.experimental import pallas as pl
from jax.experimental.pallas import tpu as pltpu
from jax.sharding import PartitionSpec as P

HD = 128
KVH = 8
STEPS = 2
PAIR = 2
LANES = 128
EXT = 8
EPS = 1e-05
NEG = -1e30
SCALE = HD ** (-0.5)
NT = (((1,), (1,)), ((), ()))
TN = (((0,), (0,)), ((), ()))


def iota(shape, dim):
    return lax.broadcasted_iota(jnp.int32, shape, dim)


def dot(a, b, dims=(((1,), (0,)), ((), ()))):
    return lax.dot_general(a, b, dims, preferred_element_type=jnp.float32)


def head_major(shape, pages, per_page, heads):
    o, s = iota(shape, 0), iota(shape, 1)
    row = o % per_page
    head = (o // per_page) % heads
    page = o // (per_page * heads)
    return (s == (head * pages + page) * per_page + row).astype(jnp.bfloat16)


def project_kernel(pages, per_page, width, x_ref, gain_ref, wq_ref, wkv_ref, out_ref, inv, accq, acckv):
    n = pl.program_id(0)
    chunks, rows, depth = x_ref.shape

    @pl.when(n == 0)
    def _():
        total = jnp.zeros((rows, depth), jnp.float32)
        for chunk in range(chunks):
            part = x_ref[chunk].astype(jnp.float32)
            total = total + part * part
        mean = jnp.sum(total, axis=-1, keepdims=True) / width
        inv[...] = jnp.broadcast_to(lax.rsqrt(mean + EPS), inv.shape)
        accq[...] = jnp.zeros_like(accq)
        acckv[...] = jnp.zeros_like(acckv)

    normed = (x_ref[n].astype(jnp.float32) * inv[:, :1] * gain_ref[0]).astype(jnp.bfloat16)
    accq[...] += dot(normed, wq_ref[...])
    acckv[...] += dot(normed, wkv_ref[...])

    @pl.when(n == chunks - 1)
    def _():
        heads = accq.shape[1] // HD
        query = accq[...].astype(jnp.bfloat16)
        stacked = jnp.concatenate([query[:, h * HD : (h + 1) * HD] for h in range(heads)], axis=0)
        order = head_major((rows * heads, rows * heads), pages, per_page, heads)
        query = dot(order, stacked).astype(jnp.bfloat16)
        pieces = [query]
        columns = acckv.shape[1]
        keyval = acckv[...].astype(jnp.bfloat16)
        if columns < LANES:
            keyval = jnp.concatenate(
                [keyval, jnp.zeros((rows, LANES - columns), jnp.bfloat16)], axis=1
            )
        for v in range(keyval.shape[1] // LANES):
            pieces.append(keyval[:, v * LANES : (v + 1) * LANES])
        packed = jnp.concatenate(pieces, axis=0)
        for device in range(out_ref.shape[0]):
            out_ref[device] = packed


def attend_kernel(page_rows, meta_ref, q_ref, k_ref, v_ref, reward_ref, out_ref, spread):
    i = pl.program_id(0)
    pages = pl.num_programs(0)
    width = k_ref.shape[1]
    span = KVH * page_rows
    body = out_ref.shape[1] - 2 * EXT

    @pl.when(i == 0)
    def _():
        spread[...] = jnp.zeros_like(spread)
        if reward_ref.shape[0] == KVH:
            out_ref[:, body + EXT :, :] = reward_ref[...]
        else:
            out_ref[:, body + EXT :, :] = jnp.zeros((KVH, EXT, LANES), jnp.float32)

    start = pl.multiple_of(i * page_rows, page_rows)
    for k in range(KVH):
        spread[k * page_rows : (k + 1) * page_rows, k * HD : (k + 1) * HD] = q_ref[
            k, pl.ds(start, page_rows), :
        ]
    scores = dot(k_ref[0], spread[...], NT) * SCALE
    valid = meta_ref[2 * pages] + iota((width, span), 0) < meta_ref[pages + i]
    scores = jnp.where(valid, scores, NEG)
    top = jnp.max(scores, axis=0, keepdims=True)
    expo = jnp.where(valid, jnp.exp(scores - top), 0.0)
    total = jnp.sum(expo, axis=0, keepdims=True)
    acc = dot(expo.astype(jnp.bfloat16), v_ref[0], TN)
    for k in range(KVH):
        out_ref[k, pl.ds(start, page_rows), :] = acc[
            k * page_rows : (k + 1) * page_rows, k * HD : (k + 1) * HD
        ]
        lane = (k * page_rows) // LANES * LANES
        out_ref[k, pl.ds(body + i, 1), :] = top[:, lane : lane + LANES]
        out_ref[k, pl.ds(body + pages + i, 1), :] = total[:, lane : lane + LANES]


def merge_kernel(pages, per_page, width, span, meta_ref, part_ref, q_ref, fk_ref, fv_ref, w_ref, out_ref, att, mean):
    n = pl.program_id(0)
    chunks = part_ref.shape[0]
    body = part_ref.shape[1] - 2 * EXT
    page_rows = body // pages
    heads = page_rows // per_page
    rows = pages * per_page

    @pl.when(n == 0)
    def _():
        query = q_ref[0, :body, :]
        recent = dot(query, fk_ref[...], NT) * SCALE
        line, col = iota(recent.shape, 0), iota(recent.shape, 1)
        mine = (line // page_rows) * per_page + line % per_page
        seen = (mine // STEPS == col // STEPS) & (col <= mine)
        recent = jnp.where(seen, recent, NEG)
        recent_max = jnp.max(recent, axis=-1, keepdims=True)
        recent_exp = jnp.where(seen, jnp.exp(recent - recent_max), 0.0)
        recent_total = jnp.sum(recent_exp, axis=-1, keepdims=True)
        recent_acc = dot(recent_exp.astype(jnp.bfloat16), fv_ref[...])

        maxima = [part_ref[b, body : body + pages, :] for b in range(chunks)]
        totals = [part_ref[b, body + pages : body + 2 * pages, :] for b in range(chunks)]
        top = functools.reduce(jnp.maximum, maxima)
        factors = [jnp.exp(m - top) for m in maxima]
        total = functools.reduce(jnp.add, [f * t for f, t in zip(factors, totals)])

        line, lane = iota((page_rows, LANES), 0), iota((page_rows, LANES), 1)
        pick = lane == line + meta_ref[0]

        def column(packed):
            return jnp.concatenate(
                [
                    jnp.sum(
                        jnp.where(pick, jnp.broadcast_to(packed[i : i + 1], pick.shape), 0.0),
                        axis=-1,
                        keepdims=True,
                    )
                    for i in range(pages)
                ],
                axis=0,
            )

        acc = jnp.zeros((body, HD), jnp.float32)
        for b in range(chunks):
            acc = acc + column(factors[b]) * part_ref[b, :body, :]
        cache_top, cache_total = column(top), column(total)
        top = jnp.maximum(cache_top, recent_max)
        cache_factor = jnp.exp(cache_top - top)
        recent_factor = jnp.exp(recent_max - top)
        total = cache_factor * cache_total + recent_factor * recent_total
        acc = cache_factor * acc + recent_factor * recent_acc
        attended = (acc / total).astype(jnp.bfloat16)
        order = head_major((body, body), pages, per_page, heads)
        attended = dot(order, attended, TN).astype(jnp.bfloat16)
        for h in range(heads):
            att[:, h * HD : (h + 1) * HD] = attended[h * rows : (h + 1) * rows]

        tile = functools.reduce(jnp.add, [part_ref[b, body + EXT :, :] for b in range(chunks)])
        used = EXT // 2
        value = tile[used:] * lax.rsqrt(tile[:used] / width + EPS)
        mean[...] = jnp.broadcast_to(jnp.sum(value, keepdims=True) / span, mean.shape)

    product = dot(att[...], w_ref[...])
    for c in range(w_ref.shape[1] // LANES):
        out_ref[0, c * rows : (c + 1) * rows, :] = product[:, c * LANES : (c + 1) * LANES]
    out_ref[0, out_ref.shape[1] - EXT :, :] = jnp.where(
        iota((EXT, LANES), 0) == meta_ref[1], mean[...], 0.0
    )


def sum_kernel(rows, part_ref, out_ref, reward_ref):
    total = part_ref[0]
    for b in range(1, part_ref.shape[0]):
        total = total + part_ref[b]
    for c in range(out_ref.shape[1] // LANES):
        out_ref[:, c * LANES : (c + 1) * LANES] = total[c * rows : (c + 1) * rows].astype(
            jnp.bfloat16
        )
    reward_ref[...] = total[total.shape[0] - EXT :]


def whole(shape):
    return pl.BlockSpec(shape, lambda *_: (0,) * len(shape))


def exchange(x):
    return lax.all_to_all(x, "tensor", 0, 0, tiled=True)


def local(
    chunks,
    reward_hidden,
    reward_gain,
    reward_head,
    decode_inputs,
    attn_gain,
    w_query,
    w_keyval,
    w_out,
    cache_keys,
    cache_values,
    lengths,
    slot_map,
):
    slots, width = cache_keys.shape[:2]
    depth, qcols = w_query.shape
    kvcols = w_keyval.shape[1]
    part = decode_inputs.shape[-1]
    heads = qcols // HD
    group = heads * chunks // KVH
    split = group // heads
    pages = slots // PAIR
    per_page = PAIR * STEPS
    page_rows = per_page * group
    rows = slots * STEPS
    body = rows * heads
    mine, index = lax.axis_index("dp"), lax.axis_index("tensor")
    swap = [(0, 1), (1, 0)]

    ids = jnp.arange(slot_map.shape[0])
    kept = slot_map == ids
    home = slot_map // slots
    before = kept[None, :] & (ids[None, :] // slots == home[:, None]) & (ids[None, :] < slot_map[:, None])
    place = home * slots + PAIR * jnp.sum(before, axis=1) + (slot_map != ids)
    place_own = lax.dynamic_slice_in_dim(place, mine * slots, slots)
    place_far = lax.dynamic_slice_in_dim(place, (1 - mine) * slots, slots)
    lead = place[None, :] == (mine * slots + PAIR * jnp.arange(pages))[:, None]
    page = jnp.sum(jnp.where(lead, ids[None, :], 0), axis=1) - mine * slots
    live = jnp.sum(jnp.where(lead, lengths[None, :], 0), axis=1)
    work = jnp.arange(rows)
    steps = jnp.arange(STEPS)
    both = jnp.stack([place_own, place_far]) - mine * slots
    take = (both[None, None, :, None, :] == jnp.arange(slots)[:, None, None, None, None]) & (
        steps[None, :, None, None, None] == steps[None, None, None, :, None]
    )
    take = take.reshape(rows, 2 * rows).astype(jnp.bfloat16)
    bases = jnp.stack([mine, 1 - mine]) * slots
    give = (
        (place_own[None, :, None] - bases[None, None, :])[..., None, None]
        == jnp.arange(slots)[None, None, None, :, None]
    ) & (steps[:, None, None, None, None] == steps[None, None, None, None, :])
    give = give.reshape(rows, 2 * rows).astype(jnp.bfloat16)

    own = decode_inputs.reshape(rows, part)
    far = lax.ppermute(own, "dp", swap)
    tokens = dot(take, jnp.concatenate([own, far], axis=0)).astype(jnp.bfloat16)
    tokens = exchange(jnp.broadcast_to(tokens[None], (chunks, rows, part)))

    hidden = reward_hidden.astype(jnp.float32)
    squares = jnp.sum(hidden * hidden, axis=-1)
    head_dot = jnp.sum(hidden * (reward_gain * reward_head), axis=-1)
    span = squares.shape[1]

    def tile(values):
        values = values.reshape(chunks, -1)
        size = EXT // 2 * LANES
        return jnp.pad(values, ((0, 0), (0, size - values.shape[1]))).reshape(
            chunks, EXT // 2, LANES
        )

    reward_parts = jnp.concatenate([tile(squares), tile(head_dot)], axis=1)

    kv_rows = max(kvcols // LANES, 1) * rows
    packed = pl.pallas_call(
        functools.partial(project_kernel, pages, per_page, depth),
        grid=(chunks,),
        in_specs=[
            whole((chunks, rows, part)),
            pl.BlockSpec((1, 1, part), lambda n: (n, 0, 0)),
            pl.BlockSpec((part, qcols), lambda n: (n, 0)),
            pl.BlockSpec((part, kvcols), lambda n: (n, 0)),
        ],
        out_specs=whole((chunks, body + kv_rows, LANES)),
        out_shape=jax.ShapeDtypeStruct((chunks, body + kv_rows, LANES), jnp.bfloat16),
        scratch_shapes=[
            pltpu.VMEM((rows, LANES), jnp.float32),
            pltpu.VMEM((rows, qcols), jnp.float32),
            pltpu.VMEM((rows, kvcols), jnp.float32),
        ],
        name="project",
    )(tokens, attn_gain.reshape(chunks, 1, part), w_query, w_keyval)
    gathered = exchange(packed)

    fresh = gathered[:, body:]
    if kvcols < LANES:
        fresh = fresh[..., :kvcols].transpose(1, 0, 2).reshape(rows, 2 * KVH, HD).transpose(1, 0, 2)
    else:
        fresh = fresh.reshape(2 * KVH, rows, HD)
    kv_head = index * heads // group
    fresh_k = lax.dynamic_index_in_dim(fresh, kv_head, 0, keepdims=False)
    fresh_v = lax.dynamic_index_in_dim(fresh, KVH + kv_head, 0, keepdims=False)
    queries = gathered
    if split > 1:
        queries = (
            gathered[:, :body]
            .reshape(KVH, split, pages, heads * per_page, HD)
            .transpose(0, 2, 1, 3, 4)
            .reshape(KVH, pages * page_rows, HD)
        )

    meta = jnp.concatenate([page, live, (index * width)[None]]).astype(jnp.int32)
    big = pages * page_rows
    pieces = pl.pallas_call(
        functools.partial(attend_kernel, page_rows),
        grid_spec=pltpu.PrefetchScalarGridSpec(
            num_scalar_prefetch=1,
            grid=(pages,),
            in_specs=[
                pl.BlockSpec(queries.shape, lambda i, m: (0, 0, 0)),
                pl.BlockSpec((1, width, KVH * HD), lambda i, m: (m[i], 0, 0)),
                pl.BlockSpec((1, width, KVH * HD), lambda i, m: (m[i], 0, 0)),
                pl.BlockSpec(reward_parts.shape, lambda i, m: (0, 0, 0)),
            ],
            out_specs=pl.BlockSpec((KVH, big + 2 * EXT, HD), lambda i, m: (0, 0, 0)),
            scratch_shapes=[pltpu.VMEM((KVH * page_rows, KVH * HD), jnp.bfloat16)],
        ),
        out_shape=jax.ShapeDtypeStruct((KVH, big + 2 * EXT, HD), jnp.float32),
        name="attend",
    )(meta, queries, cache_keys, cache_values, reward_parts)
    if split > 1:
        acc = (
            pieces[:, :big]
            .reshape(KVH, pages, split, heads * per_page, HD)
            .transpose(0, 2, 1, 3, 4)
            .reshape(chunks, body, HD)
        )
        extra = jnp.repeat(pieces[:, big : big + EXT], split, axis=0)
        pieces = jnp.concatenate([acc, extra, reward_parts], axis=1)
    pieces = exchange(pieces)

    chunk_rows = part // LANES * rows + EXT
    own_row = index * (slots * span // chunks) // span
    meta = jnp.stack([(index * heads * per_page) % LANES, own_row]).astype(jnp.int32)
    partial = pl.pallas_call(
        functools.partial(merge_kernel, pages, per_page, depth, span),
        grid_spec=pltpu.PrefetchScalarGridSpec(
            num_scalar_prefetch=1,
            grid=(chunks,),
            in_specs=[
                pl.BlockSpec(pieces.shape, lambda n, m: (0, 0, 0)),
                pl.BlockSpec((1,) + packed.shape[1:], lambda n, m: (0, 0, 0)),
                pl.BlockSpec((rows, HD), lambda n, m: (0, 0)),
                pl.BlockSpec((rows, HD), lambda n, m: (0, 0)),
                pl.BlockSpec((qcols, part), lambda n, m: (0, n)),
            ],
            out_specs=pl.BlockSpec((1, chunk_rows, LANES), lambda n, m: (n, 0, 0)),
            scratch_shapes=[
                pltpu.VMEM((rows, qcols), jnp.bfloat16),
                pltpu.VMEM((EXT, LANES), jnp.float32),
            ],
        ),
        out_shape=jax.ShapeDtypeStruct((chunks, chunk_rows, LANES), jnp.float32),
        name="merge",
    )(meta, pieces, packed, fresh_k, fresh_v, w_out)
    partial = exchange(partial)

    decoded, reward = pl.pallas_call(
        functools.partial(sum_kernel, rows),
        out_shape=(
            jax.ShapeDtypeStruct((rows, part), jnp.bfloat16),
            jax.ShapeDtypeStruct((EXT, LANES), jnp.float32),
        ),
        name="total",
    )(partial)
    far = lax.ppermute(decoded, "dp", swap)
    decoded = dot(give, jnp.concatenate([decoded, far], axis=0)).astype(jnp.bfloat16)
    return (reward[:slots, 0], decoded.reshape(STEPS, slots, part))


def solution(mesh):
    return jax.shard_map(
        functools.partial(local, mesh.shape["tensor"]),
        mesh=mesh,
        in_specs=(
            P(("groups", "dp"), None, "tensor"),
            P("tensor"),
            P("tensor"),
            P(None, ("groups", "dp"), "tensor"),
            P(),
            P(None, "tensor"),
            P(None, "tensor"),
            P("tensor", None),
            P(("groups", "dp"), "tensor", None),
            P(("groups", "dp"), "tensor", None),
            P("groups"),
            P("groups"),
        ),
        out_specs=(P(("groups", "dp")), P(None, ("groups", "dp"), "tensor")),
        check_vma=False,
    )
```

time: 487 us -> 114 us (0.23)
  blocking collectives: 222 us -> 0 us
  waiting for transfers between devices: 143 us -> 43.8 us
  matrix products: 49 us -> 2.45 us
  Pallas kernels: 0 us -> 31.7 us
  local copies, waits for them, and re-layouts: 20.7 us -> 6.91 us
  between operations: 14.1 us -> 0.71 us
    all_gather x6 -> x0, blocking collectives: 185 us -> none  [the longest x2 62.9 us: local(): lax.all_gather(decode_inputs[step], 'tensor', axis=1, tiled=True)]
    reduce_scatter x2 -> x0, waiting for transfers between devices: 118 us -> none  [local(): lax.psum_scatter(partial_out, 'tensor', scatter_dimension=1, tiled=True)]
    dot_general x12 -> x2, matrix products: 49 us -> 2.45 us  [dot(): return lax.dot_general(a, b, dims, preferred_element_type=jnp.float32)]
    psum x1 -> x0, blocking collectives: 37.1 us -> none  [local(): squares, head_dot = lax.psum((squares, head_dot), 'tensor')]
    pallas_call x0 -> x4, Pallas kernels: none -> 31.7 us  [the longest x1 11.8 us: local(): pl.pallas_call(functools.partial(project_kernel, pages, per_page, depth),...]
    all_to_all x6 -> x4, waiting for transfers between devices: 24.2 us -> 43.7 us  [exchange(): return lax.all_to_all(x, 'tensor', 0, 0, tiled=True)]
    gather x7 -> x0, local copies, waits for them, and re-layouts: 15.2 us -> none  [the longest x1 6.17 us: local(): values_now = jnp.take(every_v, mine, axis=0)]
    unnamed x1 -> x0, other arithmetic: 6.23 us -> none
  transfers between devices with their start and end apart: 10 -> 6, of which waited for: 7 -> 5; matrix products, arithmetic and copies ran while one was open for 14% -> 11% of each run, Pallas kernels for 0% -> 0%
where the time goes in v1:
time: 114 us; the launch traced here: 113 us
  waiting for transfers between devices  43.8 us (38%)
  Pallas kernels  31.7 us (28%)
  starting transfers between devices  18.3 us (16%)
  other arithmetic  9.6 us (8%)
  local copies, waits for them, and re-layouts  6.91 us (6%)
  matrix products  2.45 us (2%)
    all_to_all x4, waiting for transfers between devices, exchange(): return lax.all_to_all(x, 'tensor', 0, 0, tiled=True)  43.7 us
    all_to_all x4, starting transfers between devices, exchange(): return lax.all_to_all(x, 'tensor', 0, 0, tiled=True)  17.7 us
    pallas_call x1, Pallas kernels, local(): pl.pallas_call(functools.partial(project_kernel, pages, per_page, depth),...  11.8 us
    pallas_call x1, Pallas kernels, local(): pl.pallas_call(functools.partial(merge_kernel, pages, per_page, depth, sp...  11.3 us
    pallas_call x1, Pallas kernels, local(): pl.pallas_call(functools.partial(attend_kernel, page_rows), grid_spec=plt...  6.95 us
    reduce_sum x1, other arithmetic, local(): squares = jnp.sum(hidden * hidden, axis=-1)  3.64 us
    unnamed x10, local copies, waits for them, and re-layouts  3.04 us
    dot_general x2, matrix products, dot(): return lax.dot_general(a, b, dims, preferred_element_type=jnp.float32)  2.45 us
  transfers between devices with their start and end apart: 6, of which 5 were waited for; matrix products, arithmetic and copies ran while one was open for 11% of the time, Pallas kernels for 0%

profile of v1, /device:TPU:0, one launch (start us, length us, event | category | flops | bytes accessed | tf_op | source)
XLA Modules:
  0.0 113.4 jit_solution(11380806741709715676)
XLA Ops:
  2.5 0.8 convert_reduce_fusion
  4.4 0.7 mul.62
  5.1 0.9 convolution_convert_fusion.1
  6.0 0.7 broadcast_in_dim.26
  6.7 6.8 %all-to-all-start = ((bf16[8,16,1024]{2,1,0:T(8,128)(2,1)}), bf16[8,16,1024]{2,1,0:T(8,128)(2,1)S(1)}, u32[]{:S(2)}, u32[]{:S(2)}) async-start(bf16[8,16,1024]{2,1,0:T(8,128)(2,1)} %broadcast_in_dim.26), calls=%async_computation | async-start | bytes 524288 | tf_op jit(solution)/shard_map/all_to_all | solution.py:202
  13.6 3.6 %fusion = (f32[8,256]{1,0:T(8,128)S(1)}, f32[8,256]{1,0:T(8,128)S(1)}) fusion(bf16[8,256,1024]{2,1,0:T(8,128)(2,1)} %param.12, f32[1024]{0:T(1024)S(1)} %mul.62), kind=kLoop, calls=%fused_computation.2 | loop fusion | flops 10481664 | bytes 4214784 | tf_op jit(solution)/shard_map/reduce_sum | solution.py:265
  17.2 5.9 %all-to-all-done.x_ref = bf16[8,16,1024]{2,1,0:T(8,128)(2,1)S(1)} async-done(((bf16[8,16,1024]{2,1,0:T(8,128)(2,1)}), bf16[8,16,1024]{2,1,0:T(8,128)(2,1)S(1)}, u32[]{:S(2)}, u32[]{:S(2)}) %all-to-all-start) | async-done | bytes 262176 | tf_op jit(solution)/shard_map/all_to_all | solution.py:202
  23.1 0.7 copy-done.3
  23.8 11.8 %project.1.q_ref = bf16[8,160,128]{2,1,0:T(8,128)(2,1)} custom-call(bf16[8,16,1024]{2,1,0:T(8,128)(2,1)} %copy-done.3, f32[8,1,1024]{2,1,0:T(1,128)} %bitcast.22, bf16[8192,1024]{1,0:T(8,128)(2,1)} %wq_ref.1, bf16[8192,256]{1,0:T(8,128)(2,1)} %wkv_ref.1), custom_call_target="tpu_custom_call" | custom-call | tf_op jit(solution)/shard_map/project/pallas_call | solution.py:279
  35.6 3.6 %all-to-all-start.1 = ((bf16[8,160,128]{2,1,0:T(8,128)(2,1)}), bf16[8,160,128]{2,1,0:T(8,128)(2,1)S(1)}, u32[]{:S(2)}, u32[]{:S(2)}) async-start(bf16[8,160,128]{2,1,0:T(8,128)(2,1)} %project.1.q_ref), calls=%async_computation.1 | async-start | bytes 655360 | tf_op jit(solution)/shard_map/all_to_all | solution.py:202
  40.7 9.0 %all-to-all-done.1.q_ref = bf16[8,160,128]{2,1,0:T(8,128)(2,1)S(1)} async-done(((bf16[8,160,128]{2,1,0:T(8,128)(2,1)}), bf16[8,160,128]{2,1,0:T(8,128)(2,1)S(1)}, u32[]{:S(2)}, u32[]{:S(2)}) %all-to-all-start.1) | async-done | bytes 327712 | tf_op jit(solution)/shard_map/all_to_all | solution.py:202
  49.7 0.7 copy-done.2
  50.4 7.0 %attend.1 = f32[8,144,128]{2,1,0:T(8,128)} custom-call(s32[9]{0:T(128)} %pad_add_fusion.1.meta_ref, bf16[8,160,128]{2,1,0:T(8,128)(2,1)} %copy-done.2, bf16[8,256,1024]{2,1,0:T(8,128)(2,1)} %k_ref.1, bf16[8,256,1024]{2,1,0:T(8,128)(2,1)} %v_ref.1, f32[8,8,128]{2,1,0:T(8,128)} %pad_maximum_fusion.reward_ref), custom_call_target="tpu_custom_call" | custom-call | tf_op jit(solution)/shard_map/attend/pallas_call | solution.py:318
  57.4 3.6 %all-to-all-start.2 = ((f32[8,144,128]{2,1,0:T(8,128)}), f32[8,144,128]{2,1,0:T(8,128)S(1)}, u32[]{:S(2)}, u32[]{:S(2)}) async-start(f32[8,144,128]{2,1,0:T(8,128)} %attend.1), calls=%async_computation.2 | async-start | bytes 1179648 | tf_op jit(solution)/shard_map/all_to_all | solution.py:202
  61.7 0.8 slice.8
  63.1 13.7 %all-to-all-done.2.part_ref = f32[8,144,128]{2,1,0:T(8,128)S(1)} async-done(((f32[8,144,128]{2,1,0:T(8,128)}), f32[8,144,128]{2,1,0:T(8,128)S(1)}, u32[]{:S(2)}, u32[]{:S(2)}) %all-to-all-start.2) | async-done | bytes 589856 | tf_op jit(solution)/shard_map/all_to_all | solution.py:202
  76.8 0.8 copy-done
  77.7 11.3 %merge.1 = f32[8,136,128]{2,1,0:T(8,128)} custom-call(s32[2]{0:T(128)} %pad_add_fusion.meta_ref, f32[8,144,128]{2,1,0:T(8,128)} %copy-done, bf16[8,160,128]{2,1,0:T(8,128)(2,1)} %project.1.q_ref, bf16[16,128]{1,0:T(8,128)(2,1)} %get-tuple-element.11.fk_ref, bf16[16,128]{1,0:T(8,128)(2,1)} %get-tuple-element.10.fv_ref, bf16[1024,8192]{1,0:T(8,128)(2,1)} %w_ref.1), custom_call_target="tpu_custom_call" | custom-call | tf_op jit(solution)/shard_map/merge/pallas_call | solution.py:349
  88.9 3.6 %all-to-all-start.3 = ((f32[8,136,128]{2,1,0:T(8,128)}), f32[8,136,128]{2,1,0:T(8,128)S(1)}, u32[]{:S(2)}, u32[]{:S(2)}) async-start(f32[8,136,128]{2,1,0:T(8,128)} %merge.1), calls=%async_computation.3 | async-start | bytes 1114112 | tf_op jit(solution)/shard_map/all_to_all | solution.py:202
  92.9 15.0 %all-to-all-done.3.part_ref = f32[8,136,128]{2,1,0:T(8,128)S(1)} async-done(((f32[8,136,128]{2,1,0:T(8,128)}), f32[8,136,128]{2,1,0:T(8,128)S(1)}, u32[]{:S(2)}, u32[]{:S(2)}) %all-to-all-start.3) | async-done | bytes 557088 | tf_op jit(solution)/shard_map/all_to_all | solution.py:202
  107.9 0.8 copy-done.1
  108.7 1.7 %total.1 = (bf16[16,1024]{1,0:T(8,128)(2,1)}, f32[8,128]{1,0:T(8,128)}) custom-call(f32[8,136,128]{2,1,0:T(8,128)} %copy-done.1), custom_call_target="tpu_custom_call" | custom-call | tf_op jit(solution)/shard_map/total/pallas_call | solution.py:372
  110.4 1.3 %slice_reduce_fusion = f32[8]{0:T(128)} fusion(f32[8,128]{1,0:T(8,128)} %get-tuple-element.4), kind=kLoop, calls=%fused_computation.21 | loop fusion | bytes 64 | tf_op jit(solution)/shard_map/slice | solution.py:382
  111.8 1.6 %fusion.2 = bf16[2,8,1024]{2,1,0:T(8,128)(2,1)} fusion(pred[16,32]{0,1:T(32,128)(4,1)S(1)} %and.96, bf16[16,1024]{1,0:T(8,128)(2,1)S(1)} %collective-permute-done.1, bf16[16,1024]{1,0:T(8,128)(2,1)} %get-tuple-element.5), kind=kOutput, calls=%fused_computation.6 | convolution fusion | flops 1196032 | bytes 98816 | tf_op jit(solution)/shard_map/dot_general | solution.py:28
  (36 shorter events, 6.1 us)
Async XLA Ops:
  0.6 4.5 %collective-permute-start = (bf16[16,1024]{1,0:T(8,128)(2,1)}, bf16[16,1024]{1,0:T(8,128)(2,1)S(1)}, u32[]{:S(2)}, u32[]{:S(2)}) collective-permute-start(bf16[16,1024]{1,0:T(8,128)(2,1)} %bitcast.24), channel_id=1, source_target_pairs={{0,8},{8,0},{1,9},{9,1},{2,10},{10,2},{3,11},{11,3},{4,12},{12,4},... | collective-permute-start | bytes 98312 | tf_op jit(solution)/shard_map/ppermute | solution.py:260
  6.7 16.4 %all-to-all-start = ((bf16[8,16,1024]{2,1,0:T(8,128)(2,1)}), bf16[8,16,1024]{2,1,0:T(8,128)(2,1)S(1)}, u32[]{:S(2)}, u32[]{:S(2)}) async-start(bf16[8,16,1024]{2,1,0:T(8,128)(2,1)} %broadcast_in_dim.26), calls=%async_computation | async-start | bytes 524288 | tf_op jit(solution)/shard_map/all_to_all | solution.py:202
  23.1 0.7 copy-start.3
  23.8 15.4 %copy-start.4 = (s32[16]{0:T(128)S(1)}, s32[16]{0:T(128)}, u32[]{:S(2)}) copy-start(s32[16]{0:T(128)} %param.22) | copy-start | bytes 196
  35.6 14.1 %all-to-all-start.1 = ((bf16[8,160,128]{2,1,0:T(8,128)(2,1)}), bf16[8,160,128]{2,1,0:T(8,128)(2,1)S(1)}, u32[]{:S(2)}, u32[]{:S(2)}) async-start(bf16[8,160,128]{2,1,0:T(8,128)(2,1)} %project.1.q_ref), calls=%async_computation.1 | async-start | bytes 655360 | tf_op jit(solution)/shard_map/all_to_all | solution.py:202
  49.7 0.7 copy-start.2
  57.4 19.5 %all-to-all-start.2 = ((f32[8,144,128]{2,1,0:T(8,128)}), f32[8,144,128]{2,1,0:T(8,128)S(1)}, u32[]{:S(2)}, u32[]{:S(2)}) async-start(f32[8,144,128]{2,1,0:T(8,128)} %attend.1), calls=%async_computation.2 | async-start | bytes 1179648 | tf_op jit(solution)/shard_map/all_to_all | solution.py:202
  76.8 0.8 copy-start
  88.9 19.0 %all-to-all-start.3 = ((f32[8,136,128]{2,1,0:T(8,128)}), f32[8,136,128]{2,1,0:T(8,128)S(1)}, u32[]{:S(2)}, u32[]{:S(2)}) async-start(f32[8,136,128]{2,1,0:T(8,128)} %merge.1), calls=%async_computation.3 | async-start | bytes 1114112 | tf_op jit(solution)/shard_map/all_to_all | solution.py:202
  107.9 0.8 copy-start.1
  110.4 1.4 %collective-permute-start.1 = (bf16[16,1024]{1,0:T(8,128)(2,1)}, bf16[16,1024]{1,0:T(8,128)(2,1)S(1)}, u32[]{:S(2)}, u32[]{:S(2)}) collective-permute-start(bf16[16,1024]{1,0:T(8,128)(2,1)} %get-tuple-element.5), channel_id=1, source_target_pairs={{0,8},{8,0},{1,9},{9,1},{2,10},{10,2},{3,11},{11,3},{4,12},{12,4},... | collective-permute-start | bytes 98312 | tf_op jit(solution)/shard_map/ppermute | solution.py:380

commit v2 on v1

v2 whole, which is shorter than its diff:
```python
import functools

import jax
import jax.numpy as jnp
from jax import lax
from jax.experimental import pallas as pl
from jax.experimental.pallas import tpu as pltpu
from jax.sharding import PartitionSpec as P

HD = 128
KVH = 8
STEPS = 2
PAIR = 2
LANES = 128
EXT = 8
EPS = 1e-05
NEG = -1e30
SCALE = HD ** (-0.5)
NT = (((1,), (1,)), ((), ()))
TN = (((0,), (0,)), ((), ()))
MIB = 1 << 20
ANY = pl.BlockSpec(memory_space=pl.ANY)
VMEM = pl.BlockSpec(memory_space=pltpu.VMEM)
SMEM = pl.BlockSpec(memory_space=pltpu.SMEM)


def iota(shape, dim):
    return lax.broadcasted_iota(jnp.int32, shape, dim)


def dot(a, b, dims=(((1,), (0,)), ((), ()))):
    return lax.dot_general(a, b, dims, preferred_element_type=jnp.float32)


def head_major(shape, pages, per_page, heads):
    o, s = iota(shape, 0), iota(shape, 1)
    row = o % per_page
    head = (o // per_page) % heads
    page = o // (per_page * heads)
    return (s == (head * pages + page) * per_page + row).astype(jnp.bfloat16)


def aligned(index, size):
    return pl.ds(pl.multiple_of(index * size, size), size)


def project_kernel(pages, per_page, width, meta_ref, own_ref, far_ref, take_ref, gain_ref, wq_ref, wkv_ref, out_ref, tokens, wq, wkv, sems):
    me = meta_ref[0]
    chunks, rows, depth = own_ref.shape
    copies = []
    for r in range(chunks):
        source = aligned(me ^ r, depth)
        pair = (
            pltpu.make_async_copy(wq_ref.at[source], wq.at[r], sems.at[0, r]),
            pltpu.make_async_copy(wkv_ref.at[source], wkv.at[r], sems.at[1, r]),
        )
        for copy in pair:
            copy.start()
        copies.append(pair)

    total = jnp.zeros((rows, depth), jnp.float32)
    for r in range(chunks):
        both = jnp.concatenate([own_ref[r], far_ref[r]], axis=0)
        part = dot(take_ref[...], both)
        tokens[r] = part.astype(jnp.bfloat16)
        total = total + part * part
    inv = lax.rsqrt(jnp.sum(total, axis=-1, keepdims=True) / width + EPS)

    query = jnp.zeros((rows, wq.shape[2]), jnp.float32)
    keyval = jnp.zeros((rows, wkv.shape[2]), jnp.float32)
    for r in range(chunks):
        normed = (tokens[r].astype(jnp.float32) * inv * gain_ref[me ^ r]).astype(jnp.bfloat16)
        for copy in copies[r]:
            copy.wait()
        query = query + dot(normed, wq[r])
        keyval = keyval + dot(normed, wkv[r])

    heads = query.shape[1] // HD
    query = query.astype(jnp.bfloat16)
    stacked = jnp.concatenate([query[:, h * HD : (h + 1) * HD] for h in range(heads)], axis=0)
    order = head_major((rows * heads, rows * heads), pages, per_page, heads)
    body = rows * heads
    out_ref[:body] = dot(order, stacked).astype(jnp.bfloat16)
    keyval = keyval.astype(jnp.bfloat16)
    columns = keyval.shape[1]
    if columns < LANES:
        pad = jnp.zeros((rows, LANES - columns), jnp.bfloat16)
        keyval = jnp.concatenate([keyval, pad], axis=1)
    for v in range(keyval.shape[1] // LANES):
        out_ref[body + v * rows : body + (v + 1) * rows] = keyval[:, v * LANES : (v + 1) * LANES]


def attend_kernel(pages, page_rows, meta_ref, q_ref, k_ref, v_ref, reward_ref, *rest):
    outs, (spread, product, keys, values, sems) = rest[:-5], rest[-5:]
    width = k_ref.shape[1]
    span = KVH * page_rows
    body = pages * page_rows
    copies = []
    for i in range(pages):
        pair = (
            pltpu.make_async_copy(k_ref.at[meta_ref[i]], keys.at[i], sems.at[0, i]),
            pltpu.make_async_copy(v_ref.at[meta_ref[i]], values.at[i], sems.at[1, i]),
        )
        for copy in pair:
            copy.start()
        copies.append(pair)

    me = meta_ref[2 * pages + 1]
    spread[...] = jnp.zeros_like(spread)
    for i in range(pages):
        for r in range(KVH):
            spread[r * page_rows : (r + 1) * page_rows, aligned(me ^ r, HD)] = q_ref[
                r, i * page_rows : (i + 1) * page_rows, :
            ]
        copies[i][0].wait()
        scores = dot(keys[i], spread[...], NT) * SCALE
        valid = meta_ref[2 * pages] + iota((width, span), 0) < meta_ref[pages + i]
        scores = jnp.where(valid, scores, NEG)
        top = jnp.max(scores, axis=0, keepdims=True)
        expo = jnp.where(valid, jnp.exp(scores - top), 0.0)
        total = jnp.sum(expo, axis=0, keepdims=True)
        copies[i][1].wait()
        product[...] = dot(expo.astype(jnp.bfloat16), values[i], TN)
        for r in range(KVH):
            out = outs[r] if len(outs) > 1 else outs[0].at[r]
            out[i * page_rows : (i + 1) * page_rows, :] = product[
                r * page_rows : (r + 1) * page_rows, aligned(me ^ r, HD)
            ]
            lane = (r * page_rows) // LANES * LANES
            out[body + i : body + i + 1, :] = top[:, lane : lane + LANES]
            out[body + pages + i : body + pages + i + 1, :] = total[:, lane : lane + LANES]
    for r in range(KVH):
        if len(outs) > 1:
            outs[r][body + EXT :, :] = reward_ref[me ^ r]
        else:
            outs[0][r, body + EXT :, :] = jnp.zeros((EXT, LANES), jnp.float32)


def merge_kernel(pages, per_page, width, span, chunks, meta_ref, q_ref, fk_ref, fv_ref, w_ref, *rest):
    att = rest[-1]
    split = len(rest) > 3
    parts = rest[:chunks] if split else [rest[0].at[b] for b in range(chunks)]
    outs = rest[chunks:-1] if split else rest[1:-1]
    me = meta_ref[0]
    body = parts[0].shape[0] - 2 * EXT
    page_rows = body // pages
    heads = page_rows // per_page
    rows = pages * per_page

    query = q_ref[:body, :]
    recent = dot(query, fk_ref[...], NT) * SCALE
    line, col = iota(recent.shape, 0), iota(recent.shape, 1)
    mine = (line // page_rows) * per_page + line % per_page
    seen = (mine // STEPS == col // STEPS) & (col <= mine)
    recent = jnp.where(seen, recent, NEG)
    recent_max = jnp.max(recent, axis=-1, keepdims=True)
    recent_exp = jnp.where(seen, jnp.exp(recent - recent_max), 0.0)
    recent_total = jnp.sum(recent_exp, axis=-1, keepdims=True)
    recent_acc = dot(recent_exp.astype(jnp.bfloat16), fv_ref[...])

    extras = []
    for b in range(chunks):
        extra = parts[b][body : body + EXT, :]
        if split:
            shift = -(b * page_rows) % LANES
            extras.append(pltpu.roll(extra, shift, 1) if shift else extra)
        else:
            extras.append(pltpu.roll(extra, meta_ref[2], 1))
    maxima = [extra[:pages] for extra in extras]
    totals = [extra[pages : 2 * pages] for extra in extras]
    top = functools.reduce(jnp.maximum, maxima)
    factors = [jnp.exp(m - top) for m in maxima]
    total = functools.reduce(jnp.add, [f * t for f, t in zip(factors, totals)])

    pick = iota((page_rows, LANES), 0) == iota((page_rows, LANES), 1)

    def column(packed):
        return jnp.concatenate(
            [
                jnp.sum(
                    jnp.where(pick, jnp.broadcast_to(packed[i : i + 1], pick.shape), 0.0),
                    axis=-1,
                    keepdims=True,
                )
                for i in range(pages)
            ],
            axis=0,
        )

    acc = jnp.zeros((body, HD), jnp.float32)
    for b in range(chunks):
        acc = acc + column(factors[b]) * parts[b][:body, :]
    cache_top, cache_total = column(top), column(total)
    top = jnp.maximum(cache_top, recent_max)
    cache_factor = jnp.exp(cache_top - top)
    recent_factor = jnp.exp(recent_max - top)
    total = cache_factor * cache_total + recent_factor * recent_total
    acc = cache_factor * acc + recent_factor * recent_acc
    attended = (acc / total).astype(jnp.bfloat16)
    order = head_major((body, body), pages, per_page, heads)
    attended = dot(order, attended, TN).astype(jnp.bfloat16)
    for h in range(heads):
        att[:, h * HD : (h + 1) * HD] = attended[h * rows : (h + 1) * rows]

    tile = functools.reduce(jnp.add, [parts[b][body + EXT :, :] for b in range(chunks)])
    used = EXT // 2
    value = tile[used:] * lax.rsqrt(tile[:used] / width + EPS)
    mean = jnp.sum(value, keepdims=True) / span
    mean = jnp.where(iota((EXT, LANES), 0) == meta_ref[1], mean, 0.0)

    part = w_ref.shape[1] // chunks
    for r in range(chunks):
        out = outs[r] if split else outs[0].at[me ^ r]
        product = dot(att[...], w_ref[:, aligned(me ^ r, part)])
        for c in range(part // LANES):
            out[c * rows : (c + 1) * rows, :] = product[:, c * LANES : (c + 1) * LANES]
        out[out.shape[0] - EXT :, :] = mean


def sum_kernel(rows, *refs):
    parts, (out_ref, reward_ref) = refs[:-2], refs[-2:]
    if len(parts) == 1:
        parts = [parts[0].at[b] for b in range(parts[0].shape[0])]
    total = parts[0][...]
    for part in parts[1:]:
        total = total + part[...]
    for c in range(out_ref.shape[1] // LANES):
        out_ref[:, c * LANES : (c + 1) * LANES] = total[c * rows : (c + 1) * rows].astype(
            jnp.bfloat16
        )
    reward_ref[...] = total[total.shape[0] - EXT :]


def partner(x, chunks, bits):
    return lax.ppermute(x, "tensor", [(i, i ^ bits) for i in range(chunks)])


def spread_all(x, chunks, index):
    if chunks != KVH:
        every = lax.all_to_all(jnp.broadcast_to(x[None], (chunks,) + x.shape), "tensor", 0, 0, tiled=True)
        return jnp.take(every, index ^ jnp.arange(chunks), axis=0)
    pair = jnp.stack([x, partner(x, chunks, 1)])
    others = [partner(pair, chunks, bits) for bits in (2, 4, 6)]
    return jnp.stack([pair] + others).reshape((chunks,) + x.shape)


def trade(blocks, chunks):
    if len(blocks) == 1:
        return [lax.all_to_all(blocks[0], "tensor", 0, 0, tiled=True)]
    traded = {bits: partner(blocks[bits], chunks, bits) for bits in (4, 5, 6, 7, 2, 3, 1)}
    return [blocks[0]] + [traded[bits] for bits in range(1, chunks)]


def local(
    chunks,
    reward_hidden,
    reward_gain,
    reward_head,
    decode_inputs,
    attn_gain,
    w_query,
    w_keyval,
    w_out,
    cache_keys,
    cache_values,
    lengths,
    slot_map,
):
    slots, width = cache_keys.shape[:2]
    depth, qcols = w_query.shape
    kvcols = w_keyval.shape[1]
    part = decode_inputs.shape[-1]
    heads = qcols // HD
    group = heads * chunks // KVH
    split = group // heads
    pages = slots // PAIR
    per_page = PAIR * STEPS
    page_rows = per_page * group
    rows = slots * STEPS
    body = rows * heads
    mine, index = lax.axis_index("dp"), lax.axis_index("tensor")
    swap = [(0, 1), (1, 0)]

    ids = jnp.arange(slot_map.shape[0])
    kept = slot_map == ids
    home = slot_map // slots
    before = kept[None, :] & (ids[None, :] // slots == home[:, None]) & (ids[None, :] < slot_map[:, None])
    place = home * slots + PAIR * jnp.sum(before, axis=1) + (slot_map != ids)
    place_own = lax.dynamic_slice_in_dim(place, mine * slots, slots)
    place_far = lax.dynamic_slice_in_dim(place, (1 - mine) * slots, slots)
    lead = place[None, :] == (mine * slots + PAIR * jnp.arange(pages))[:, None]
    page = jnp.sum(jnp.where(lead, ids[None, :], 0), axis=1) - mine * slots
    live = jnp.sum(jnp.where(lead, lengths[None, :], 0), axis=1)
    work = jnp.arange(rows)
    steps = jnp.arange(STEPS)
    both = jnp.stack([place_own, place_far]) - mine * slots
    take = (both[None, None, :, None, :] == jnp.arange(slots)[:, None, None, None, None]) & (
        steps[None, :, None, None, None] == steps[None, None, None, :, None]
    )
    take = take.reshape(rows, 2 * rows).astype(jnp.bfloat16)
    bases = jnp.stack([mine, 1 - mine]) * slots
    give = (
        (place_own[None, :, None] - bases[None, None, :])[..., None, None]
        == jnp.arange(slots)[None, None, None, :, None]
    ) & (steps[:, None, None, None, None] == steps[None, None, None, None, :])
    give = give.reshape(rows, 2 * rows).astype(jnp.bfloat16)

    direct = chunks == KVH
    own = spread_all(decode_inputs.reshape(rows, part), chunks, index)
    far = lax.ppermute(own, "dp", swap)

    hidden = reward_hidden.astype(jnp.float32)
    squares = jnp.sum(hidden * hidden, axis=-1)
    head_dot = jnp.sum(hidden * (reward_gain * reward_head), axis=-1)
    span = squares.shape[1]

    def tile(values):
        values = values.reshape(chunks, -1)
        size = EXT // 2 * LANES
        return jnp.pad(values, ((0, 0), (0, size - values.shape[1]))).reshape(
            chunks, EXT // 2, LANES
        )

    reward_parts = jnp.concatenate([tile(squares), tile(head_dot)], axis=1)

    pieces = max(kvcols // LANES, 1)
    packed_rows = body + pieces * rows
    packed = pl.pallas_call(
        functools.partial(project_kernel, pages, per_page, depth),
        in_specs=[SMEM, VMEM, VMEM, VMEM, VMEM, ANY, ANY],
        out_specs=VMEM,
        out_shape=jax.ShapeDtypeStruct((packed_rows, LANES), jnp.bfloat16),
        scratch_shapes=[
            pltpu.VMEM((chunks, rows, part), jnp.bfloat16),
            pltpu.VMEM((chunks, part, qcols), jnp.bfloat16),
            pltpu.VMEM((chunks, part, kvcols), jnp.bfloat16),
            pltpu.SemaphoreType.DMA((2, chunks)),
        ],
        compiler_params=pltpu.CompilerParams(vmem_limit_bytes=28 * MIB),
        cost_estimate=pl.CostEstimate(
            flops=2 * rows * depth * (qcols + kvcols),
            bytes_accessed=2 * depth * (qcols + kvcols),
            transcendentals=0,
        ),
        name="project",
    )(index[None], own, far, take, attn_gain.reshape(chunks, 1, part), w_query, w_keyval)
    gathered = spread_all(packed, chunks, index)

    kv_head = index * heads // group
    if kvcols < LANES:
        fresh = jnp.take(gathered[:, body:, :kvcols], index ^ jnp.arange(chunks), axis=0)
        fresh = fresh.transpose(1, 0, 2).reshape(rows, 2 * KVH, HD).transpose(1, 0, 2)
        fresh_k = lax.dynamic_index_in_dim(fresh, kv_head, 0, keepdims=False)
        fresh_v = lax.dynamic_index_in_dim(fresh, KVH + kv_head, 0, keepdims=False)
    else:

        def fresh_of(column):
            start = (column // pieces) ^ index, body + column % pieces * rows, 0
            return lax.dynamic_slice(gathered, start, (1, rows, LANES))[0]

        fresh_k, fresh_v = fresh_of(kv_head), fresh_of(KVH + kv_head)
    queries = gathered
    if not direct:
        queries = (
            jnp.take(gathered[:, :body], index ^ jnp.arange(chunks), axis=0)
            .reshape(KVH, split, pages, heads * per_page, HD)
            .transpose(0, 2, 1, 3, 4)
            .reshape(KVH, pages * page_rows, HD)
        )

    base = index if direct else index * 0
    meta = jnp.concatenate([page, live, (index * width)[None], base[None]]).astype(jnp.int32)
    big = pages * page_rows
    block = (big + 2 * EXT, HD)
    attended = pl.pallas_call(
        functools.partial(attend_kernel, pages, page_rows),
        in_specs=[SMEM, VMEM, ANY, ANY, VMEM],
        out_specs=[VMEM] * (KVH if direct else 1),
        out_shape=(
            [jax.ShapeDtypeStruct(block, jnp.float32)] * KVH
            if direct
            else [jax.ShapeDtypeStruct((KVH,) + block, jnp.float32)]
        ),
        scratch_shapes=[
            pltpu.VMEM((KVH * page_rows, KVH * HD), jnp.bfloat16),
            pltpu.VMEM((KVH * page_rows, KVH * HD), jnp.float32),
            pltpu.VMEM((pages, width, KVH * HD), jnp.bfloat16),
            pltpu.VMEM((pages, width, KVH * HD), jnp.bfloat16),
            pltpu.SemaphoreType.DMA((2, pages)),
        ],
        compiler_params=pltpu.CompilerParams(vmem_limit_bytes=12 * MIB),
        cost_estimate=pl.CostEstimate(
            flops=4 * pages * width * KVH * HD * KVH * page_rows,
            bytes_accessed=4 * pages * width * KVH * HD,
            transcendentals=pages * width * KVH * page_rows,
        ),
        name="attend",
    )(meta, queries, cache_keys, cache_values, reward_parts)
    if not direct:
        acc = (
            attended[0][:, :big]
            .reshape(KVH, pages, split, heads * per_page, HD)
            .transpose(0, 2, 1, 3, 4)
            .reshape(chunks, body, HD)
        )
        extra = jnp.repeat(attended[0][:, big : big + EXT], split, axis=0)
        attended = [jnp.concatenate([acc, extra, reward_parts], axis=1)]
    parts = trade(attended, chunks)

    chunk_rows = part // LANES * rows + EXT
    own_row = index * (slots * span // chunks) // span
    shift = -(index * heads * per_page) % LANES
    meta = jnp.stack([index, own_row, shift]).astype(jnp.int32)
    partial = pl.pallas_call(
        functools.partial(merge_kernel, pages, per_page, depth, span, chunks),
        in_specs=[SMEM] + [VMEM] * (4 + len(parts)),
        out_specs=[VMEM] * len(parts),
        out_shape=(
            [jax.ShapeDtypeStruct((chunk_rows, LANES), jnp.float32)] * chunks
            if direct
            else [jax.ShapeDtypeStruct((chunks, chunk_rows, LANES), jnp.float32)]
        ),
        scratch_shapes=[pltpu.VMEM((rows, qcols), jnp.bfloat16)],
        compiler_params=pltpu.CompilerParams(vmem_limit_bytes=8 * MIB),
        cost_estimate=pl.CostEstimate(
            flops=2 * rows * qcols * depth, bytes_accessed=2 * qcols * depth, transcendentals=0
        ),
        name="merge",
    )(meta, packed, fresh_k, fresh_v, w_out, *parts)
    partial = trade(partial, chunks)

    decoded, reward = pl.pallas_call(
        functools.partial(sum_kernel, rows),
        out_shape=(
            jax.ShapeDtypeStruct((rows, part), jnp.bfloat16),
            jax.ShapeDtypeStruct((EXT, LANES), jnp.float32),
        ),
        compiler_params=pltpu.CompilerParams(vmem_limit_bytes=8 * MIB),
        name="total",
    )(*partial)
    far = lax.ppermute(decoded, "dp", swap)
    decoded = dot(give, jnp.concatenate([decoded, far], axis=0)).astype(jnp.bfloat16)
    return (reward[:slots, 0], decoded.reshape(STEPS, slots, part))


def solution(mesh):
    return jax.shard_map(
        functools.partial(local, mesh.shape["tensor"]),
        mesh=mesh,
        in_specs=(
            P(("groups", "dp"), None, "tensor"),
            P("tensor"),
            P("tensor"),
            P(None, ("groups", "dp"), "tensor"),
            P(),
            P(None, "tensor"),
            P(None, "tensor"),
            P("tensor", None),
            P(("groups", "dp"), "tensor", None),
            P(("groups", "dp"), "tensor", None),
            P("groups"),
            P("groups"),
        ),
        out_specs=(P(("groups", "dp")), P(None, ("groups", "dp"), "tensor")),
        check_vma=False,
    )
```

time: 114 us -> 106 us (0.930)
  waiting for transfers between devices: 43.8 us -> 25 us
  Pallas kernels: 31.7 us -> 14.2 us
  starting transfers between devices: 18.3 us -> 35.2 us
  local copies, waits for them, and re-layouts: 6.91 us -> 19.9 us
  matrix products: 2.45 us -> 0.81 us
    all_to_all x4 -> x0, waiting for transfers between devices: 43.7 us -> none  [exchange(): return lax.all_to_all(x, 'tensor', 0, 0, tiled=True)]
    ppermute x0 -> x22, starting transfers between devices: none -> 35.1 us  [partner(): return lax.ppermute(x, 'tensor', [(i, i ^ bits) for i in range(chunks)])]
    ppermute x0 -> x22, waiting for transfers between devices: none -> 23.2 us  [partner(): return lax.ppermute(x, 'tensor', [(i, i ^ bits) for i in range(chunks)])]
    all_to_all x4 -> x0, starting transfers between devices: 17.7 us -> none  [exchange(): return lax.all_to_all(x, 'tensor', 0, 0, tiled=True)]
    unnamed x10 -> x12, local copies, waits for them, and re-layouts: 3.04 us -> 18.8 us
    pallas_call x1, Pallas kernels: 11.3 us -> 3.5 us  [local(): pl.pallas_call(functools.partial(merge_kernel, pages, per_page, depth, sp...]
    pallas_call x1, Pallas kernels: 11.8 us -> 5.72 us  [local(): pl.pallas_call(functools.partial(project_kernel, pages, per_page, depth),...]
    pallas_call x1, Pallas kernels: 6.95 us -> 4.93 us  [local(): pl.pallas_call(functools.partial(attend_kernel, pages, page_rows), in_spe...]
  transfers between devices with their start and end apart: 6 -> 24, of which waited for: 5 -> 11; matrix products, arithmetic and copies ran while one was open for 11% -> 9% of each run, Pallas kernels for 0% -> 0%
where the time goes in v2:
time: 106 us; the launch traced here: 105 us
  starting transfers between devices  35.2 us (33%)
  waiting for transfers between devices  25 us (24%)
  local copies, waits for them, and re-layouts  19.9 us (19%)
  Pallas kernels  14.2 us (13%)
  other arithmetic  9.44 us (9%)
    ppermute x22, starting transfers between devices, partner(): return lax.ppermute(x, 'tensor', [(i, i ^ bits) for i in range(chunks)])  35.1 us
    ppermute x22, waiting for transfers between devices, partner(): return lax.ppermute(x, 'tensor', [(i, i ^ bits) for i in range(chunks)])  23.2 us
    unnamed x12, local copies, waits for them, and re-layouts  18.8 us
    pallas_call x1, Pallas kernels, local(): pl.pallas_call(functools.partial(project_kernel, pages, per_page, depth),...  5.72 us
    pallas_call x1, Pallas kernels, local(): pl.pallas_call(functools.partial(attend_kernel, pages, page_rows), in_spe...  4.93 us
    reduce_sum x1, other arithmetic, local(): squares = jnp.sum(hidden * hidden, axis=-1)  3.64 us
    pallas_call x1, Pallas kernels, local(): pl.pallas_call(functools.partial(merge_kernel, pages, per_page, depth, sp...  3.5 us
  transfers between devices with their start and end apart: 24, of which 11 were waited for; matrix products, arithmetic and copies ran while one was open for 9% of the time, Pallas kernels for 0%

profile of v2, /device:TPU:0, one launch (start us, length us, event | category | flops | bytes accessed | tf_op | source)
XLA Modules:
  0.0 105.4 jit_solution(4917480825174641646)
XLA Ops:
  0.6 3.1 %collective-permute-start = (bf16[16,1024]{1,0:T(8,128)(2,1)}, bf16[16,1024]{1,0:T(8,128)(2,1)S(1)}, u32[]{:S(2)}, u32[]{:S(2)}) collective-permute-start(bf16[16,1024]{1,0:T(8,128)(2,1)} %bitcast.49), channel_id=1, source_target_pairs={{0,1},{1,0},{2,3},{3,2},{4,5},{5,4},{6,7},{7,6},{8,9},{9,8},{10,11... | collective-permute-start | bytes 98312 | tf_op jit(solution)/shard_map/ppermute | solution.py:235
  7.5 3.6 %fusion = (f32[8,256]{1,0:T(8,128)S(1)}, f32[8,256]{1,0:T(8,128)S(1)}) fusion(bf16[8,256,1024]{2,1,0:T(8,128)(2,1)} %param.12, f32[1024]{0:T(1024)S(1)} %mul.71), kind=kLoop, calls=%fused_computation.2 | loop fusion | flops 10481664 | bytes 4214784 | tf_op jit(solution)/shard_map/reduce_sum | solution.py:313
  14.5 2.6 %collective-permute-start.2 = (bf16[2,16,1024]{2,1,0:T(8,128)(2,1)S(1)}, bf16[2,16,1024]{2,1,0:T(8,128)(2,1)S(1)}, u32[]{:S(2)}, u32[]{:S(2)}) collective-permute-start(bf16[2,16,1024]{2,1,0:T(8,128)(2,1)S(1)} %get-tuple-element.47), channel_id=1, source_target_pairs={{0,4},{1,5},{2,6},{3,7},{4,0},{5,1},{6,2},{7,3},{8,12},{9,13},{10,... | collective-permute-start | bytes 196616 | tf_op jit(solution)/shard_map/ppermute | solution.py:235
  17.3 4.2 %collective-permute-done.2 = bf16[2,16,1024]{2,1,0:T(8,128)(2,1)S(1)} collective-permute-done((bf16[2,16,1024]{2,1,0:T(8,128)(2,1)S(1)}, bf16[2,16,1024]{2,1,0:T(8,128)(2,1)S(1)}, u32[]{:S(2)}, u32[]{:S(2)}) %collective-permute-start.2) | collective-permute-done | bytes 65568 | tf_op jit(solution)/shard_map/ppermute | solution.py:235
  24.8 5.8 %copy-done = bf16[8192,1024]{1,0:T(8,128)(2,1)S(1)} copy-done((bf16[8192,1024]{1,0:T(8,128)(2,1)S(1)}, bf16[8192,1024]{1,0:T(8,128)(2,1)}, u32[]{:S(2)}) %copy-start) | copy-done | bytes 16777240
  30.5 2.2 %copy-done.2 = bf16[8192,256]{1,0:T(8,128)(2,1)S(1)} copy-done((bf16[8192,256]{1,0:T(8,128)(2,1)S(1)}, bf16[8192,256]{1,0:T(8,128)(2,1)}, u32[]{:S(2)}) %copy-start.2) | copy-done | bytes 4194328
  33.5 5.7 %project.1.q_ref = bf16[160,128]{1,0:T(8,128)(2,1)S(1)} custom-call(s32[1]{0:T(128)} %bitcast.meta_ref, bf16[8,16,1024]{2,1,0:T(8,128)(2,1)S(1)} %bitcast.39, bf16[8,16,1024]{2,1,0:T(8,128)(2,1)S(1)} %collective-permute-done.4.far_ref, bf16[16,32]{1,0:T(8,128)(2,1)S(1)} %reshape.207.take_ref, f32[8,1,1024]{2,1,0:T(1,128)S(1)} %bitcast.41, ...), custom_call_target="tpu_custom_call" | custom-call | flops 335544320 | bytes 20971520 | tf_op jit(solution)/shard_map/project/pallas_call | solution.py:328
  39.9 3.4 %collective-permute-done.5 = bf16[160,128]{1,0:T(8,128)(2,1)S(1)} collective-permute-done((bf16[160,128]{1,0:T(8,128)(2,1)S(1)}, bf16[160,128]{1,0:T(8,128)(2,1)S(1)}, u32[]{:S(2)}, u32[]{:S(2)}) %collective-permute-start.5) | collective-permute-done | bytes 40992 | tf_op jit(solution)/shard_map/ppermute | solution.py:235
  43.4 2.1 %collective-permute-start.7 = (bf16[2,160,128]{2,1,0:T(8,128)(2,1)S(1)}, bf16[2,160,128]{2,1,0:T(8,128)(2,1)S(1)}, u32[]{:S(2)}, u32[]{:S(2)}) collective-permute-start(bf16[2,160,128]{2,1,0:T(8,128)(2,1)S(1)} %get-tuple-element.45), channel_id=1, source_target_pairs={{0,4},{1,5},{2,6},{3,7},{4,0},{5,1},{6,2},{7,3},{8,12},{9,13},{10,... | collective-permute-start | bytes 245768 | tf_op jit(solution)/shard_map/ppermute | solution.py:235
  45.4 2.3 %collective-permute-start.8 = (bf16[2,160,128]{2,1,0:T(8,128)(2,1)S(1)}, bf16[2,160,128]{2,1,0:T(8,128)(2,1)S(1)}, u32[]{:S(2)}, u32[]{:S(2)}) collective-permute-start(bf16[2,160,128]{2,1,0:T(8,128)(2,1)S(1)} %get-tuple-element.45), channel_id=1, source_target_pairs={{0,6},{1,7},{2,4},{3,5},{4,2},{5,3},{6,0},{7,1},{8,14},{9,15},{10,... | collective-permute-start | bytes 245768 | tf_op jit(solution)/shard_map/ppermute | solution.py:235
  47.8 4.5 %collective-permute-done.7 = bf16[2,160,128]{2,1,0:T(8,128)(2,1)S(1)} collective-permute-done((bf16[2,160,128]{2,1,0:T(8,128)(2,1)S(1)}, bf16[2,160,128]{2,1,0:T(8,128)(2,1)S(1)}, u32[]{:S(2)}, u32[]{:S(2)}) %collective-permute-start.7) | collective-permute-done | bytes 81952 | tf_op jit(solution)/shard_map/ppermute | solution.py:235
  52.4 2.2 %copy-done.3 = bf16[8,256,1024]{2,1,0:T(8,128)(2,1)S(1)} copy-done((bf16[8,256,1024]{2,1,0:T(8,128)(2,1)S(1)}, bf16[8,256,1024]{2,1,0:T(8,128)(2,1)}, u32[]{:S(2)}) %copy-start.3) | copy-done | bytes 4194328
  54.5 2.2 %copy-done.4 = bf16[8,256,1024]{2,1,0:T(8,128)(2,1)S(1)} copy-done((bf16[8,256,1024]{2,1,0:T(8,128)(2,1)S(1)}, bf16[8,256,1024]{2,1,0:T(8,128)(2,1)}, u32[]{:S(2)}) %copy-start.4) | copy-done | bytes 4194328
  56.7 4.9 %attend.1 = (f32[144,128]{1,0:T(8,128)S(1)}, f32[144,128]{1,0:T(8,128)S(1)}, f32[144,128]{1,0:T(8,128)S(1)}, f32[144,128]{1,0:T(8,128)S(1)}, f32[144,128]{1,0:T(...) custom-call(s32[10]{0:T(128)S(1)} %pad_add_fusion.1.meta_ref, ...), custom_call_target="tpu_custom_call" | custom-call | flops 1073741824 | bytes 4194304 | tf_op jit(solution)/shard_map/attend/pallas_call | solution.py:375
  63.8 2.2 %collective-permute-start.12 = (f32[144,128]{1,0:T(8,128)S(1)}, f32[144,128]{1,0:T(8,128)S(1)}, u32[]{:S(2)}, u32[]{:S(2)}) collective-permute-start(f32[144,128]{1,0:T(8,128)S(1)} %get-tuple-element.24), channel_id=1, source_target_pairs={{0,4},{1,5},{2,6},{3,7},{4,0},{5,1},{6,2},{7,3},{8,12},{9,13},{10,... | collective-permute-start | bytes 221192 | tf_op jit(solution)/shard_map/ppermute | solution.py:235
  67.7 2.2 %collective-permute-start.14 = (f32[144,128]{1,0:T(8,128)S(1)}, f32[144,128]{1,0:T(8,128)S(1)}, u32[]{:S(2)}, u32[]{:S(2)}) collective-permute-start(f32[144,128]{1,0:T(8,128)S(1)} %get-tuple-element.26), channel_id=1, source_target_pairs={{0,6},{1,7},{2,4},{3,5},{4,2},{5,3},{6,0},{7,1},{8,14},{9,15},{10,... | collective-permute-start | bytes 221192 | tf_op jit(solution)/shard_map/ppermute | solution.py:235
  74.2 3.2 %collective-permute-done.13.rest_5_ = f32[144,128]{1,0:T(8,128)S(1)} collective-permute-done((f32[144,128]{1,0:T(8,128)S(1)}, f32[144,128]{1,0:T(8,128)S(1)}, u32[]{:S(2)}, u32[]{:S(2)}) %collective-permute-start.13) | collective-permute-done | bytes 73760 | tf_op jit(solution)/shard_map/ppermute | solution.py:235
  77.4 5.8 %copy-done.1 = bf16[1024,8192]{1,0:T(8,128)(2,1)S(1)} copy-done((bf16[1024,8192]{1,0:T(8,128)(2,1)S(1)}, bf16[1024,8192]{1,0:T(8,128)(2,1)}, u32[]{:S(2)}) %copy-start.1) | copy-done | bytes 16777240
  83.2 3.5 %merge.1 = (f32[136,128]{1,0:T(8,128)S(1)}, f32[136,128]{1,0:T(8,128)S(1)}, f32[136,128]{1,0:T(8,128)S(1)}, f32[136,128]{1,0:T(8,128)S(1)}, f32[136,128]{1,0:T(8...) custom-call(s32[3]{0:T(128)S(1)} %pad_add_fusion.meta_ref, ...), custom_call_target="tpu_custom_call" | custom-call | flops 268435456 | bytes 16777216 | tf_op jit(solution)/shard_map/merge/pallas_call | solution.py:414
  87.8 1.9 %collective-permute-start.17 = (f32[136,128]{1,0:T(8,128)S(1)}, f32[136,128]{1,0:T(8,128)S(1)}, u32[]{:S(2)}, u32[]{:S(2)}) collective-permute-start(f32[136,128]{1,0:T(8,128)S(1)} %get-tuple-element.30), channel_id=1, source_target_pairs={{0,2},{1,3},{2,0},{3,1},{4,6},{5,7},{6,4},{7,5},{8,10},{9,11},{10,... | collective-permute-start | bytes 208904 | tf_op jit(solution)/shard_map/ppermute | solution.py:235
  90.4 2.5 %collective-permute-start.19 = (f32[136,128]{1,0:T(8,128)S(1)}, f32[136,128]{1,0:T(8,128)S(1)}, u32[]{:S(2)}, u32[]{:S(2)}) collective-permute-start(f32[136,128]{1,0:T(8,128)S(1)} %get-tuple-element.32), channel_id=1, source_target_pairs={{0,4},{1,5},{2,6},{3,7},{4,0},{5,1},{6,2},{7,3},{8,12},{9,13},{10,... | collective-permute-start | bytes 208904 | tf_op jit(solution)/shard_map/ppermute | solution.py:235
  93.8 2.4 %collective-permute-start.21 = (f32[136,128]{1,0:T(8,128)S(1)}, f32[136,128]{1,0:T(8,128)S(1)}, u32[]{:S(2)}, u32[]{:S(2)}) collective-permute-start(f32[136,128]{1,0:T(8,128)S(1)} %get-tuple-element.34), channel_id=1, source_target_pairs={{0,6},{1,7},{2,4},{3,5},{4,2},{5,3},{6,0},{7,1},{8,14},{9,15},{10,... | collective-permute-start | bytes 208904 | tf_op jit(solution)/shard_map/ppermute | solution.py:235
  96.2 1.8 %collective-permute-start.22 = (f32[136,128]{1,0:T(8,128)S(1)}, f32[136,128]{1,0:T(8,128)S(1)}, u32[]{:S(2)}, u32[]{:S(2)}) collective-permute-start(f32[136,128]{1,0:T(8,128)S(1)} %get-tuple-element.35), channel_id=1, source_target_pairs={{0,7},{1,6},{2,5},{3,4},{4,3},{5,2},{6,1},{7,0},{8,15},{9,14},{10,... | collective-permute-start | bytes 208904 | tf_op jit(solution)/shard_map/ppermute | solution.py:235
  98.2 2.5 %collective-permute-done.19.refs_4_ = f32[136,128]{1,0:T(8,128)S(1)} collective-permute-done((f32[136,128]{1,0:T(8,128)S(1)}, f32[136,128]{1,0:T(8,128)S(1)}, u32[]{:S(2)}, u32[]{:S(2)}) %collective-permute-start.19) | collective-permute-done | bytes 69664 | tf_op jit(solution)/shard_map/ppermute | solution.py:235
  (75 shorter events, 28.0 us)
Async XLA Ops:
  0.6 11.4 %collective-permute-start = (bf16[16,1024]{1,0:T(8,128)(2,1)}, bf16[16,1024]{1,0:T(8,128)(2,1)S(1)}, u32[]{:S(2)}, u32[]{:S(2)}) collective-permute-start(bf16[16,1024]{1,0:T(8,128)(2,1)} %bitcast.49), channel_id=1, source_target_pairs={{0,1},{1,0},{2,3},{3,2},{4,5},{5,4},{6,7},{7,6},{8,9},{9,8},{10,11... | collective-permute-start | bytes 98312 | tf_op jit(solution)/shard_map/ppermute | solution.py:235
  12.8 4.5 %collective-permute-start.1 = (bf16[2,16,1024]{2,1,0:T(8,128)(2,1)S(1)}, bf16[2,16,1024]{2,1,0:T(8,128)(2,1)S(1)}, u32[]{:S(2)}, u32[]{:S(2)}) collective-permute-start(bf16[2,16,1024]{2,1,0:T(8,128)(2,1)S(1)} %get-tuple-element.47), channel_id=1, source_target_pairs={{0,2},{1,3},{2,0},{3,1},{4,6},{5,7},{6,4},{7,5},{8,10},{9,11},{10,... | collective-permute-start | bytes 196616 | tf_op jit(solution)/shard_map/ppermute | solution.py:235
  14.5 7.0 %collective-permute-start.2 = (bf16[2,16,1024]{2,1,0:T(8,128)(2,1)S(1)}, bf16[2,16,1024]{2,1,0:T(8,128)(2,1)S(1)}, u32[]{:S(2)}, u32[]{:S(2)}) collective-permute-start(bf16[2,16,1024]{2,1,0:T(8,128)(2,1)S(1)} %get-tuple-element.47), channel_id=1, source_target_pairs={{0,4},{1,5},{2,6},{3,7},{4,0},{5,1},{6,2},{7,3},{8,12},{9,13},{10,... | collective-permute-start | bytes 196616 | tf_op jit(solution)/shard_map/ppermute | solution.py:235
  17.1 6.1 %collective-permute-start.3 = (bf16[2,16,1024]{2,1,0:T(8,128)(2,1)S(1)}, bf16[2,16,1024]{2,1,0:T(8,128)(2,1)S(1)}, u32[]{:S(2)}, u32[]{:S(2)}) collective-permute-start(bf16[2,16,1024]{2,1,0:T(8,128)(2,1)S(1)} %get-tuple-element.47), channel_id=1, source_target_pairs={{0,6},{1,7},{2,4},{3,5},{4,2},{5,3},{6,0},{7,1},{8,14},{9,15},{10,... | collective-permute-start | bytes 196616 | tf_op jit(solution)/shard_map/ppermute | solution.py:235
  23.2 1.6 %collective-permute-start.4 = (bf16[8,16,1024]{2,1,0:T(8,128)(2,1)S(1)}, bf16[8,16,1024]{2,1,0:T(8,128)(2,1)S(1)}, u32[]{:S(2)}, u32[]{:S(2)}) collective-permute-start(bf16[8,16,1024]{2,1,0:T(8,128)(2,1)S(1)} %bitcast.38), channel_id=1, source_target_pairs={{0,8},{8,0},{1,9},{9,1},{2,10},{10,2},{3,11},{11,3},{4,12},{12,4},... | collective-permute-start | bytes 786440 | tf_op jit(solution)/shard_map/ppermute | solution.py:310
  39.2 4.1 %collective-permute-start.5 = (bf16[160,128]{1,0:T(8,128)(2,1)S(1)}, bf16[160,128]{1,0:T(8,128)(2,1)S(1)}, u32[]{:S(2)}, u32[]{:S(2)}) collective-permute-start(bf16[160,128]{1,0:T(8,128)(2,1)S(1)} %project.1.q_ref), channel_id=1, source_target_pairs={{0,1},{1,0},{2,3},{3,2},{4,5},{5,4},{6,7},{7,6},{8,9},{9,8},{10,11... | collective-permute-start | bytes 122888 | tf_op jit(solution)/shard_map/ppermute | solution.py:235
  43.3 4.5 %collective-permute-start.6 = (bf16[2,160,128]{2,1,0:T(8,128)(2,1)S(1)}, bf16[2,160,128]{2,1,0:T(8,128)(2,1)S(1)}, u32[]{:S(2)}, u32[]{:S(2)}) collective-permute-start(bf16[2,160,128]{2,1,0:T(8,128)(2,1)S(1)} %get-tuple-element.45), channel_id=1, source_target_pairs={{0,2},{1,3},{2,0},{3,1},{4,6},{5,7},{6,4},{7,5},{8,10},{9,11},{10,... | collective-permute-start | bytes 245768 | tf_op jit(solution)/shard_map/ppermute | solution.py:235
  43.4 8.9 %collective-permute-start.7 = (bf16[2,160,128]{2,1,0:T(8,128)(2,1)S(1)}, bf16[2,160,128]{2,1,0:T(8,128)(2,1)S(1)}, u32[]{:S(2)}, u32[]{:S(2)}) collective-permute-start(bf16[2,160,128]{2,1,0:T(8,128)(2,1)S(1)} %get-tuple-element.45), channel_id=1, source_target_pairs={{0,4},{1,5},{2,6},{3,7},{4,0},{5,1},{6,2},{7,3},{8,12},{9,13},{10,... | collective-permute-start | bytes 245768 | tf_op jit(solution)/shard_map/ppermute | solution.py:235
  45.4 6.9 %collective-permute-start.8 = (bf16[2,160,128]{2,1,0:T(8,128)(2,1)S(1)}, bf16[2,160,128]{2,1,0:T(8,128)(2,1)S(1)}, u32[]{:S(2)}, u32[]{:S(2)}) collective-permute-start(bf16[2,160,128]{2,1,0:T(8,128)(2,1)S(1)} %get-tuple-element.45), channel_id=1, source_target_pairs={{0,6},{1,7},{2,4},{3,5},{4,2},{5,3},{6,0},{7,1},{8,14},{9,15},{10,... | collective-permute-start | bytes 245768 | tf_op jit(solution)/shard_map/ppermute | solution.py:235
  61.7 8.2 %collective-permute-start.10 = (f32[144,128]{1,0:T(8,128)S(1)}, f32[144,128]{1,0:T(8,128)S(1)}, u32[]{:S(2)}, u32[]{:S(2)}) collective-permute-start(f32[144,128]{1,0:T(8,128)S(1)} %get-tuple-element.22), channel_id=1, source_target_pairs={{0,2},{1,3},{2,0},{3,1},{4,6},{5,7},{6,4},{7,5},{8,10},{9,11},{10,... | collective-permute-start | bytes 221192 | tf_op jit(solution)/shard_map/ppermute | solution.py:235
  63.2 8.3 %collective-permute-start.11 = (f32[144,128]{1,0:T(8,128)S(1)}, f32[144,128]{1,0:T(8,128)S(1)}, u32[]{:S(2)}, u32[]{:S(2)}) collective-permute-start(f32[144,128]{1,0:T(8,128)S(1)} %get-tuple-element.23), channel_id=1, source_target_pairs={{0,3},{1,2},{2,1},{3,0},{4,7},{5,6},{6,5},{7,4},{8,11},{9,10},{10,... | collective-permute-start | bytes 221192 | tf_op jit(solution)/shard_map/ppermute | solution.py:235
  63.8 10.4 %collective-permute-start.12 = (f32[144,128]{1,0:T(8,128)S(1)}, f32[144,128]{1,0:T(8,128)S(1)}, u32[]{:S(2)}, u32[]{:S(2)}) collective-permute-start(f32[144,128]{1,0:T(8,128)S(1)} %get-tuple-element.24), channel_id=1, source_target_pairs={{0,4},{1,5},{2,6},{3,7},{4,0},{5,1},{6,2},{7,3},{8,12},{9,13},{10,... | collective-permute-start | bytes 221192 | tf_op jit(solution)/shard_map/ppermute | solution.py:235
  65.9 11.4 %collective-permute-start.13 = (f32[144,128]{1,0:T(8,128)S(1)}, f32[144,128]{1,0:T(8,128)S(1)}, u32[]{:S(2)}, u32[]{:S(2)}) collective-permute-start(f32[144,128]{1,0:T(8,128)S(1)} %get-tuple-element.25), channel_id=1, source_target_pairs={{0,5},{1,4},{2,7},{3,6},{4,1},{5,0},{6,3},{7,2},{8,13},{9,12},{10,... | collective-permute-start | bytes 221192 | tf_op jit(solution)/shard_map/ppermute | solution.py:235
  67.7 9.7 %collective-permute-start.14 = (f32[144,128]{1,0:T(8,128)S(1)}, f32[144,128]{1,0:T(8,128)S(1)}, u32[]{:S(2)}, u32[]{:S(2)}) collective-permute-start(f32[144,128]{1,0:T(8,128)S(1)} %get-tuple-element.26), channel_id=1, source_target_pairs={{0,6},{1,7},{2,4},{3,5},{4,2},{5,3},{6,0},{7,1},{8,14},{9,15},{10,... | collective-permute-start | bytes 221192 | tf_op jit(solution)/shard_map/ppermute | solution.py:235
  69.9 7.5 %collective-permute-start.15 = (f32[144,128]{1,0:T(8,128)S(1)}, f32[144,128]{1,0:T(8,128)S(1)}, u32[]{:S(2)}, u32[]{:S(2)}) collective-permute-start(f32[144,128]{1,0:T(8,128)S(1)} %get-tuple-element.27), channel_id=1, source_target_pairs={{0,7},{1,6},{2,5},{3,4},{4,3},{5,2},{6,1},{7,0},{8,15},{9,14},{10,... | collective-permute-start | bytes 221192 | tf_op jit(solution)/shard_map/ppermute | solution.py:235
  71.4 5.9 %collective-permute-start.9 = (f32[144,128]{1,0:T(8,128)S(1)}, f32[144,128]{1,0:T(8,128)S(1)}, u32[]{:S(2)}, u32[]{:S(2)}) collective-permute-start(f32[144,128]{1,0:T(8,128)S(1)} %get-tuple-element.21), channel_id=1, source_target_pairs={{0,1},{1,0},{2,3},{3,2},{4,5},{5,4},{6,7},{7,6},{8,9},{9,8},{10,11... | collective-permute-start | bytes 221192 | tf_op jit(solution)/shard_map/ppermute | solution.py:235
  86.7 7.1 %collective-permute-start.16 = (f32[136,128]{1,0:T(8,128)S(1)}, f32[136,128]{1,0:T(8,128)S(1)}, u32[]{:S(2)}, u32[]{:S(2)}) collective-permute-start(f32[136,128]{1,0:T(8,128)S(1)} %get-tuple-element.29), channel_id=1, source_target_pairs={{0,1},{1,0},{2,3},{3,2},{4,5},{5,4},{6,7},{7,6},{8,9},{9,8},{10,11... | collective-permute-start | bytes 208904 | tf_op jit(solution)/shard_map/ppermute | solution.py:235
  87.8 8.5 %collective-permute-start.17 = (f32[136,128]{1,0:T(8,128)S(1)}, f32[136,128]{1,0:T(8,128)S(1)}, u32[]{:S(2)}, u32[]{:S(2)}) collective-permute-start(f32[136,128]{1,0:T(8,128)S(1)} %get-tuple-element.30), channel_id=1, source_target_pairs={{0,2},{1,3},{2,0},{3,1},{4,6},{5,7},{6,4},{7,5},{8,10},{9,11},{10,... | collective-permute-start | bytes 208904 | tf_op jit(solution)/shard_map/ppermute | solution.py:235
  89.7 8.5 %collective-permute-start.18 = (f32[136,128]{1,0:T(8,128)S(1)}, f32[136,128]{1,0:T(8,128)S(1)}, u32[]{:S(2)}, u32[]{:S(2)}) collective-permute-start(f32[136,128]{1,0:T(8,128)S(1)} %get-tuple-element.31), channel_id=1, source_target_pairs={{0,3},{1,2},{2,1},{3,0},{4,7},{5,6},{6,5},{7,4},{8,11},{9,10},{10,... | collective-permute-start | bytes 208904 | tf_op jit(solution)/shard_map/ppermute | solution.py:235
  90.4 10.3 %collective-permute-start.19 = (f32[136,128]{1,0:T(8,128)S(1)}, f32[136,128]{1,0:T(8,128)S(1)}, u32[]{:S(2)}, u32[]{:S(2)}) collective-permute-start(f32[136,128]{1,0:T(8,128)S(1)} %get-tuple-element.32), channel_id=1, source_target_pairs={{0,4},{1,5},{2,6},{3,7},{4,0},{5,1},{6,2},{7,3},{8,12},{9,13},{10,... | collective-permute-start | bytes 208904 | tf_op jit(solution)/shard_map/ppermute | solution.py:235
  92.8 9.6 %collective-permute-start.20 = (f32[136,128]{1,0:T(8,128)S(1)}, f32[136,128]{1,0:T(8,128)S(1)}, u32[]{:S(2)}, u32[]{:S(2)}) collective-permute-start(f32[136,128]{1,0:T(8,128)S(1)} %get-tuple-element.33), channel_id=1, source_target_pairs={{0,5},{1,4},{2,7},{3,6},{4,1},{5,0},{6,3},{7,2},{8,13},{9,12},{10,... | collective-permute-start | bytes 208904 | tf_op jit(solution)/shard_map/ppermute | solution.py:235
  93.8 8.7 %collective-permute-start.21 = (f32[136,128]{1,0:T(8,128)S(1)}, f32[136,128]{1,0:T(8,128)S(1)}, u32[]{:S(2)}, u32[]{:S(2)}) collective-permute-start(f32[136,128]{1,0:T(8,128)S(1)} %get-tuple-element.34), channel_id=1, source_target_pairs={{0,6},{1,7},{2,4},{3,5},{4,2},{5,3},{6,0},{7,1},{8,14},{9,15},{10,... | collective-permute-start | bytes 208904 | tf_op jit(solution)/shard_map/ppermute | solution.py:235
  96.2 7.1 %collective-permute-start.22 = (f32[136,128]{1,0:T(8,128)S(1)}, f32[136,128]{1,0:T(8,128)S(1)}, u32[]{:S(2)}, u32[]{:S(2)}) collective-permute-start(f32[136,128]{1,0:T(8,128)S(1)} %get-tuple-element.35), channel_id=1, source_target_pairs={{0,7},{1,6},{2,5},{3,4},{4,3},{5,2},{6,1},{7,0},{8,15},{9,14},{10,... | collective-permute-start | bytes 208904 | tf_op jit(solution)/shard_map/ppermute | solution.py:235
  103.4 1.3 %collective-permute-start.23 = (bf16[16,1024]{1,0:T(8,128)(2,1)S(1)}, bf16[16,1024]{1,0:T(8,128)(2,1)S(1)}, u32[]{:S(2)}, u32[]{:S(2)}) collective-permute-start(bf16[16,1024]{1,0:T(8,128)(2,1)S(1)} %get-tuple-element.37), channel_id=1, source_target_pairs={{0,8},{8,0},{1,9},{9,1},{2,10},{10,2},{3,11},{11,3},{4,12},{12,4},... | collective-permute-start | bytes 98312 | tf_op jit(solution)/shard_map/ppermute | solution.py:441
  (6 other events, 18.9 us)

commit v3 on v2

--- a/solution.py
+++ b/solution.py
@@ -44,19 +44,98 @@
     return pl.ds(pl.multiple_of(index * size, size), size)
 
 
-def project_kernel(pages, per_page, width, meta_ref, own_ref, far_ref, take_ref, gain_ref, wq_ref, wkv_ref, out_ref, tokens, wq, wkv, sems):
-    me = meta_ref[0]
+def plan_kernel(slots, steps, map_ref, length_ref, meta_ref, take_ref, give_ref, before_ref, place_ref):
+    count = map_ref.shape[0]
+    mine = lax.axis_index("dp")
+    base = mine * slots
+    for block in range(count // slots):
+        found = jnp.int32(0)
+        for s in range(block * slots, (block + 1) * slots):
+            before_ref[s] = found
+            found = found + (map_ref[s] == s).astype(jnp.int32)
+    for s in range(slots):
+        own = map_ref[base + s] == base + s
+
+        @pl.when(own)
+        def _():
+            slot = before_ref[base + s]
+            meta_ref[slot] = jnp.int32(s)
+            meta_ref[slots // PAIR + slot] = length_ref[base + s]
+
+    for r in range(count):
+        source = map_ref[r]
+        place_ref[r] = (
+            lax.div(source, slots) * slots
+            + PAIR * before_ref[source]
+            + (source != r).astype(jnp.int32)
+        )
+    rows = slots * steps
+    line, col = iota((rows, 2 * rows), 0), iota((rows, 2 * rows), 1)
+    same = line % steps == (col // slots) % steps
+    take = jnp.zeros((rows, 2 * rows), jnp.bool_)
+    give = jnp.zeros((rows, 2 * rows), jnp.bool_)
+    for side in range(2):
+        start = base if side == 0 else (1 - mine) * slots
+        for s in range(slots):
+            target = place_ref[start + s] - base
+            column = (col // rows == side) & (col % slots == s)
+            take = take | (same & column & (line // steps == target))
+    for s in range(slots):
+        place = place_ref[base + s]
+        far = (lax.div(place, slots) != mine).astype(jnp.int32)
+        target = far * rows + lax.rem(place, slots) * steps
+        give = give | ((line % slots == s) & (col == line // slots + target))
+    take_ref[...] = take.astype(jnp.float32).astype(jnp.bfloat16)
+    give_ref[...] = give.astype(jnp.float32).astype(jnp.bfloat16)
+
+
+def pull_kernel(after_ref, src_ref, out_ref, sems):
+    parts = sems.shape[0]
+    size = src_ref.shape[0] // parts
+    copies = [
+        pltpu.make_async_copy(
+            src_ref.at[pl.ds(p * size, size)], out_ref.at[pl.ds(p * size, size)], sems.at[p]
+        )
+        for p in range(parts)
+    ]
+    for copy in copies:
+        copy.start()
+    for copy in copies:
+        copy.wait()
+
+
+def side_kernel(pages, after_ref, meta_ref, k_ref, v_ref, hidden_ref, gain_ref, head_ref, keys_ref, values_ref, squares_ref, dots_ref, buffer, sems, page_sems):
+    slots = hidden_ref.shape[0]
+    loads = [
+        pltpu.make_async_copy(hidden_ref.at[s], buffer.at[s], sems.at[s]) for s in range(slots)
+    ]
+    for load in loads:
+        load.start()
+    copies = []
+    for i in range(pages):
+        page = meta_ref[i]
+        copies.append(pltpu.make_async_copy(k_ref.at[page], keys_ref.at[i], page_sems.at[0, i]))
+        copies.append(pltpu.make_async_copy(v_ref.at[page], values_ref.at[i], page_sems.at[1, i]))
+    for copy in copies:
+        copy.start()
+    weight = gain_ref[...] * head_ref[...]
+    for s in range(slots):
+        loads[s].wait()
+        hidden = buffer[s].astype(jnp.float32)
+        squares_ref[s] = jnp.sum(hidden * hidden, axis=-1)
+        dots_ref[s] = jnp.sum(hidden * weight, axis=-1)
+    for copy in copies:
+        copy.wait()
+
+
+def project_kernel(pages, per_page, width, own_ref, far_ref, take_ref, gain_ref, wq_ref, wkv_ref, out_ref, tokens, wkv, sems):
+    me = lax.axis_index("tensor")
     chunks, rows, depth = own_ref.shape
     copies = []
     for r in range(chunks):
-        source = aligned(me ^ r, depth)
-        pair = (
-            pltpu.make_async_copy(wq_ref.at[source], wq.at[r], sems.at[0, r]),
-            pltpu.make_async_copy(wkv_ref.at[source], wkv.at[r], sems.at[1, r]),
-        )
-        for copy in pair:
-            copy.start()
-        copies.append(pair)
+        copy = pltpu.make_async_copy(wkv_ref.at[aligned(me ^ r, depth)], wkv.at[r], sems.at[r])
+        copy.start()
+        copies.append(copy)
 
     total = jnp.zeros((rows, depth), jnp.float32)
     for r in range(chunks):
@@ -66,13 +145,12 @@
         total = total + part * part
     inv = lax.rsqrt(jnp.sum(total, axis=-1, keepdims=True) / width + EPS)
 
-    query = jnp.zeros((rows, wq.shape[2]), jnp.float32)
+    query = jnp.zeros((rows, wq_ref.shape[1]), jnp.float32)
     keyval = jnp.zeros((rows, wkv.shape[2]), jnp.float32)
     for r in range(chunks):
         normed = (tokens[r].astype(jnp.float32) * inv * gain_ref[me ^ r]).astype(jnp.bfloat16)
-        for copy in copies[r]:
-            copy.wait()
-        query = query + dot(normed, wq[r])
+        query = query + dot(normed, wq_ref[aligned(me ^ r, depth), :])
+        copies[r].wait()
         keyval = keyval + dot(normed, wkv[r])
 
     heads = query.shape[1] // HD
@@ -90,37 +168,26 @@
         out_ref[body + v * rows : body + (v + 1) * rows] = keyval[:, v * LANES : (v + 1) * LANES]
 
 
-def attend_kernel(pages, page_rows, meta_ref, q_ref, k_ref, v_ref, reward_ref, *rest):
-    outs, (spread, product, keys, values, sems) = rest[:-5], rest[-5:]
+def attend_kernel(pages, page_rows, split, meta_ref, q_ref, k_ref, v_ref, squares_ref, dots_ref, *rest):
+    outs, (spread, product) = rest[:-2], rest[-2:]
     width = k_ref.shape[1]
     span = KVH * page_rows
     body = pages * page_rows
-    copies = []
-    for i in range(pages):
-        pair = (
-            pltpu.make_async_copy(k_ref.at[meta_ref[i]], keys.at[i], sems.at[0, i]),
-            pltpu.make_async_copy(v_ref.at[meta_ref[i]], values.at[i], sems.at[1, i]),
-        )
-        for copy in pair:
-            copy.start()
-        copies.append(pair)
-
-    me = meta_ref[2 * pages + 1]
+    first = lax.axis_index("tensor") * width
+    me = lax.axis_index("tensor") if len(outs) > 1 else 0
     spread[...] = jnp.zeros_like(spread)
     for i in range(pages):
         for r in range(KVH):
             spread[r * page_rows : (r + 1) * page_rows, aligned(me ^ r, HD)] = q_ref[
                 r, i * page_rows : (i + 1) * page_rows, :
             ]
-        copies[i][0].wait()
-        scores = dot(keys[i], spread[...], NT) * SCALE
-        valid = meta_ref[2 * pages] + iota((width, span), 0) < meta_ref[pages + i]
+        scores = dot(k_ref[i], spread[...], NT) * SCALE
+        valid = first + iota((width, span), 0) < meta_ref[pages + i]
         scores = jnp.where(valid, scores, NEG)
         top = jnp.max(scores, axis=0, keepdims=True)
         expo = jnp.where(valid, jnp.exp(scores - top), 0.0)
         total = jnp.sum(expo, axis=0, keepdims=True)
-        copies[i][1].wait()
-        product[...] = dot(expo.astype(jnp.bfloat16), values[i], TN)
+        product[...] = dot(expo.astype(jnp.bfloat16), v_ref[i], TN)
         for r in range(KVH):
             out = outs[r] if len(outs) > 1 else outs[0].at[r]
             out[i * page_rows : (i + 1) * page_rows, :] = product[
@@ -131,24 +198,39 @@
             out[body + pages + i : body + pages + i + 1, :] = total[:, lane : lane + LANES]
     for r in range(KVH):
         if len(outs) > 1:
-            outs[r][body + EXT :, :] = reward_ref[me ^ r]
+            outs[r][body + EXT :, :] = jnp.concatenate(
+                [squares_ref[me ^ r], dots_ref[me ^ r]], axis=0
+            )
         else:
             outs[0][r, body + EXT :, :] = jnp.zeros((EXT, LANES), jnp.float32)
 
 
-def merge_kernel(pages, per_page, width, span, chunks, meta_ref, q_ref, fk_ref, fv_ref, w_ref, *rest):
+def merge_kernel(pages, per_page, width, span, slots, chunks, q_ref, gathered_ref, w_ref, *rest):
     att = rest[-1]
     split = len(rest) > 3
     parts = rest[:chunks] if split else [rest[0].at[b] for b in range(chunks)]
     outs = rest[chunks:-1] if split else rest[1:-1]
-    me = meta_ref[0]
+    me = lax.axis_index("tensor")
     body = parts[0].shape[0] - 2 * EXT
     page_rows = body // pages
     heads = page_rows // per_page
     rows = pages * per_page
 
+    kv_head = lax.div(me * heads, heads * chunks // KVH)
+    if split:
+        pieces = (gathered_ref.shape[1] - body) // rows
+
+        def fresh_of(column):
+            source = lax.div(column, pieces) ^ me
+            start = pl.multiple_of(body + lax.rem(column, pieces) * rows, rows)
+            return gathered_ref[source, pl.ds(start, rows), :]
+
+        fresh_k, fresh_v = fresh_of(kv_head), fresh_of(KVH + kv_head)
+    else:
+        fresh_k, fresh_v = gathered_ref[kv_head], gathered_ref[KVH + kv_head]
+
     query = q_ref[:body, :]
-    recent = dot(query, fk_ref[...], NT) * SCALE
+    recent = dot(query, fresh_k, NT) * SCALE
     line, col = iota(recent.shape, 0), iota(recent.shape, 1)
     mine = (line // page_rows) * per_page + line % per_page
     seen = (mine // STEPS == col // STEPS) & (col <= mine)
@@ -156,7 +238,7 @@
     recent_max = jnp.max(recent, axis=-1, keepdims=True)
     recent_exp = jnp.where(seen, jnp.exp(recent - recent_max), 0.0)
     recent_total = jnp.sum(recent_exp, axis=-1, keepdims=True)
-    recent_acc = dot(recent_exp.astype(jnp.bfloat16), fv_ref[...])
+    recent_acc = dot(recent_exp.astype(jnp.bfloat16), fresh_v)
 
     extras = []
     for b in range(chunks):
@@ -165,7 +247,8 @@
             shift = -(b * page_rows) % LANES
             extras.append(pltpu.roll(extra, shift, 1) if shift else extra)
         else:
-            extras.append(pltpu.roll(extra, meta_ref[2], 1))
+            shift = lax.rem(LANES - lax.rem(me * page_rows, LANES), LANES)
+            extras.append(pltpu.roll(extra, shift, 1))
     maxima = [extra[:pages] for extra in extras]
     totals = [extra[pages : 2 * pages] for extra in extras]
     top = functools.reduce(jnp.maximum, maxima)
@@ -206,7 +289,8 @@
     used = EXT // 2
     value = tile[used:] * lax.rsqrt(tile[:used] / width + EPS)
     mean = jnp.sum(value, keepdims=True) / span
-    mean = jnp.where(iota((EXT, LANES), 0) == meta_ref[1], mean, 0.0)
+    own = lax.div(me * (slots * span // chunks), span)
+    mean = jnp.where(iota((EXT, LANES), 0) == own, mean, 0.0)
 
     part = w_ref.shape[1] // chunks
     for r in range(chunks):
@@ -238,10 +322,10 @@
 def spread_all(x, chunks, index):
     if chunks != KVH:
         every = lax.all_to_all(jnp.broadcast_to(x[None], (chunks,) + x.shape), "tensor", 0, 0, tiled=True)
-        return jnp.take(every, index ^ jnp.arange(chunks), axis=0)
+        return jnp.take(every, index ^ jnp.arange(chunks), axis=0), x
     pair = jnp.stack([x, partner(x, chunks, 1)])
     others = [partner(pair, chunks, bits) for bits in (2, 4, 6)]
-    return jnp.stack([pair] + others).reshape((chunks,) + x.shape)
+    return jnp.stack([pair] + others).reshape((chunks,) + x.shape), pair
 
 
 def trade(blocks, chunks):
@@ -278,41 +362,89 @@
     page_rows = per_page * group
     rows = slots * STEPS
     body = rows * heads
-    mine, index = lax.axis_index("dp"), lax.axis_index("tensor")
+    index = lax.axis_index("tensor")
     swap = [(0, 1), (1, 0)]
-
-    ids = jnp.arange(slot_map.shape[0])
-    kept = slot_map == ids
-    home = slot_map // slots
-    before = kept[None, :] & (ids[None, :] // slots == home[:, None]) & (ids[None, :] < slot_map[:, None])
-    place = home * slots + PAIR * jnp.sum(before, axis=1) + (slot_map != ids)
-    place_own = lax.dynamic_slice_in_dim(place, mine * slots, slots)
-    place_far = lax.dynamic_slice_in_dim(place, (1 - mine) * slots, slots)
-    lead = place[None, :] == (mine * slots + PAIR * jnp.arange(pages))[:, None]
-    page = jnp.sum(jnp.where(lead, ids[None, :], 0), axis=1) - mine * slots
-    live = jnp.sum(jnp.where(lead, lengths[None, :], 0), axis=1)
-    work = jnp.arange(rows)
-    steps = jnp.arange(STEPS)
-    both = jnp.stack([place_own, place_far]) - mine * slots
-    take = (both[None, None, :, None, :] == jnp.arange(slots)[:, None, None, None, None]) & (
-        steps[None, :, None, None, None] == steps[None, None, None, :, None]
-    )
-    take = take.reshape(rows, 2 * rows).astype(jnp.bfloat16)
-    bases = jnp.stack([mine, 1 - mine]) * slots
-    give = (
-        (place_own[None, :, None] - bases[None, None, :])[..., None, None]
-        == jnp.arange(slots)[None, None, None, :, None]
-    ) & (steps[:, None, None, None, None] == steps[None, None, None, None, :])
-    give = give.reshape(rows, 2 * rows).astype(jnp.bfloat16)
-
     direct = chunks == KVH
-    own = spread_all(decode_inputs.reshape(rows, part), chunks, index)
+
+    meta, take, give = pl.pallas_call(
+        functools.partial(plan_kernel, slots, STEPS),
+        in_specs=[SMEM, SMEM],
+        out_specs=[SMEM, VMEM, VMEM],
+        out_shape=(
+            jax.ShapeDtypeStruct((2 * pages,), jnp.int32),
+            jax.ShapeDtypeStruct((rows, 2 * rows), jnp.bfloat16),
+            jax.ShapeDtypeStruct((rows, 2 * rows), jnp.bfloat16),
+        ),
+        scratch_shapes=[
+            pltpu.SMEM(slot_map.shape, jnp.int32),
+            pltpu.SMEM(slot_map.shape, jnp.int32),
+        ],
+        compiler_params=pltpu.CompilerParams(vmem_limit_bytes=MIB),
+        name="plan",
+    )(slot_map, lengths)
+
+    own, after = spread_all(decode_inputs.reshape(rows, part), chunks, index)
+    w_query = pl.pallas_call(
+        pull_kernel,
+        in_specs=[ANY, ANY],
+        out_specs=VMEM,
+        out_shape=pltpu.VMEM(w_query.shape, w_query.dtype),
+        scratch_shapes=[pltpu.SemaphoreType.DMA((KVH,))],
+        compiler_params=pltpu.CompilerParams(vmem_limit_bytes=46 * MIB),
+        cost_estimate=pl.CostEstimate(
+            flops=0, bytes_accessed=4 * depth * qcols, transcendentals=0
+        ),
+        name="pull",
+    )(after, w_query)
     far = lax.ppermute(own, "dp", swap)
 
-    hidden = reward_hidden.astype(jnp.float32)
-    squares = jnp.sum(hidden * hidden, axis=-1)
-    head_dot = jnp.sum(hidden * (reward_gain * reward_head), axis=-1)
-    span = squares.shape[1]
+    pieces = max(kvcols // LANES, 1)
+    packed_rows = body + pieces * rows
+    packed = pl.pallas_call(
+        functools.partial(project_kernel, pages, per_page, depth),
+        in_specs=[VMEM, VMEM, VMEM, VMEM, VMEM, ANY],
+        out_specs=VMEM,
+        out_shape=jax.ShapeDtypeStruct((packed_rows, LANES), jnp.bfloat16),
+        scratch_shapes=[
+            pltpu.VMEM((chunks, rows, part), jnp.bfloat16),
+            pltpu.VMEM((chunks, part, kvcols), jnp.bfloat16),
+            pltpu.SemaphoreType.DMA((chunks,)),
+        ],
+        compiler_params=pltpu.CompilerParams(vmem_limit_bytes=46 * MIB),
+        cost_estimate=pl.CostEstimate(
+            flops=2 * rows * depth * (qcols + kvcols),
+            bytes_accessed=2 * depth * (qcols + kvcols),
+            transcendentals=0,
+        ),
+        name="project",
+    )(own, far, take, attn_gain.reshape(chunks, 1, part), w_query, w_keyval)
+    gathered, after = spread_all(packed, chunks, index)
+
+    span = reward_hidden.shape[1]
+    page_shape = (pages,) + cache_keys.shape[1:]
+    keys, values, squares, dots = pl.pallas_call(
+        functools.partial(side_kernel, pages),
+        in_specs=[ANY, SMEM, ANY, ANY, ANY, VMEM, VMEM],
+        out_specs=[VMEM] * 4,
+        out_shape=(
+            pltpu.VMEM(page_shape, cache_keys.dtype),
+            pltpu.VMEM(page_shape, cache_values.dtype),
+            jax.ShapeDtypeStruct((slots, span), jnp.float32),
+            jax.ShapeDtypeStruct((slots, span), jnp.float32),
+        ),
+        scratch_shapes=[
+            pltpu.VMEM(reward_hidden.shape, reward_hidden.dtype),
+            pltpu.SemaphoreType.DMA((slots,)),
+            pltpu.SemaphoreType.DMA((2, pages)),
+        ],
+        compiler_params=pltpu.CompilerParams(vmem_limit_bytes=40 * MIB),
+        cost_estimate=pl.CostEstimate(
+            flops=4 * reward_hidden.size,
+            bytes_accessed=2 * reward_hidden.size + 8 * pages * width * KVH * HD,
+            transcendentals=0,
+        ),
+        name="side",
+    )(after, meta, cache_keys, cache_values, reward_hidden, reward_gain[None], reward_head[None])
 
     def tile(values):
         values = values.reshape(chunks, -1)
@@ -321,44 +453,11 @@
             chunks, EXT // 2, LANES
         )
 
-    reward_parts = jnp.concatenate([tile(squares), tile(head_dot)], axis=1)
-
-    pieces = max(kvcols // LANES, 1)
-    packed_rows = body + pieces * rows
-    packed = pl.pallas_call(
-        functools.partial(project_kernel, pages, per_page, depth),
-        in_specs=[SMEM, VMEM, VMEM, VMEM, VMEM, ANY, ANY],
-        out_specs=VMEM,
-        out_shape=jax.ShapeDtypeStruct((packed_rows, LANES), jnp.bfloat16),
-        scratch_shapes=[
-            pltpu.VMEM((chunks, rows, part), jnp.bfloat16),
-            pltpu.VMEM((chunks, part, qcols), jnp.bfloat16),
-            pltpu.VMEM((chunks, part, kvcols), jnp.bfloat16),
-            pltpu.SemaphoreType.DMA((2, chunks)),
-        ],
-        compiler_params=pltpu.CompilerParams(vmem_limit_bytes=28 * MIB),
-        cost_estimate=pl.CostEstimate(
-            flops=2 * rows * depth * (qcols + kvcols),
-            bytes_accessed=2 * depth * (qcols + kvcols),
-            transcendentals=0,
-        ),
-        name="project",
-    )(index[None], own, far, take, attn_gain.reshape(chunks, 1, part), w_query, w_keyval)
-    gathered = spread_all(packed, chunks, index)
-
-    kv_head = index * heads // group
-    if kvcols < LANES:
+    squares, dots = tile(squares), tile(dots)
+    fresh = gathered
+    if not direct:
         fresh = jnp.take(gathered[:, body:, :kvcols], index ^ jnp.arange(chunks), axis=0)
         fresh = fresh.transpose(1, 0, 2).reshape(rows, 2 * KVH, HD).transpose(1, 0, 2)
-        fresh_k = lax.dynamic_index_in_dim(fresh, kv_head, 0, keepdims=False)
-        fresh_v = lax.dynamic_index_in_dim(fresh, KVH + kv_head, 0, keepdims=False)
-    else:
-
-        def fresh_of(column):
-            start = (column // pieces) ^ index, body + column % pieces * rows, 0
-            return lax.dynamic_slice(gathered, start, (1, rows, LANES))[0]
-
-        fresh_k, fresh_v = fresh_of(kv_head), fresh_of(KVH + kv_head)
     queries = gathered
     if not direct:
         queries = (
@@ -368,13 +467,11 @@
             .reshape(KVH, pages * page_rows, HD)
         )
 
-    base = index if direct else index * 0
-    meta = jnp.concatenate([page, live, (index * width)[None], base[None]]).astype(jnp.int32)
     big = pages * page_rows
     block = (big + 2 * EXT, HD)
     attended = pl.pallas_call(
-        functools.partial(attend_kernel, pages, page_rows),
-        in_specs=[SMEM, VMEM, ANY, ANY, VMEM],
+        functools.partial(attend_kernel, pages, page_rows, split),
+        in_specs=[SMEM] + [VMEM] * 5,
         out_specs=[VMEM] * (KVH if direct else 1),
         out_shape=(
             [jax.ShapeDtypeStruct(block, jnp.float32)] * KVH
@@ -384,9 +481,6 @@
         scratch_shapes=[
             pltpu.VMEM((KVH * page_rows, KVH * HD), jnp.bfloat16),
             pltpu.VMEM((KVH * page_rows, KVH * HD), jnp.float32),
-            pltpu.VMEM((pages, width, KVH * HD), jnp.bfloat16),
-            pltpu.VMEM((pages, width, KVH * HD), jnp.bfloat16),
-            pltpu.SemaphoreType.DMA((2, pages)),
         ],
         compiler_params=pltpu.CompilerParams(vmem_limit_bytes=12 * MIB),
         cost_estimate=pl.CostEstimate(
@@ -395,7 +489,7 @@
             transcendentals=pages * width * KVH * page_rows,
         ),
         name="attend",
-    )(meta, queries, cache_keys, cache_values, reward_parts)
+    )(meta, queries, keys, values, squares, dots)
     if not direct:
         acc = (
             attended[0][:, :big]
@@ -404,16 +498,13 @@
             .reshape(chunks, body, HD)
         )
         extra = jnp.repeat(attended[0][:, big : big + EXT], split, axis=0)
-        attended = [jnp.concatenate([acc, extra, reward_parts], axis=1)]
+        attended = [jnp.concatenate([acc, extra, squares, dots], axis=1)]
     parts = trade(attended, chunks)
 
     chunk_rows = part // LANES * rows + EXT
-    own_row = index * (slots * span // chunks) // span
-    shift = -(index * heads * per_page) % LANES
-    meta = jnp.stack([index, own_row, shift]).astype(jnp.int32)
     partial = pl.pallas_call(
-        functools.partial(merge_kernel, pages, per_page, depth, span, chunks),
-        in_specs=[SMEM] + [VMEM] * (4 + len(parts)),
+        functools.partial(merge_kernel, pages, per_page, depth, span, slots, chunks),
+        in_specs=[VMEM] * (3 + len(parts)),
         out_specs=[VMEM] * len(parts),
         out_shape=(
             [jax.ShapeDtypeStruct((chunk_rows, LANES), jnp.float32)] * chunks
@@ -426,7 +517,7 @@
             flops=2 * rows * qcols * depth, bytes_accessed=2 * qcols * depth, transcendentals=0
         ),
         name="merge",
-    )(meta, packed, fresh_k, fresh_v, w_out, *parts)
+    )(packed, fresh, w_out, *parts)
     partial = trade(partial, chunks)
 
     decoded, reward = pl.pallas_call(

time: 106 us -> 106 us (level)
  Pallas kernels: 14.2 us -> 27.5 us
  other arithmetic: 9.44 us -> 0.86 us
  waiting for transfers between devices: 25 us -> 20.7 us
  starting transfers between devices: 35.2 us -> 36.8 us
  local copies, waits for them, and re-layouts: 19.9 us -> 18.6 us
    pallas_call x1 -> x4, Pallas kernels: 4.93 us -> 13.9 us  [the longest x1 5.93 us: local(): pl.pallas_call(pull_kernel, in_specs=[ANY, ANY], out_specs=VMEM, out_shap...]
    reduce_sum x3 -> x0, other arithmetic: 5.35 us -> none  [the longest x1 3.64 us: local(): squares = jnp.sum(hidden * hidden, axis=-1)]
    pallas_call x1, Pallas kernels: 5.72 us -> 10.7 us  [local(): pl.pallas_call(functools.partial(project_kernel, pages, per_page, depth),...]
    ppermute x22, waiting for transfers between devices: 23.2 us -> 20.1 us  [partner(): return lax.ppermute(x, 'tensor', [(i, i ^ bits) for i in range(chunks)])]
    ppermute x22, starting transfers between devices: 35.1 us -> 36.6 us  [partner(): return lax.ppermute(x, 'tensor', [(i, i ^ bits) for i in range(chunks)])]
    ppermute x1, waiting for transfers between devices: 1.24 us -> 0.01 us  [local(): far = lax.ppermute(own, 'dp', swap)]
    unnamed x12 -> x26, local copies, waits for them, and re-layouts: 18.8 us -> 18 us
  transfers between devices with their start and end apart: 24 -> 24, of which waited for: 11 -> 11; matrix products, arithmetic and copies ran while one was open for 9% -> 1% of each run, Pallas kernels for 0% -> 10%
where the time goes in v3:
time: 106 us
  starting transfers between devices  36.8 us (35%)
  Pallas kernels  27.5 us (26%)
  waiting for transfers between devices  20.7 us (20%)
  local copies, waits for them, and re-layouts  18.6 us (18%)
    ppermute x22, starting transfers between devices, partner(): return lax.ppermute(x, 'tensor', [(i, i ^ bits) for i in range(chunks)])  36.6 us
    ppermute x22, waiting for transfers between devices, partner(): return lax.ppermute(x, 'tensor', [(i, i ^ bits) for i in range(chunks)])  20.1 us
    unnamed x26, local copies, waits for them, and re-layouts  18 us
    pallas_call x1, Pallas kernels, local(): pl.pallas_call(functools.partial(project_kernel, pages, per_page, depth),...  10.7 us
    pallas_call x1, Pallas kernels, local(): pl.pallas_call(pull_kernel, in_specs=[ANY, ANY], out_specs=VMEM, out_shap...  5.93 us
    pallas_call x1, Pallas kernels, local(): pl.pallas_call(functools.partial(side_kernel, pages), in_specs=[ANY, SMEM...  3.71 us
    pallas_call x1, Pallas kernels, local(): pl.pallas_call(functools.partial(merge_kernel, pages, per_page, depth, sp...  2.99 us
    pallas_call x1, Pallas kernels, local(): pl.pallas_call(functools.partial(attend_kernel, pages, page_rows, split),...  2.89 us
  transfers between devices with their start and end apart: 24, of which 11 were waited for; matrix products, arithmetic and copies ran while one was open for 1% of the time, Pallas kernels for 10%

profile of v3, /device:TPU:0, one launch (start us, length us, event | category | flops | bytes accessed | tf_op | source)
XLA Modules:
  0.0 106.1 jit_solution(12736909974945689951)
XLA Ops:
  0.6 3.1 %collective-permute-start = (bf16[16,1024]{1,0:T(8,128)(2,1)}, bf16[16,1024]{1,0:T(8,128)(2,1)S(1)}, u32[]{:S(2)}, u32[]{:S(2)}) collective-permute-start(bf16[16,1024]{1,0:T(8,128)(2,1)} %bitcast.38), channel_id=1, source_target_pairs={{0,1},{1,0},{2,3},{3,2},{4,5},{5,4},{6,7},{7,6},{8,9},{9,8},{10,11... | collective-permute-start | bytes 98312 | tf_op jit(solution)/shard_map/ppermute | solution.py:319
  3.7 2.1 %collective-permute-done = bf16[16,1024]{1,0:T(8,128)(2,1)S(1)} collective-permute-done((bf16[16,1024]{1,0:T(8,128)(2,1)}, bf16[16,1024]{1,0:T(8,128)(2,1)S(1)}, u32[]{:S(2)}, u32[]{:S(2)}) %collective-permute-start) | collective-permute-done | bytes 32800 | tf_op jit(solution)/shard_map/ppermute | solution.py:319
  6.6 2.1 %collective-permute-start.1 = (bf16[2,16,1024]{2,1,0:T(8,128)(2,1)S(1)}, bf16[2,16,1024]{2,1,0:T(8,128)(2,1)S(1)}, u32[]{:S(2)}, u32[]{:S(2)}) collective-permute-start(bf16[2,16,1024]{2,1,0:T(8,128)(2,1)S(1)} %get-tuple-element.55.after_ref), channel_id=1, source_target_pairs={{0,2},{1,3},{2,0},{3,1},{4,6},{5,7},{6,4},{7,5},{8,10},{9,11},{10,... | collective-permute-start | bytes 196616 | tf_op jit(solution)/shard_map/ppermute | solution.py:319
  8.7 2.6 %collective-permute-start.2 = (bf16[2,16,1024]{2,1,0:T(8,128)(2,1)S(1)}, bf16[2,16,1024]{2,1,0:T(8,128)(2,1)S(1)}, u32[]{:S(2)}, u32[]{:S(2)}) collective-permute-start(bf16[2,16,1024]{2,1,0:T(8,128)(2,1)S(1)} %get-tuple-element.55.after_ref), channel_id=1, source_target_pairs={{0,4},{1,5},{2,6},{3,7},{4,0},{5,1},{6,2},{7,3},{8,12},{9,13},{10,... | collective-permute-start | bytes 196616 | tf_op jit(solution)/shard_map/ppermute | solution.py:319
  11.6 3.7 %collective-permute-done.2 = bf16[2,16,1024]{2,1,0:T(8,128)(2,1)S(1)} collective-permute-done((bf16[2,16,1024]{2,1,0:T(8,128)(2,1)S(1)}, bf16[2,16,1024]{2,1,0:T(8,128)(2,1)S(1)}, u32[]{:S(2)}, u32[]{:S(2)}) %collective-permute-start.2) | collective-permute-done | bytes 65568 | tf_op jit(solution)/shard_map/ppermute | solution.py:319
  15.3 2.1 %collective-permute-done.3 = bf16[2,16,1024]{2,1,0:T(8,128)(2,1)S(1)} collective-permute-done((bf16[2,16,1024]{2,1,0:T(8,128)(2,1)S(1)}, bf16[2,16,1024]{2,1,0:T(8,128)(2,1)S(1)}, u32[]{:S(2)}, u32[]{:S(2)}) %collective-permute-start.3) | collective-permute-done | bytes 65568 | tf_op jit(solution)/shard_map/ppermute | solution.py:319
  20.2 5.9 %pull.1.wq_ref = bf16[8192,1024]{1,0:T(8,128)(2,1)S(1)} custom-call(bf16[2,16,1024]{2,1,0:T(8,128)(2,1)} %copy-done.12, bf16[8192,1024]{1,0:T(8,128)(2,1)} %src_ref.1), custom_call_target="tpu_custom_call" | custom-call | bytes 33554432 | tf_op jit(solution)/shard_map/pull/pallas_call | solution.py:387
  26.1 5.7 %copy-done = bf16[8192,1024]{1,0:T(8,128)(2,1)} copy-done((bf16[8192,1024]{1,0:T(8,128)(2,1)}, bf16[8192,1024]{1,0:T(8,128)(2,1)S(1)}, u32[]{:S(2)}) %copy-start) | copy-done | bytes 16777240
  31.9 2.2 %copy-done.2 = bf16[8192,256]{1,0:T(8,128)(2,1)S(1)} copy-done((bf16[8192,256]{1,0:T(8,128)(2,1)S(1)}, bf16[8192,256]{1,0:T(8,128)(2,1)}, u32[]{:S(2)}) %copy-start.2) | copy-done | bytes 4194328
  34.1 10.7 %project.1.q_ref = bf16[160,128]{1,0:T(8,128)(2,1)S(1)} custom-call(bf16[8,16,1024]{2,1,0:T(8,128)(2,1)S(1)} %bitcast.26, bf16[8,16,1024]{2,1,0:T(8,128)(2,1)S(1)} %collective-permute-done.4.far_ref, bf16[16,32]{1,0:T(8,128)(2,1)S(1)} %get-tuple-element.27.take_ref, f32[8,1,1024]{2,1,0:T(1,128)S(1)} %bitcast.28, bf16[8192,1024]{1,0:T(8,128)(2,1)} %copy-done, ...), custom_call_target="tpu_custom_call" | custom-call | flops 335544320 | bytes 20971520 | tf_op jit(solution)/shard_map/project/pallas_call | solution.py:403
  46.3 2.5 %collective-permute-done.5 = bf16[160,128]{1,0:T(8,128)(2,1)S(1)} collective-permute-done((bf16[160,128]{1,0:T(8,128)(2,1)S(1)}, bf16[160,128]{1,0:T(8,128)(2,1)S(1)}, u32[]{:S(2)}, u32[]{:S(2)}) %collective-permute-start.5) | collective-permute-done | bytes 40992 | tf_op jit(solution)/shard_map/ppermute | solution.py:319
  50.4 2.9 %collective-permute-start.8 = (bf16[2,160,128]{2,1,0:T(8,128)(2,1)S(1)}, bf16[2,160,128]{2,1,0:T(8,128)(2,1)S(1)}, u32[]{:S(2)}, u32[]{:S(2)}) collective-permute-start(bf16[2,160,128]{2,1,0:T(8,128)(2,1)S(1)} %get-tuple-element.53.after_ref), channel_id=1, source_target_pairs={{0,6},{1,7},{2,4},{3,5},{4,2},{5,3},{6,0},{7,1},{8,14},{9,15},{10,... | collective-permute-start | bytes 245768 | tf_op jit(solution)/shard_map/ppermute | solution.py:319
  53.3 3.7 %side.1 = (bf16[4,256,1024]{2,1,0:T(8,128)(2,1)S(1)}, bf16[4,256,1024]{2,1,0:T(8,128)(2,1)S(1)}, f32[8,256]{1,0:T(8,128)S(1)}, f32[8,256]{1,0:T(8,128)S(1)}) custom-call(bf16[2,160,128]{2,1,0:T(8,128)(2,1)S(1)} %get-tuple-element.53.after_ref, s32[8]{0:T(128)S(1)} %get-tuple-element.28.meta_ref, bf16[8,256,1024]{2,1,0:T(8,128)(2,1)S(1)} %copy-done.3, ...), custom_call_target="tpu_custom_call" | custom-call | flops 8388608 | bytes 12582912 | tf_op jit(solution)/shard_map/side/pallas_call | solution.py:425
  60.1 2.9 %attend.1 = (f32[144,128]{1,0:T(8,128)S(1)}, f32[144,128]{1,0:T(8,128)S(1)}, f32[144,128]{1,0:T(8,128)S(1)}, f32[144,128]{1,0:T(8,128)S(1)}, f32[144,128]{1,0:T(...) custom-call(s32[8]{0:T(128)S(1)} %get-tuple-element.28.meta_ref, ...), custom_call_target="tpu_custom_call" | custom-call | flops 1073741824 | bytes 4194304 | tf_op jit(solution)/shard_map/attend/pallas_call | solution.py:472
  64.0 2.0 %collective-permute-start.11 = (f32[144,128]{1,0:T(8,128)S(1)}, f32[144,128]{1,0:T(8,128)S(1)}, u32[]{:S(2)}, u32[]{:S(2)}) collective-permute-start(f32[144,128]{1,0:T(8,128)S(1)} %get-tuple-element.36), channel_id=1, source_target_pairs={{0,3},{1,2},{2,1},{3,0},{4,7},{5,6},{6,5},{7,4},{8,11},{9,10},{10,... | collective-permute-start | bytes 221192 | tf_op jit(solution)/shard_map/ppermute | solution.py:319
  70.2 3.4 %collective-permute-start.15 = (f32[144,128]{1,0:T(8,128)S(1)}, f32[144,128]{1,0:T(8,128)S(1)}, u32[]{:S(2)}, u32[]{:S(2)}) collective-permute-start(f32[144,128]{1,0:T(8,128)S(1)} %get-tuple-element.40), channel_id=1, source_target_pairs={{0,7},{1,6},{2,5},{3,4},{4,3},{5,2},{6,1},{7,0},{8,15},{9,14},{10,... | collective-permute-start | bytes 221192 | tf_op jit(solution)/shard_map/ppermute | solution.py:319
  76.0 2.6 %collective-permute-done.13.rest_5_ = f32[144,128]{1,0:T(8,128)S(1)} collective-permute-done((f32[144,128]{1,0:T(8,128)S(1)}, f32[144,128]{1,0:T(8,128)S(1)}, u32[]{:S(2)}, u32[]{:S(2)}) %collective-permute-start.13) | collective-permute-done | bytes 73760 | tf_op jit(solution)/shard_map/ppermute | solution.py:319
  78.7 5.8 %copy-done.1 = bf16[1024,8192]{1,0:T(8,128)(2,1)S(1)} copy-done((bf16[1024,8192]{1,0:T(8,128)(2,1)S(1)}, bf16[1024,8192]{1,0:T(8,128)(2,1)}, u32[]{:S(2)}) %copy-start.1) | copy-done | bytes 16777240
  84.5 3.0 %merge.1 = (f32[136,128]{1,0:T(8,128)S(1)}, f32[136,128]{1,0:T(8,128)S(1)}, f32[136,128]{1,0:T(8,128)S(1)}, f32[136,128]{1,0:T(8,128)S(1)}, f32[136,128]{1,0:T(8...) custom-call(bf16[160,128]{1,0:T(8,128)(2,1)S(1)} %project.1.q_ref, ...), custom_call_target="tpu_custom_call" | custom-call | flops 268435456 | bytes 16777216 | tf_op jit(solution)/shard_map/merge/pallas_call | solution.py:505
  88.8 2.1 %collective-permute-start.17 = (f32[136,128]{1,0:T(8,128)S(1)}, f32[136,128]{1,0:T(8,128)S(1)}, u32[]{:S(2)}, u32[]{:S(2)}) collective-permute-start(f32[136,128]{1,0:T(8,128)S(1)} %get-tuple-element.43), channel_id=1, source_target_pairs={{0,2},{1,3},{2,0},{3,1},{4,6},{5,7},{6,4},{7,5},{8,10},{9,11},{10,... | collective-permute-start | bytes 208904 | tf_op jit(solution)/shard_map/ppermute | solution.py:319
  91.4 2.3 %collective-permute-start.19 = (f32[136,128]{1,0:T(8,128)S(1)}, f32[136,128]{1,0:T(8,128)S(1)}, u32[]{:S(2)}, u32[]{:S(2)}) collective-permute-start(f32[136,128]{1,0:T(8,128)S(1)} %get-tuple-element.45), channel_id=1, source_target_pairs={{0,4},{1,5},{2,6},{3,7},{4,0},{5,1},{6,2},{7,3},{8,12},{9,13},{10,... | collective-permute-start | bytes 208904 | tf_op jit(solution)/shard_map/ppermute | solution.py:319
  96.7 2.4 %collective-permute-start.22 = (f32[136,128]{1,0:T(8,128)S(1)}, f32[136,128]{1,0:T(8,128)S(1)}, u32[]{:S(2)}, u32[]{:S(2)}) collective-permute-start(f32[136,128]{1,0:T(8,128)S(1)} %get-tuple-element.48), channel_id=1, source_target_pairs={{0,7},{1,6},{2,5},{3,4},{4,3},{5,2},{6,1},{7,0},{8,15},{9,14},{10,... | collective-permute-start | bytes 208904 | tf_op jit(solution)/shard_map/ppermute | solution.py:319
  99.1 2.6 %collective-permute-done.19.refs_4_ = f32[136,128]{1,0:T(8,128)S(1)} collective-permute-done((f32[136,128]{1,0:T(8,128)S(1)}, f32[136,128]{1,0:T(8,128)S(1)}, u32[]{:S(2)}, u32[]{:S(2)}) %collective-permute-start.19) | collective-permute-done | bytes 69664 | tf_op jit(solution)/shard_map/ppermute | solution.py:319
  101.7 2.3 %collective-permute-done.20.refs_5_ = f32[136,128]{1,0:T(8,128)S(1)} collective-permute-done((f32[136,128]{1,0:T(8,128)S(1)}, f32[136,128]{1,0:T(8,128)S(1)}, u32[]{:S(2)}, u32[]{:S(2)}) %collective-permute-start.20) | collective-permute-done | bytes 69664 | tf_op jit(solution)/shard_map/ppermute | solution.py:319
  (67 shorter events, 24.5 us)
Async XLA Ops:
  0.6 5.2 %collective-permute-start = (bf16[16,1024]{1,0:T(8,128)(2,1)}, bf16[16,1024]{1,0:T(8,128)(2,1)S(1)}, u32[]{:S(2)}, u32[]{:S(2)}) collective-permute-start(bf16[16,1024]{1,0:T(8,128)(2,1)} %bitcast.38), channel_id=1, source_target_pairs={{0,1},{1,0},{2,3},{3,2},{4,5},{5,4},{6,7},{7,6},{8,9},{9,8},{10,11... | collective-permute-start | bytes 98312 | tf_op jit(solution)/shard_map/ppermute | solution.py:319
  6.6 5.0 %collective-permute-start.1 = (bf16[2,16,1024]{2,1,0:T(8,128)(2,1)S(1)}, bf16[2,16,1024]{2,1,0:T(8,128)(2,1)S(1)}, u32[]{:S(2)}, u32[]{:S(2)}) collective-permute-start(bf16[2,16,1024]{2,1,0:T(8,128)(2,1)S(1)} %get-tuple-element.55.after_ref), channel_id=1, source_target_pairs={{0,2},{1,3},{2,0},{3,1},{4,6},{5,7},{6,4},{7,5},{8,10},{9,11},{10,... | collective-permute-start | bytes 196616 | tf_op jit(solution)/shard_map/ppermute | solution.py:319
  8.7 6.6 %collective-permute-start.2 = (bf16[2,16,1024]{2,1,0:T(8,128)(2,1)S(1)}, bf16[2,16,1024]{2,1,0:T(8,128)(2,1)S(1)}, u32[]{:S(2)}, u32[]{:S(2)}) collective-permute-start(bf16[2,16,1024]{2,1,0:T(8,128)(2,1)S(1)} %get-tuple-element.55.after_ref), channel_id=1, source_target_pairs={{0,4},{1,5},{2,6},{3,7},{4,0},{5,1},{6,2},{7,3},{8,12},{9,13},{10,... | collective-permute-start | bytes 196616 | tf_op jit(solution)/shard_map/ppermute | solution.py:319
  11.3 6.1 %collective-permute-start.3 = (bf16[2,16,1024]{2,1,0:T(8,128)(2,1)S(1)}, bf16[2,16,1024]{2,1,0:T(8,128)(2,1)S(1)}, u32[]{:S(2)}, u32[]{:S(2)}) collective-permute-start(bf16[2,16,1024]{2,1,0:T(8,128)(2,1)S(1)} %get-tuple-element.55.after_ref), channel_id=1, source_target_pairs={{0,6},{1,7},{2,4},{3,5},{4,2},{5,3},{6,0},{7,1},{8,14},{9,15},{10,... | collective-permute-start | bytes 196616 | tf_op jit(solution)/shard_map/ppermute | solution.py:319
  17.4 14.4 %collective-permute-start.4 = (bf16[8,16,1024]{2,1,0:T(8,128)(2,1)S(1)}, bf16[8,16,1024]{2,1,0:T(8,128)(2,1)S(1)}, u32[]{:S(2)}, u32[]{:S(2)}) collective-permute-start(bf16[8,16,1024]{2,1,0:T(8,128)(2,1)S(1)} %bitcast.25), channel_id=1, source_target_pairs={{0,8},{8,0},{1,9},{9,1},{2,10},{10,2},{3,11},{11,3},{4,12},{12,4},... | collective-permute-start | bytes 786440 | tf_op jit(solution)/shard_map/ppermute | solution.py:399
  44.7 4.1 %collective-permute-start.5 = (bf16[160,128]{1,0:T(8,128)(2,1)S(1)}, bf16[160,128]{1,0:T(8,128)(2,1)S(1)}, u32[]{:S(2)}, u32[]{:S(2)}) collective-permute-start(bf16[160,128]{1,0:T(8,128)(2,1)S(1)} %project.1.q_ref), channel_id=1, source_target_pairs={{0,1},{1,0},{2,3},{3,2},{4,5},{5,4},{6,7},{7,6},{8,9},{9,8},{10,11... | collective-permute-start | bytes 122888 | tf_op jit(solution)/shard_map/ppermute | solution.py:319
  48.8 9.6 %collective-permute-start.6 = (bf16[2,160,128]{2,1,0:T(8,128)(2,1)S(1)}, bf16[2,160,128]{2,1,0:T(8,128)(2,1)S(1)}, u32[]{:S(2)}, u32[]{:S(2)}) collective-permute-start(bf16[2,160,128]{2,1,0:T(8,128)(2,1)S(1)} %get-tuple-element.53.after_ref), channel_id=1, source_target_pairs={{0,2},{1,3},{2,0},{3,1},{4,6},{5,7},{6,4},{7,5},{8,10},{9,11},{10,... | collective-permute-start | bytes 245768 | tf_op jit(solution)/shard_map/ppermute | solution.py:319
  48.9 9.5 %collective-permute-start.7 = (bf16[2,160,128]{2,1,0:T(8,128)(2,1)S(1)}, bf16[2,160,128]{2,1,0:T(8,128)(2,1)S(1)}, u32[]{:S(2)}, u32[]{:S(2)}) collective-permute-start(bf16[2,160,128]{2,1,0:T(8,128)(2,1)S(1)} %get-tuple-element.53.after_ref), channel_id=1, source_target_pairs={{0,4},{1,5},{2,6},{3,7},{4,0},{5,1},{6,2},{7,3},{8,12},{9,13},{10,... | collective-permute-start | bytes 245768 | tf_op jit(solution)/shard_map/ppermute | solution.py:319
  50.4 8.0 %collective-permute-start.8 = (bf16[2,160,128]{2,1,0:T(8,128)(2,1)S(1)}, bf16[2,160,128]{2,1,0:T(8,128)(2,1)S(1)}, u32[]{:S(2)}, u32[]{:S(2)}) collective-permute-start(bf16[2,160,128]{2,1,0:T(8,128)(2,1)S(1)} %get-tuple-element.53.after_ref), channel_id=1, source_target_pairs={{0,6},{1,7},{2,4},{3,5},{4,2},{5,3},{6,0},{7,1},{8,14},{9,15},{10,... | collective-permute-start | bytes 245768 | tf_op jit(solution)/shard_map/ppermute | solution.py:319
  63.0 7.3 %collective-permute-start.10 = (f32[144,128]{1,0:T(8,128)S(1)}, f32[144,128]{1,0:T(8,128)S(1)}, u32[]{:S(2)}, u32[]{:S(2)}) collective-permute-start(f32[144,128]{1,0:T(8,128)S(1)} %get-tuple-element.35), channel_id=1, source_target_pairs={{0,2},{1,3},{2,0},{3,1},{4,6},{5,7},{6,4},{7,5},{8,10},{9,11},{10,... | collective-permute-start | bytes 221192 | tf_op jit(solution)/shard_map/ppermute | solution.py:319
  64.0 9.7 %collective-permute-start.11 = (f32[144,128]{1,0:T(8,128)S(1)}, f32[144,128]{1,0:T(8,128)S(1)}, u32[]{:S(2)}, u32[]{:S(2)}) collective-permute-start(f32[144,128]{1,0:T(8,128)S(1)} %get-tuple-element.36), channel_id=1, source_target_pairs={{0,3},{1,2},{2,1},{3,0},{4,7},{5,6},{6,5},{7,4},{8,11},{9,10},{10,... | collective-permute-start | bytes 221192 | tf_op jit(solution)/shard_map/ppermute | solution.py:319
  66.0 10.0 %collective-permute-start.12 = (f32[144,128]{1,0:T(8,128)S(1)}, f32[144,128]{1,0:T(8,128)S(1)}, u32[]{:S(2)}, u32[]{:S(2)}) collective-permute-start(f32[144,128]{1,0:T(8,128)S(1)} %get-tuple-element.37), channel_id=1, source_target_pairs={{0,4},{1,5},{2,6},{3,7},{4,0},{5,1},{6,2},{7,3},{8,12},{9,13},{10,... | collective-permute-start | bytes 221192 | tf_op jit(solution)/shard_map/ppermute | solution.py:319
  67.3 11.3 %collective-permute-start.13 = (f32[144,128]{1,0:T(8,128)S(1)}, f32[144,128]{1,0:T(8,128)S(1)}, u32[]{:S(2)}, u32[]{:S(2)}) collective-permute-start(f32[144,128]{1,0:T(8,128)S(1)} %get-tuple-element.38), channel_id=1, source_target_pairs={{0,5},{1,4},{2,7},{3,6},{4,1},{5,0},{6,3},{7,2},{8,13},{9,12},{10,... | collective-permute-start | bytes 221192 | tf_op jit(solution)/shard_map/ppermute | solution.py:319
  68.9 9.7 %collective-permute-start.14 = (f32[144,128]{1,0:T(8,128)S(1)}, f32[144,128]{1,0:T(8,128)S(1)}, u32[]{:S(2)}, u32[]{:S(2)}) collective-permute-start(f32[144,128]{1,0:T(8,128)S(1)} %get-tuple-element.39), channel_id=1, source_target_pairs={{0,6},{1,7},{2,4},{3,5},{4,2},{5,3},{6,0},{7,1},{8,14},{9,15},{10,... | collective-permute-start | bytes 221192 | tf_op jit(solution)/shard_map/ppermute | solution.py:319
  70.2 8.4 %collective-permute-start.15 = (f32[144,128]{1,0:T(8,128)S(1)}, f32[144,128]{1,0:T(8,128)S(1)}, u32[]{:S(2)}, u32[]{:S(2)}) collective-permute-start(f32[144,128]{1,0:T(8,128)S(1)} %get-tuple-element.40), channel_id=1, source_target_pairs={{0,7},{1,6},{2,5},{3,4},{4,3},{5,2},{6,1},{7,0},{8,15},{9,14},{10,... | collective-permute-start | bytes 221192 | tf_op jit(solution)/shard_map/ppermute | solution.py:319
  73.7 5.1 %collective-permute-start.9 = (f32[144,128]{1,0:T(8,128)S(1)}, f32[144,128]{1,0:T(8,128)S(1)}, u32[]{:S(2)}, u32[]{:S(2)}) collective-permute-start(f32[144,128]{1,0:T(8,128)S(1)} %get-tuple-element.34), channel_id=1, source_target_pairs={{0,1},{1,0},{2,3},{3,2},{4,5},{5,4},{6,7},{7,6},{8,9},{9,8},{10,11... | collective-permute-start | bytes 221192 | tf_op jit(solution)/shard_map/ppermute | solution.py:319
  87.5 7.2 %collective-permute-start.16 = (f32[136,128]{1,0:T(8,128)S(1)}, f32[136,128]{1,0:T(8,128)S(1)}, u32[]{:S(2)}, u32[]{:S(2)}) collective-permute-start(f32[136,128]{1,0:T(8,128)S(1)} %get-tuple-element.42), channel_id=1, source_target_pairs={{0,1},{1,0},{2,3},{3,2},{4,5},{5,4},{6,7},{7,6},{8,9},{9,8},{10,11... | collective-permute-start | bytes 208904 | tf_op jit(solution)/shard_map/ppermute | solution.py:319
  88.8 7.9 %collective-permute-start.17 = (f32[136,128]{1,0:T(8,128)S(1)}, f32[136,128]{1,0:T(8,128)S(1)}, u32[]{:S(2)}, u32[]{:S(2)}) collective-permute-start(f32[136,128]{1,0:T(8,128)S(1)} %get-tuple-element.43), channel_id=1, source_target_pairs={{0,2},{1,3},{2,0},{3,1},{4,6},{5,7},{6,4},{7,5},{8,10},{9,11},{10,... | collective-permute-start | bytes 208904 | tf_op jit(solution)/shard_map/ppermute | solution.py:319
  90.9 8.2 %collective-permute-start.18 = (f32[136,128]{1,0:T(8,128)S(1)}, f32[136,128]{1,0:T(8,128)S(1)}, u32[]{:S(2)}, u32[]{:S(2)}) collective-permute-start(f32[136,128]{1,0:T(8,128)S(1)} %get-tuple-element.44), channel_id=1, source_target_pairs={{0,3},{1,2},{2,1},{3,0},{4,7},{5,6},{6,5},{7,4},{8,11},{9,10},{10,... | collective-permute-start | bytes 208904 | tf_op jit(solution)/shard_map/ppermute | solution.py:319
  91.4 10.2 %collective-permute-start.19 = (f32[136,128]{1,0:T(8,128)S(1)}, f32[136,128]{1,0:T(8,128)S(1)}, u32[]{:S(2)}, u32[]{:S(2)}) collective-permute-start(f32[136,128]{1,0:T(8,128)S(1)} %get-tuple-element.45), channel_id=1, source_target_pairs={{0,4},{1,5},{2,6},{3,7},{4,0},{5,1},{6,2},{7,3},{8,12},{9,13},{10,... | collective-permute-start | bytes 208904 | tf_op jit(solution)/shard_map/ppermute | solution.py:319
  93.8 10.2 %collective-permute-start.20 = (f32[136,128]{1,0:T(8,128)S(1)}, f32[136,128]{1,0:T(8,128)S(1)}, u32[]{:S(2)}, u32[]{:S(2)}) collective-permute-start(f32[136,128]{1,0:T(8,128)S(1)} %get-tuple-element.46), channel_id=1, source_target_pairs={{0,5},{1,4},{2,7},{3,6},{4,1},{5,0},{6,3},{7,2},{8,13},{9,12},{10,... | collective-permute-start | bytes 208904 | tf_op jit(solution)/shard_map/ppermute | solution.py:319
  94.7 9.3 %collective-permute-start.21 = (f32[136,128]{1,0:T(8,128)S(1)}, f32[136,128]{1,0:T(8,128)S(1)}, u32[]{:S(2)}, u32[]{:S(2)}) collective-permute-start(f32[136,128]{1,0:T(8,128)S(1)} %get-tuple-element.47), channel_id=1, source_target_pairs={{0,6},{1,7},{2,4},{3,5},{4,2},{5,3},{6,0},{7,1},{8,14},{9,15},{10,... | collective-permute-start | bytes 208904 | tf_op jit(solution)/shard_map/ppermute | solution.py:319
  96.7 7.4 %collective-permute-start.22 = (f32[136,128]{1,0:T(8,128)S(1)}, f32[136,128]{1,0:T(8,128)S(1)}, u32[]{:S(2)}, u32[]{:S(2)}) collective-permute-start(f32[136,128]{1,0:T(8,128)S(1)} %get-tuple-element.48), channel_id=1, source_target_pairs={{0,7},{1,6},{2,5},{3,4},{4,3},{5,2},{6,1},{7,0},{8,15},{9,14},{10,... | collective-permute-start | bytes 208904 | tf_op jit(solution)/shard_map/ppermute | solution.py:319
  104.1 1.3 %collective-permute-start.23 = (bf16[16,1024]{1,0:T(8,128)(2,1)S(1)}, bf16[16,1024]{1,0:T(8,128)(2,1)S(1)}, u32[]{:S(2)}, u32[]{:S(2)}) collective-permute-start(bf16[16,1024]{1,0:T(8,128)(2,1)S(1)} %get-tuple-element.51), channel_id=1, source_target_pairs={{0,8},{8,0},{1,9},{9,1},{2,10},{10,2},{3,11},{11,3},{4,12},{12,4},... | collective-permute-start | bytes 98312 | tf_op jit(solution)/shard_map/ppermute | solution.py:532
  (13 other events, 120.1 us)

commit v4 on v3

--- a/solution.py
+++ b/solution.py
@@ -44,7 +44,8 @@
     return pl.ds(pl.multiple_of(index * size, size), size)
 
 
-def plan_kernel(slots, steps, map_ref, length_ref, meta_ref, take_ref, give_ref, before_ref, place_ref):
+def plan_kernel(slots, steps, map_ref, length_ref, *rest):
+    meta_ref, take_ref, give_ref, before_ref, place_ref = rest[-5:]
     count = map_ref.shape[0]
     mine = lax.axis_index("dp")
     base = mine * slots
@@ -89,54 +90,33 @@
     give_ref[...] = give.astype(jnp.float32).astype(jnp.bfloat16)
 
 
-def pull_kernel(after_ref, src_ref, out_ref, sems):
-    parts = sems.shape[0]
-    size = src_ref.shape[0] // parts
-    copies = [
-        pltpu.make_async_copy(
-            src_ref.at[pl.ds(p * size, size)], out_ref.at[pl.ds(p * size, size)], sems.at[p]
-        )
-        for p in range(parts)
-    ]
-    for copy in copies:
-        copy.start()
-    for copy in copies:
-        copy.wait()
-
-
-def side_kernel(pages, after_ref, meta_ref, k_ref, v_ref, hidden_ref, gain_ref, head_ref, keys_ref, values_ref, squares_ref, dots_ref, buffer, sems, page_sems):
+def reward_kernel(after_ref, hidden_ref, gain_ref, head_ref, *rest):
+    out_ref, buffer, sems = rest[-3:]
     slots = hidden_ref.shape[0]
     loads = [
         pltpu.make_async_copy(hidden_ref.at[s], buffer.at[s], sems.at[s]) for s in range(slots)
     ]
     for load in loads:
         load.start()
-    copies = []
-    for i in range(pages):
-        page = meta_ref[i]
-        copies.append(pltpu.make_async_copy(k_ref.at[page], keys_ref.at[i], page_sems.at[0, i]))
-        copies.append(pltpu.make_async_copy(v_ref.at[page], values_ref.at[i], page_sems.at[1, i]))
-    for copy in copies:
-        copy.start()
     weight = gain_ref[...] * head_ref[...]
     for s in range(slots):
         loads[s].wait()
         hidden = buffer[s].astype(jnp.float32)
-        squares_ref[s] = jnp.sum(hidden * hidden, axis=-1)
-        dots_ref[s] = jnp.sum(hidden * weight, axis=-1)
-    for copy in copies:
-        copy.wait()
-
-
-def project_kernel(pages, per_page, width, own_ref, far_ref, take_ref, gain_ref, wq_ref, wkv_ref, out_ref, tokens, wkv, sems):
+        for half, value in enumerate((hidden * hidden, hidden * weight)):
+            sums = jnp.sum(value, axis=-1)
+            if len(out_ref.shape) == 2:
+                out_ref[half * slots + s] = sums
+                continue
+            for c in range(EXT // 2):
+                piece = jnp.zeros((LANES,), jnp.float32)
+                if c < sums.shape[0] // LANES:
+                    piece = sums[c * LANES : (c + 1) * LANES]
+                out_ref[s, half * (EXT // 2) + c] = piece
+
+
+def project_kernel(pages, per_page, width, own_ref, far_ref, take_ref, gain_ref, wq_ref, wkv_ref, out_ref, tokens):
     me = lax.axis_index("tensor")
     chunks, rows, depth = own_ref.shape
-    copies = []
-    for r in range(chunks):
-        copy = pltpu.make_async_copy(wkv_ref.at[aligned(me ^ r, depth)], wkv.at[r], sems.at[r])
-        copy.start()
-        copies.append(copy)
-
     total = jnp.zeros((rows, depth), jnp.float32)
     for r in range(chunks):
         both = jnp.concatenate([own_ref[r], far_ref[r]], axis=0)
@@ -146,12 +126,11 @@
     inv = lax.rsqrt(jnp.sum(total, axis=-1, keepdims=True) / width + EPS)
 
     query = jnp.zeros((rows, wq_ref.shape[1]), jnp.float32)
-    keyval = jnp.zeros((rows, wkv.shape[2]), jnp.float32)
+    keyval = jnp.zeros((rows, wkv_ref.shape[1]), jnp.float32)
     for r in range(chunks):
         normed = (tokens[r].astype(jnp.float32) * inv * gain_ref[me ^ r]).astype(jnp.bfloat16)
         query = query + dot(normed, wq_ref[aligned(me ^ r, depth), :])
-        copies[r].wait()
-        keyval = keyval + dot(normed, wkv[r])
+        keyval = keyval + dot(normed, wkv_ref[aligned(me ^ r, depth), :])
 
     heads = query.shape[1] // HD
     query = query.astype(jnp.bfloat16)
@@ -168,7 +147,7 @@
         out_ref[body + v * rows : body + (v + 1) * rows] = keyval[:, v * LANES : (v + 1) * LANES]
 
 
-def attend_kernel(pages, page_rows, split, meta_ref, q_ref, k_ref, v_ref, squares_ref, dots_ref, *rest):
+def attend_kernel(pages, page_rows, split, meta_ref, q_ref, k_ref, v_ref, reward_ref, *rest):
     outs, (spread, product) = rest[:-2], rest[-2:]
     width = k_ref.shape[1]
     span = KVH * page_rows
@@ -181,13 +160,13 @@
             spread[r * page_rows : (r + 1) * page_rows, aligned(me ^ r, HD)] = q_ref[
                 r, i * page_rows : (i + 1) * page_rows, :
             ]
-        scores = dot(k_ref[i], spread[...], NT) * SCALE
+        scores = dot(k_ref[meta_ref[i]], spread[...], NT) * SCALE
         valid = first + iota((width, span), 0) < meta_ref[pages + i]
         scores = jnp.where(valid, scores, NEG)
         top = jnp.max(scores, axis=0, keepdims=True)
         expo = jnp.where(valid, jnp.exp(scores - top), 0.0)
         total = jnp.sum(expo, axis=0, keepdims=True)
-        product[...] = dot(expo.astype(jnp.bfloat16), v_ref[i], TN)
+        product[...] = dot(expo.astype(jnp.bfloat16), v_ref[meta_ref[i]], TN)
         for r in range(KVH):
             out = outs[r] if len(outs) > 1 else outs[0].at[r]
             out[i * page_rows : (i + 1) * page_rows, :] = product[
@@ -198,9 +177,7 @@
             out[body + pages + i : body + pages + i + 1, :] = total[:, lane : lane + LANES]
     for r in range(KVH):
         if len(outs) > 1:
-            outs[r][body + EXT :, :] = jnp.concatenate(
-                [squares_ref[me ^ r], dots_ref[me ^ r]], axis=0
-            )
+            outs[r][body + EXT :, :] = reward_ref[me ^ r]
         else:
             outs[0][r, body + EXT :, :] = jnp.zeros((EXT, LANES), jnp.float32)
 
@@ -319,11 +296,13 @@
     return lax.ppermute(x, "tensor", [(i, i ^ bits) for i in range(chunks)])
 
 
-def spread_all(x, chunks, index):
+def spread_all(x, chunks, index, tie=None):
     if chunks != KVH:
         every = lax.all_to_all(jnp.broadcast_to(x[None], (chunks,) + x.shape), "tensor", 0, 0, tiled=True)
         return jnp.take(every, index ^ jnp.arange(chunks), axis=0), x
     pair = jnp.stack([x, partner(x, chunks, 1)])
+    if tie is not None:
+        pair, tie = lax.optimization_barrier((pair, tie))
     others = [partner(pair, chunks, bits) for bits in (2, 4, 6)]
     return jnp.stack([pair] + others).reshape((chunks,) + x.shape), pair
 
@@ -368,7 +347,7 @@
 
     meta, take, give = pl.pallas_call(
         functools.partial(plan_kernel, slots, STEPS),
-        in_specs=[SMEM, SMEM],
+        in_specs=[SMEM, SMEM] + [ANY] * 3,
         out_specs=[SMEM, VMEM, VMEM],
         out_shape=(
             jax.ShapeDtypeStruct((2 * pages,), jnp.int32),
@@ -379,38 +358,25 @@
             pltpu.SMEM(slot_map.shape, jnp.int32),
             pltpu.SMEM(slot_map.shape, jnp.int32),
         ],
-        compiler_params=pltpu.CompilerParams(vmem_limit_bytes=MIB),
+        compiler_params=pltpu.CompilerParams(vmem_limit_bytes=42 * MIB),
+        cost_estimate=pl.CostEstimate(flops=0, bytes_accessed=1000, transcendentals=0),
         name="plan",
-    )(slot_map, lengths)
-
-    own, after = spread_all(decode_inputs.reshape(rows, part), chunks, index)
-    w_query = pl.pallas_call(
-        pull_kernel,
-        in_specs=[ANY, ANY],
-        out_specs=VMEM,
-        out_shape=pltpu.VMEM(w_query.shape, w_query.dtype),
-        scratch_shapes=[pltpu.SemaphoreType.DMA((KVH,))],
-        compiler_params=pltpu.CompilerParams(vmem_limit_bytes=46 * MIB),
-        cost_estimate=pl.CostEstimate(
-            flops=0, bytes_accessed=4 * depth * qcols, transcendentals=0
-        ),
-        name="pull",
-    )(after, w_query)
+    )(slot_map, lengths, w_out, w_out, w_out)
+
+    own, _ = spread_all(decode_inputs.reshape(rows, part), chunks, index, take)
     far = lax.ppermute(own, "dp", swap)
 
     pieces = max(kvcols // LANES, 1)
     packed_rows = body + pieces * rows
     packed = pl.pallas_call(
         functools.partial(project_kernel, pages, per_page, depth),
-        in_specs=[VMEM, VMEM, VMEM, VMEM, VMEM, ANY],
+        in_specs=[VMEM] * 6,
         out_specs=VMEM,
         out_shape=jax.ShapeDtypeStruct((packed_rows, LANES), jnp.bfloat16),
         scratch_shapes=[
             pltpu.VMEM((chunks, rows, part), jnp.bfloat16),
-            pltpu.VMEM((chunks, part, kvcols), jnp.bfloat16),
-            pltpu.SemaphoreType.DMA((chunks,)),
         ],
-        compiler_params=pltpu.CompilerParams(vmem_limit_bytes=46 * MIB),
+        compiler_params=pltpu.CompilerParams(vmem_limit_bytes=4 * MIB),
         cost_estimate=pl.CostEstimate(
             flops=2 * rows * depth * (qcols + kvcols),
             bytes_accessed=2 * depth * (qcols + kvcols),
@@ -421,30 +387,26 @@
     gathered, after = spread_all(packed, chunks, index)
 
     span = reward_hidden.shape[1]
-    page_shape = (pages,) + cache_keys.shape[1:]
-    keys, values, squares, dots = pl.pallas_call(
-        functools.partial(side_kernel, pages),
-        in_specs=[ANY, SMEM, ANY, ANY, ANY, VMEM, VMEM],
-        out_specs=[VMEM] * 4,
-        out_shape=(
-            pltpu.VMEM(page_shape, cache_keys.dtype),
-            pltpu.VMEM(page_shape, cache_values.dtype),
-            jax.ShapeDtypeStruct((slots, span), jnp.float32),
-            jax.ShapeDtypeStruct((slots, span), jnp.float32),
+    tiled = direct and slots == chunks
+    reward_parts = pl.pallas_call(
+        reward_kernel,
+        in_specs=[ANY, ANY, VMEM, VMEM] + [ANY] * 0,
+        out_specs=VMEM,
+        out_shape=jax.ShapeDtypeStruct(
+            (slots, EXT, LANES) if tiled else (2 * slots, span), jnp.float32
         ),
         scratch_shapes=[
             pltpu.VMEM(reward_hidden.shape, reward_hidden.dtype),
             pltpu.SemaphoreType.DMA((slots,)),
-            pltpu.SemaphoreType.DMA((2, pages)),
         ],
-        compiler_params=pltpu.CompilerParams(vmem_limit_bytes=40 * MIB),
+        compiler_params=pltpu.CompilerParams(vmem_limit_bytes=8 * MIB),
         cost_estimate=pl.CostEstimate(
             flops=4 * reward_hidden.size,
-            bytes_accessed=2 * reward_hidden.size + 8 * pages * width * KVH * HD,
+            bytes_accessed=2 * reward_hidden.size,
             transcendentals=0,
         ),
-        name="side",
-    )(after, meta, cache_keys, cache_values, reward_hidden, reward_gain[None], reward_head[None])
+        name="reward",
+    )(after, reward_hidden, reward_gain[None], reward_head[None])
 
     def tile(values):
         values = values.reshape(chunks, -1)
@@ -453,7 +415,10 @@
             chunks, EXT // 2, LANES
         )
 
-    squares, dots = tile(squares), tile(dots)
+    if not tiled:
+        reward_parts = jnp.concatenate(
+            [tile(reward_parts[:slots]), tile(reward_parts[slots:])], axis=1
+        )
     fresh = gathered
     if not direct:
         fresh = jnp.take(gathered[:, body:, :kvcols], index ^ jnp.arange(chunks), axis=0)
@@ -471,7 +436,7 @@
     block = (big + 2 * EXT, HD)
     attended = pl.pallas_call(
         functools.partial(attend_kernel, pages, page_rows, split),
-        in_specs=[SMEM] + [VMEM] * 5,
+        in_specs=[SMEM] + [VMEM] * 4,
         out_specs=[VMEM] * (KVH if direct else 1),
         out_shape=(
             [jax.ShapeDtypeStruct(block, jnp.float32)] * KVH
@@ -482,14 +447,14 @@
             pltpu.VMEM((KVH * page_rows, KVH * HD), jnp.bfloat16),
             pltpu.VMEM((KVH * page_rows, KVH * HD), jnp.float32),
         ],
-        compiler_params=pltpu.CompilerParams(vmem_limit_bytes=12 * MIB),
+        compiler_params=pltpu.CompilerParams(vmem_limit_bytes=6 * MIB),
         cost_estimate=pl.CostEstimate(
             flops=4 * pages * width * KVH * HD * KVH * page_rows,
             bytes_accessed=4 * pages * width * KVH * HD,
             transcendentals=pages * width * KVH * page_rows,
         ),
         name="attend",
-    )(meta, queries, keys, values, squares, dots)
+    )(meta, queries, cache_keys, cache_values, reward_parts)
     if not direct:
         acc = (
             attended[0][:, :big]
@@ -498,7 +463,7 @@
             .reshape(chunks, body, HD)
         )
         extra = jnp.repeat(attended[0][:, big : big + EXT], split, axis=0)
-        attended = [jnp.concatenate([acc, extra, squares, dots], axis=1)]
+        attended = [jnp.concatenate([acc, extra, reward_parts], axis=1)]
     parts = trade(attended, chunks)
 
     chunk_rows = part // LANES * rows + EXT

time: 106 us -> 79.9 us (0.75)
  Pallas kernels: 27.5 us -> 12.9 us
  local copies, waits for them, and re-layouts: 18.6 us -> 5.29 us
  waiting for transfers between devices: 20.7 us -> 24.7 us
  starting transfers between devices: 36.8 us -> 35.1 us
    unnamed x26 -> x36, local copies, waits for them, and re-layouts: 18 us -> 4.67 us
    pallas_call x1, Pallas kernels: 10.7 us -> 3.28 us  [local(): pl.pallas_call(functools.partial(project_kernel, pages, per_page, depth),...]
    pallas_call x2 -> x1, Pallas kernels: 9.64 us -> 2.31 us  [local(): pl.pallas_call(reward_kernel, in_specs=[ANY, ANY, VMEM, VMEM] + [ANY] * 0...]
    ppermute x22, waiting for transfers between devices: 20.1 us -> 22.6 us  [partner(): return lax.ppermute(x, 'tensor', [(i, i ^ bits) for i in range(chunks)])]
    ppermute x22, starting transfers between devices: 36.6 us -> 35 us  [partner(): return lax.ppermute(x, 'tensor', [(i, i ^ bits) for i in range(chunks)])]
    ppermute x1, waiting for transfers between devices: 0.01 us -> 1.52 us  [local(): far = lax.ppermute(own, 'dp', swap)]
  transfers between devices with their start and end apart: 24 -> 24, of which waited for: 11 -> 10; matrix products, arithmetic and copies ran while one was open for 1% -> 1% of each run, Pallas kernels for 10% -> 5%
where the time goes in v4:
time: 79.9 us; the launch traced here: 79.7 us
  starting transfers between devices  35.1 us (44%)
  waiting for transfers between devices  24.7 us (31%)
  Pallas kernels  12.9 us (16%)
  local copies, waits for them, and re-layouts  5.29 us (7%)
  between operations  0.91 us (1%)
    ppermute x22, starting transfers between devices, partner(): return lax.ppermute(x, 'tensor', [(i, i ^ bits) for i in range(chunks)])  35 us
    ppermute x22, waiting for transfers between devices, partner(): return lax.ppermute(x, 'tensor', [(i, i ^ bits) for i in range(chunks)])  22.6 us
    unnamed x36, local copies, waits for them, and re-layouts  4.67 us
    pallas_call x1, Pallas kernels, local(): pl.pallas_call(functools.partial(project_kernel, pages, per_page, depth),...  3.28 us
    pallas_call x1, Pallas kernels, local(): pl.pallas_call(functools.partial(merge_kernel, pages, per_page, depth, sp...  3 us
    pallas_call x1, Pallas kernels, local(): pl.pallas_call(functools.partial(attend_kernel, pages, page_rows, split),...  2.92 us
    pallas_call x1, Pallas kernels, local(): pl.pallas_call(reward_kernel, in_specs=[ANY, ANY, VMEM, VMEM] + [ANY] * 0...  2.31 us
  transfers between devices with their start and end apart: 24, of which 10 were waited for; matrix products, arithmetic and copies ran while one was open for 1% of the time, Pallas kernels for 5%

profile of v4, /device:TPU:0, one launch (start us, length us, event | category | flops | bytes accessed | tf_op | source)
XLA Modules:
  0.0 79.7 jit_solution(5040397555591080137)
XLA Ops:
  0.7 3.1 %collective-permute-start = (bf16[16,1024]{1,0:T(8,128)(2,1)}, bf16[16,1024]{1,0:T(8,128)(2,1)S(1)}, u32[]{:S(2)}, u32[]{:S(2)}) collective-permute-start(bf16[16,1024]{1,0:T(8,128)(2,1)} %bitcast.42), channel_id=1, source_target_pairs={{0,1},{1,0},{2,3},{3,2},{4,5},{5,4},{6,7},{7,6},{8,9},{9,8},{10,11... | collective-permute-start | bytes 98312 | tf_op jit(solution)/shard_map/ppermute | solution.py:296
  7.5 4.1 %collective-permute-start.3 = (bf16[2,16,1024]{2,1,0:T(8,128)(2,1)S(1)}, bf16[2,16,1024]{2,1,0:T(8,128)(2,1)S(1)}, u32[]{:S(2)}, u32[]{:S(2)}) collective-permute-start(bf16[2,16,1024]{2,1,0:T(8,128)(2,1)S(1)} %pad_maximum_fusion.3), channel_id=1, source_target_pairs={{0,6},{1,7},{2,4},{3,5},{4,2},{5,3},{6,0},{7,1},{8,14},{9,15},{10,... | collective-permute-start | bytes 196616 | tf_op jit(solution)/shard_map/ppermute | solution.py:296
  12.3 2.0 %collective-permute-done.3 = bf16[2,16,1024]{2,1,0:T(8,128)(2,1)S(1)} collective-permute-done((bf16[2,16,1024]{2,1,0:T(8,128)(2,1)S(1)}, bf16[2,16,1024]{2,1,0:T(8,128)(2,1)S(1)}, u32[]{:S(2)}, u32[]{:S(2)}) %collective-permute-start.3) | collective-permute-done | bytes 65568 | tf_op jit(solution)/shard_map/ppermute | solution.py:296
  14.3 2.7 %collective-permute-done.2 = bf16[2,16,1024]{2,1,0:T(8,128)(2,1)S(1)} collective-permute-done((bf16[2,16,1024]{2,1,0:T(8,128)(2,1)S(1)}, bf16[2,16,1024]{2,1,0:T(8,128)(2,1)S(1)}, u32[]{:S(2)}, u32[]{:S(2)}) %collective-permute-start.2) | collective-permute-done | bytes 65568 | tf_op jit(solution)/shard_map/ppermute | solution.py:296
  18.7 2.2 %copy-done.3 = bf16[8192,256]{1,0:T(8,128)(2,1)S(1)} copy-done((bf16[8192,256]{1,0:T(8,128)(2,1)S(1)}, bf16[8192,256]{1,0:T(8,128)(2,1)}, u32[]{:S(2)}) %copy-start.3) | copy-done | bytes 4194328
  20.9 3.3 %project.1.q_ref = bf16[160,128]{1,0:T(8,128)(2,1)S(1)} custom-call(bf16[8,16,1024]{2,1,0:T(8,128)(2,1)S(1)} %bitcast.29, bf16[8,16,1024]{2,1,0:T(8,128)(2,1)S(1)} %collective-permute-done.4.far_ref, bf16[16,32]{1,0:T(8,128)(2,1)S(1)} %get-tuple-element.24.take_ref, f32[8,1,1024]{2,1,0:T(1,128)S(1)} %bitcast.31, bf16[8192,1024]{1,0:T(8,128)(2,1)S(1)} %bitcast.25, ...), custom_call_target="tpu_custom_call" | custom-call | flops 335544320 | bytes 20971520 | tf_op jit(solution)/shard_map/project/pallas_call | solution.py:371
  24.3 3.9 %collective-permute-done.5 = bf16[160,128]{1,0:T(8,128)(2,1)S(1)} collective-permute-done((bf16[160,128]{1,0:T(8,128)(2,1)S(1)}, bf16[160,128]{1,0:T(8,128)(2,1)S(1)}, u32[]{:S(2)}, u32[]{:S(2)}) %collective-permute-start.5) | collective-permute-done | bytes 40992 | tf_op jit(solution)/shard_map/ppermute | solution.py:296
  28.3 2.8 %collective-permute-start.8 = (bf16[2,160,128]{2,1,0:T(8,128)(2,1)S(1)}, bf16[2,160,128]{2,1,0:T(8,128)(2,1)S(1)}, u32[]{:S(2)}, u32[]{:S(2)}) collective-permute-start(bf16[2,160,128]{2,1,0:T(8,128)(2,1)S(1)} %get-tuple-element.47.after_ref), channel_id=1, source_target_pairs={{0,6},{1,7},{2,4},{3,5},{4,2},{5,3},{6,0},{7,1},{8,14},{9,15},{10,... | collective-permute-start | bytes 245768 | tf_op jit(solution)/shard_map/ppermute | solution.py:296
  31.1 1.7 %collective-permute-start.6 = (bf16[2,160,128]{2,1,0:T(8,128)(2,1)S(1)}, bf16[2,160,128]{2,1,0:T(8,128)(2,1)S(1)}, u32[]{:S(2)}, u32[]{:S(2)}) collective-permute-start(bf16[2,160,128]{2,1,0:T(8,128)(2,1)S(1)} %get-tuple-element.47.after_ref), channel_id=1, source_target_pairs={{0,2},{1,3},{2,0},{3,1},{4,6},{5,7},{6,4},{7,5},{8,10},{9,11},{10,... | collective-permute-start | bytes 245768 | tf_op jit(solution)/shard_map/ppermute | solution.py:296
  32.8 2.3 %reward.1.reward_ref = f32[8,8,128]{2,1,0:T(8,128)S(1)} custom-call(bf16[2,160,128]{2,1,0:T(8,128)(2,1)S(1)} %get-tuple-element.47.after_ref, bf16[8,256,1024]{2,1,0:T(8,128)(2,1)S(1)} %copy-done, f32[1,1024]{1,0:T(1,128)S(1)} %bitcast.32, f32[1,1024]{1,0:T(1,128)S(1)} %bitcast.33), custom_call_target="tpu_custom_call" | custom-call | flops 8388608 | bytes 4194304 | tf_op jit(solution)/shard_map/reward/pallas_call | solution.py:391
  35.1 2.8 %collective-permute-done.7 = bf16[2,160,128]{2,1,0:T(8,128)(2,1)S(1)} collective-permute-done((bf16[2,160,128]{2,1,0:T(8,128)(2,1)S(1)}, bf16[2,160,128]{2,1,0:T(8,128)(2,1)S(1)}, u32[]{:S(2)}, u32[]{:S(2)}) %collective-permute-start.7) | collective-permute-done | bytes 81952 | tf_op jit(solution)/shard_map/ppermute | solution.py:296
  38.0 2.9 %attend.1 = (f32[144,128]{1,0:T(8,128)S(1)}, f32[144,128]{1,0:T(8,128)S(1)}, f32[144,128]{1,0:T(8,128)S(1)}, f32[144,128]{1,0:T(8,128)S(1)}, f32[144,128]{1,0:T(...) custom-call(s32[8]{0:T(128)S(1)} %get-tuple-element.26.meta_ref, ...), custom_call_target="tpu_custom_call" | custom-call | flops 1073741824 | bytes 4194304 | tf_op jit(solution)/shard_map/attend/pallas_call | solution.py:437
  41.3 3.1 %collective-permute-start.11 = (f32[144,128]{1,0:T(8,128)S(1)}, f32[144,128]{1,0:T(8,128)S(1)}, u32[]{:S(2)}, u32[]{:S(2)}) collective-permute-start(f32[144,128]{1,0:T(8,128)S(1)} %get-tuple-element.30), channel_id=1, source_target_pairs={{0,3},{1,2},{2,1},{3,0},{4,7},{5,6},{6,5},{7,4},{8,11},{9,10},{10,... | collective-permute-start | bytes 221192 | tf_op jit(solution)/shard_map/ppermute | solution.py:296
  47.1 2.6 %collective-permute-start.14 = (f32[144,128]{1,0:T(8,128)S(1)}, f32[144,128]{1,0:T(8,128)S(1)}, u32[]{:S(2)}, u32[]{:S(2)}) collective-permute-start(f32[144,128]{1,0:T(8,128)S(1)} %get-tuple-element.33), channel_id=1, source_target_pairs={{0,6},{1,7},{2,4},{3,5},{4,2},{5,3},{6,0},{7,1},{8,14},{9,15},{10,... | collective-permute-start | bytes 221192 | tf_op jit(solution)/shard_map/ppermute | solution.py:296
  49.7 2.4 %collective-permute-start.15 = (f32[144,128]{1,0:T(8,128)S(1)}, f32[144,128]{1,0:T(8,128)S(1)}, u32[]{:S(2)}, u32[]{:S(2)}) collective-permute-start(f32[144,128]{1,0:T(8,128)S(1)} %get-tuple-element.34), channel_id=1, source_target_pairs={{0,7},{1,6},{2,5},{3,4},{4,3},{5,2},{6,1},{7,0},{8,15},{9,14},{10,... | collective-permute-start | bytes 221192 | tf_op jit(solution)/shard_map/ppermute | solution.py:296
  52.1 2.4 %collective-permute-done.12.rest_4_ = f32[144,128]{1,0:T(8,128)S(1)} collective-permute-done((f32[144,128]{1,0:T(8,128)S(1)}, f32[144,128]{1,0:T(8,128)S(1)}, u32[]{:S(2)}, u32[]{:S(2)}) %collective-permute-start.12) | collective-permute-done | bytes 73760 | tf_op jit(solution)/shard_map/ppermute | solution.py:296
  54.5 2.8 %collective-permute-done.13.rest_5_ = f32[144,128]{1,0:T(8,128)S(1)} collective-permute-done((f32[144,128]{1,0:T(8,128)S(1)}, f32[144,128]{1,0:T(8,128)S(1)}, u32[]{:S(2)}, u32[]{:S(2)}) %collective-permute-start.13) | collective-permute-done | bytes 73760 | tf_op jit(solution)/shard_map/ppermute | solution.py:296
  57.4 3.0 %merge.1 = (f32[136,128]{1,0:T(8,128)S(1)}, f32[136,128]{1,0:T(8,128)S(1)}, f32[136,128]{1,0:T(8,128)S(1)}, f32[136,128]{1,0:T(8,128)S(1)}, f32[136,128]{1,0:T(8...) custom-call(bf16[160,128]{1,0:T(8,128)(2,1)S(1)} %project.1.q_ref, ...), custom_call_target="tpu_custom_call" | custom-call | flops 268435456 | bytes 16777216 | tf_op jit(solution)/shard_map/merge/pallas_call | solution.py:470
  61.7 2.4 %collective-permute-start.17 = (f32[136,128]{1,0:T(8,128)S(1)}, f32[136,128]{1,0:T(8,128)S(1)}, u32[]{:S(2)}, u32[]{:S(2)}) collective-permute-start(f32[136,128]{1,0:T(8,128)S(1)} %get-tuple-element.37), channel_id=1, source_target_pairs={{0,2},{1,3},{2,0},{3,1},{4,6},{5,7},{6,4},{7,5},{8,10},{9,11},{10,... | collective-permute-start | bytes 208904 | tf_op jit(solution)/shard_map/ppermute | solution.py:296
  64.1 2.5 %collective-permute-start.19 = (f32[136,128]{1,0:T(8,128)S(1)}, f32[136,128]{1,0:T(8,128)S(1)}, u32[]{:S(2)}, u32[]{:S(2)}) collective-permute-start(f32[136,128]{1,0:T(8,128)S(1)} %get-tuple-element.39), channel_id=1, source_target_pairs={{0,4},{1,5},{2,6},{3,7},{4,0},{5,1},{6,2},{7,3},{8,12},{9,13},{10,... | collective-permute-start | bytes 208904 | tf_op jit(solution)/shard_map/ppermute | solution.py:296
  68.0 2.0 %collective-permute-start.21 = (f32[136,128]{1,0:T(8,128)S(1)}, f32[136,128]{1,0:T(8,128)S(1)}, u32[]{:S(2)}, u32[]{:S(2)}) collective-permute-start(f32[136,128]{1,0:T(8,128)S(1)} %get-tuple-element.41), channel_id=1, source_target_pairs={{0,6},{1,7},{2,4},{3,5},{4,2},{5,3},{6,0},{7,1},{8,14},{9,15},{10,... | collective-permute-start | bytes 208904 | tf_op jit(solution)/shard_map/ppermute | solution.py:296
  69.9 1.9 %collective-permute-start.22 = (f32[136,128]{1,0:T(8,128)S(1)}, f32[136,128]{1,0:T(8,128)S(1)}, u32[]{:S(2)}, u32[]{:S(2)}) collective-permute-start(f32[136,128]{1,0:T(8,128)S(1)} %get-tuple-element.42), channel_id=1, source_target_pairs={{0,7},{1,6},{2,5},{3,4},{4,3},{5,2},{6,1},{7,0},{8,15},{9,14},{10,... | collective-permute-start | bytes 208904 | tf_op jit(solution)/shard_map/ppermute | solution.py:296
  71.8 2.5 %collective-permute-done.19.refs_4_ = f32[136,128]{1,0:T(8,128)S(1)} collective-permute-done((f32[136,128]{1,0:T(8,128)S(1)}, f32[136,128]{1,0:T(8,128)S(1)}, u32[]{:S(2)}, u32[]{:S(2)}) %collective-permute-start.19) | collective-permute-done | bytes 69664 | tf_op jit(solution)/shard_map/ppermute | solution.py:296
  74.3 3.4 %collective-permute-done.20.refs_5_ = f32[136,128]{1,0:T(8,128)S(1)} collective-permute-done((f32[136,128]{1,0:T(8,128)S(1)}, f32[136,128]{1,0:T(8,128)S(1)}, u32[]{:S(2)}, u32[]{:S(2)}) %collective-permute-start.20) | collective-permute-done | bytes 69664 | tf_op jit(solution)/shard_map/ppermute | solution.py:296
  (74 shorter events, 14.2 us)
Async XLA Ops:
  0.7 6.8 %collective-permute-start = (bf16[16,1024]{1,0:T(8,128)(2,1)}, bf16[16,1024]{1,0:T(8,128)(2,1)S(1)}, u32[]{:S(2)}, u32[]{:S(2)}) collective-permute-start(bf16[16,1024]{1,0:T(8,128)(2,1)} %bitcast.42), channel_id=1, source_target_pairs={{0,1},{1,0},{2,3},{3,2},{4,5},{5,4},{6,7},{7,6},{8,9},{9,8},{10,11... | collective-permute-start | bytes 98312 | tf_op jit(solution)/shard_map/ppermute | solution.py:296
  7.5 6.7 %collective-permute-start.3 = (bf16[2,16,1024]{2,1,0:T(8,128)(2,1)S(1)}, bf16[2,16,1024]{2,1,0:T(8,128)(2,1)S(1)}, u32[]{:S(2)}, u32[]{:S(2)}) collective-permute-start(bf16[2,16,1024]{2,1,0:T(8,128)(2,1)S(1)} %pad_maximum_fusion.3), channel_id=1, source_target_pairs={{0,6},{1,7},{2,4},{3,5},{4,2},{5,3},{6,0},{7,1},{8,14},{9,15},{10,... | collective-permute-start | bytes 196616 | tf_op jit(solution)/shard_map/ppermute | solution.py:296
  11.6 5.4 %collective-permute-start.2 = (bf16[2,16,1024]{2,1,0:T(8,128)(2,1)S(1)}, bf16[2,16,1024]{2,1,0:T(8,128)(2,1)S(1)}, u32[]{:S(2)}, u32[]{:S(2)}) collective-permute-start(bf16[2,16,1024]{2,1,0:T(8,128)(2,1)S(1)} %pad_maximum_fusion.3), channel_id=1, source_target_pairs={{0,4},{1,5},{2,6},{3,7},{4,0},{5,1},{6,2},{7,3},{8,12},{9,13},{10,... | collective-permute-start | bytes 196616 | tf_op jit(solution)/shard_map/ppermute | solution.py:296
  11.6 5.4 %collective-permute-start.1 = (bf16[2,16,1024]{2,1,0:T(8,128)(2,1)S(1)}, bf16[2,16,1024]{2,1,0:T(8,128)(2,1)S(1)}, u32[]{:S(2)}, u32[]{:S(2)}) collective-permute-start(bf16[2,16,1024]{2,1,0:T(8,128)(2,1)S(1)} %pad_maximum_fusion.3), channel_id=1, source_target_pairs={{0,2},{1,3},{2,0},{3,1},{4,6},{5,7},{6,4},{7,5},{8,10},{9,11},{10,... | collective-permute-start | bytes 196616 | tf_op jit(solution)/shard_map/ppermute | solution.py:296
  17.0 1.6 %collective-permute-start.4 = (bf16[8,16,1024]{2,1,0:T(8,128)(2,1)S(1)}, bf16[8,16,1024]{2,1,0:T(8,128)(2,1)S(1)}, u32[]{:S(2)}, u32[]{:S(2)}) collective-permute-start(bf16[8,16,1024]{2,1,0:T(8,128)(2,1)S(1)} %bitcast.28), channel_id=1, source_target_pairs={{0,8},{8,0},{1,9},{9,1},{2,10},{10,2},{3,11},{11,3},{4,12},{12,4},... | collective-permute-start | bytes 786440 | tf_op jit(solution)/shard_map/ppermute | solution.py:367
  24.2 4.1 %collective-permute-start.5 = (bf16[160,128]{1,0:T(8,128)(2,1)S(1)}, bf16[160,128]{1,0:T(8,128)(2,1)S(1)}, u32[]{:S(2)}, u32[]{:S(2)}) collective-permute-start(bf16[160,128]{1,0:T(8,128)(2,1)S(1)} %project.1.q_ref), channel_id=1, source_target_pairs={{0,1},{1,0},{2,3},{3,2},{4,5},{5,4},{6,7},{7,6},{8,9},{9,8},{10,11... | collective-permute-start | bytes 122888 | tf_op jit(solution)/shard_map/ppermute | solution.py:296
  28.3 6.8 %collective-permute-start.8 = (bf16[2,160,128]{2,1,0:T(8,128)(2,1)S(1)}, bf16[2,160,128]{2,1,0:T(8,128)(2,1)S(1)}, u32[]{:S(2)}, u32[]{:S(2)}) collective-permute-start(bf16[2,160,128]{2,1,0:T(8,128)(2,1)S(1)} %get-tuple-element.47.after_ref), channel_id=1, source_target_pairs={{0,6},{1,7},{2,4},{3,5},{4,2},{5,3},{6,0},{7,1},{8,14},{9,15},{10,... | collective-permute-start | bytes 245768 | tf_op jit(solution)/shard_map/ppermute | solution.py:296
  31.1 6.8 %collective-permute-start.7 = (bf16[2,160,128]{2,1,0:T(8,128)(2,1)S(1)}, bf16[2,160,128]{2,1,0:T(8,128)(2,1)S(1)}, u32[]{:S(2)}, u32[]{:S(2)}) collective-permute-start(bf16[2,160,128]{2,1,0:T(8,128)(2,1)S(1)} %get-tuple-element.47.after_ref), channel_id=1, source_target_pairs={{0,4},{1,5},{2,6},{3,7},{4,0},{5,1},{6,2},{7,3},{8,12},{9,13},{10,... | collective-permute-start | bytes 245768 | tf_op jit(solution)/shard_map/ppermute | solution.py:296
  31.1 6.8 %collective-permute-start.6 = (bf16[2,160,128]{2,1,0:T(8,128)(2,1)S(1)}, bf16[2,160,128]{2,1,0:T(8,128)(2,1)S(1)}, u32[]{:S(2)}, u32[]{:S(2)}) collective-permute-start(bf16[2,160,128]{2,1,0:T(8,128)(2,1)S(1)} %get-tuple-element.47.after_ref), channel_id=1, source_target_pairs={{0,2},{1,3},{2,0},{3,1},{4,6},{5,7},{6,4},{7,5},{8,10},{9,11},{10,... | collective-permute-start | bytes 245768 | tf_op jit(solution)/shard_map/ppermute | solution.py:296
  40.9 6.2 %collective-permute-start.9 = (f32[144,128]{1,0:T(8,128)S(1)}, f32[144,128]{1,0:T(8,128)S(1)}, u32[]{:S(2)}, u32[]{:S(2)}) collective-permute-start(f32[144,128]{1,0:T(8,128)S(1)} %get-tuple-element.28), channel_id=1, source_target_pairs={{0,1},{1,0},{2,3},{3,2},{4,5},{5,4},{6,7},{7,6},{8,9},{9,8},{10,11... | collective-permute-start | bytes 221192 | tf_op jit(solution)/shard_map/ppermute | solution.py:296
  41.2 8.5 %collective-permute-start.10 = (f32[144,128]{1,0:T(8,128)S(1)}, f32[144,128]{1,0:T(8,128)S(1)}, u32[]{:S(2)}, u32[]{:S(2)}) collective-permute-start(f32[144,128]{1,0:T(8,128)S(1)} %get-tuple-element.29), channel_id=1, source_target_pairs={{0,2},{1,3},{2,0},{3,1},{4,6},{5,7},{6,4},{7,5},{8,10},{9,11},{10,... | collective-permute-start | bytes 221192 | tf_op jit(solution)/shard_map/ppermute | solution.py:296
  41.3 10.8 %collective-permute-start.11 = (f32[144,128]{1,0:T(8,128)S(1)}, f32[144,128]{1,0:T(8,128)S(1)}, u32[]{:S(2)}, u32[]{:S(2)}) collective-permute-start(f32[144,128]{1,0:T(8,128)S(1)} %get-tuple-element.30), channel_id=1, source_target_pairs={{0,3},{1,2},{2,1},{3,0},{4,7},{5,6},{6,5},{7,4},{8,11},{9,10},{10,... | collective-permute-start | bytes 221192 | tf_op jit(solution)/shard_map/ppermute | solution.py:296
  44.4 10.0 %collective-permute-start.12 = (f32[144,128]{1,0:T(8,128)S(1)}, f32[144,128]{1,0:T(8,128)S(1)}, u32[]{:S(2)}, u32[]{:S(2)}) collective-permute-start(f32[144,128]{1,0:T(8,128)S(1)} %get-tuple-element.31), channel_id=1, source_target_pairs={{0,4},{1,5},{2,6},{3,7},{4,0},{5,1},{6,2},{7,3},{8,12},{9,13},{10,... | collective-permute-start | bytes 221192 | tf_op jit(solution)/shard_map/ppermute | solution.py:296
  45.6 11.7 %collective-permute-start.13 = (f32[144,128]{1,0:T(8,128)S(1)}, f32[144,128]{1,0:T(8,128)S(1)}, u32[]{:S(2)}, u32[]{:S(2)}) collective-permute-start(f32[144,128]{1,0:T(8,128)S(1)} %get-tuple-element.32), channel_id=1, source_target_pairs={{0,5},{1,4},{2,7},{3,6},{4,1},{5,0},{6,3},{7,2},{8,13},{9,12},{10,... | collective-permute-start | bytes 221192 | tf_op jit(solution)/shard_map/ppermute | solution.py:296
  47.1 10.2 %collective-permute-start.14 = (f32[144,128]{1,0:T(8,128)S(1)}, f32[144,128]{1,0:T(8,128)S(1)}, u32[]{:S(2)}, u32[]{:S(2)}) collective-permute-start(f32[144,128]{1,0:T(8,128)S(1)} %get-tuple-element.33), channel_id=1, source_target_pairs={{0,6},{1,7},{2,4},{3,5},{4,2},{5,3},{6,0},{7,1},{8,14},{9,15},{10,... | collective-permute-start | bytes 221192 | tf_op jit(solution)/shard_map/ppermute | solution.py:296
  49.7 7.6 %collective-permute-start.15 = (f32[144,128]{1,0:T(8,128)S(1)}, f32[144,128]{1,0:T(8,128)S(1)}, u32[]{:S(2)}, u32[]{:S(2)}) collective-permute-start(f32[144,128]{1,0:T(8,128)S(1)} %get-tuple-element.34), channel_id=1, source_target_pairs={{0,7},{1,6},{2,5},{3,4},{4,3},{5,2},{6,1},{7,0},{8,15},{9,14},{10,... | collective-permute-start | bytes 221192 | tf_op jit(solution)/shard_map/ppermute | solution.py:296
  60.4 7.6 %collective-permute-start.16 = (f32[136,128]{1,0:T(8,128)S(1)}, f32[136,128]{1,0:T(8,128)S(1)}, u32[]{:S(2)}, u32[]{:S(2)}) collective-permute-start(f32[136,128]{1,0:T(8,128)S(1)} %get-tuple-element.36), channel_id=1, source_target_pairs={{0,1},{1,0},{2,3},{3,2},{4,5},{5,4},{6,7},{7,6},{8,9},{9,8},{10,11... | collective-permute-start | bytes 208904 | tf_op jit(solution)/shard_map/ppermute | solution.py:296
  61.7 8.2 %collective-permute-start.17 = (f32[136,128]{1,0:T(8,128)S(1)}, f32[136,128]{1,0:T(8,128)S(1)}, u32[]{:S(2)}, u32[]{:S(2)}) collective-permute-start(f32[136,128]{1,0:T(8,128)S(1)} %get-tuple-element.37), channel_id=1, source_target_pairs={{0,2},{1,3},{2,0},{3,1},{4,6},{5,7},{6,4},{7,5},{8,10},{9,11},{10,... | collective-permute-start | bytes 208904 | tf_op jit(solution)/shard_map/ppermute | solution.py:296
  64.1 7.7 %collective-permute-start.18 = (f32[136,128]{1,0:T(8,128)S(1)}, f32[136,128]{1,0:T(8,128)S(1)}, u32[]{:S(2)}, u32[]{:S(2)}) collective-permute-start(f32[136,128]{1,0:T(8,128)S(1)} %get-tuple-element.38), channel_id=1, source_target_pairs={{0,3},{1,2},{2,1},{3,0},{4,7},{5,6},{6,5},{7,4},{8,11},{9,10},{10,... | collective-permute-start | bytes 208904 | tf_op jit(solution)/shard_map/ppermute | solution.py:296
  64.1 10.2 %collective-permute-start.19 = (f32[136,128]{1,0:T(8,128)S(1)}, f32[136,128]{1,0:T(8,128)S(1)}, u32[]{:S(2)}, u32[]{:S(2)}) collective-permute-start(f32[136,128]{1,0:T(8,128)S(1)} %get-tuple-element.39), channel_id=1, source_target_pairs={{0,4},{1,5},{2,6},{3,7},{4,0},{5,1},{6,2},{7,3},{8,12},{9,13},{10,... | collective-permute-start | bytes 208904 | tf_op jit(solution)/shard_map/ppermute | solution.py:296
  66.6 11.1 %collective-permute-start.20 = (f32[136,128]{1,0:T(8,128)S(1)}, f32[136,128]{1,0:T(8,128)S(1)}, u32[]{:S(2)}, u32[]{:S(2)}) collective-permute-start(f32[136,128]{1,0:T(8,128)S(1)} %get-tuple-element.40), channel_id=1, source_target_pairs={{0,5},{1,4},{2,7},{3,6},{4,1},{5,0},{6,3},{7,2},{8,13},{9,12},{10,... | collective-permute-start | bytes 208904 | tf_op jit(solution)/shard_map/ppermute | solution.py:296
  68.0 9.7 %collective-permute-start.21 = (f32[136,128]{1,0:T(8,128)S(1)}, f32[136,128]{1,0:T(8,128)S(1)}, u32[]{:S(2)}, u32[]{:S(2)}) collective-permute-start(f32[136,128]{1,0:T(8,128)S(1)} %get-tuple-element.41), channel_id=1, source_target_pairs={{0,6},{1,7},{2,4},{3,5},{4,2},{5,3},{6,0},{7,1},{8,14},{9,15},{10,... | collective-permute-start | bytes 208904 | tf_op jit(solution)/shard_map/ppermute | solution.py:296
  69.9 7.8 %collective-permute-start.22 = (f32[136,128]{1,0:T(8,128)S(1)}, f32[136,128]{1,0:T(8,128)S(1)}, u32[]{:S(2)}, u32[]{:S(2)}) collective-permute-start(f32[136,128]{1,0:T(8,128)S(1)} %get-tuple-element.42), channel_id=1, source_target_pairs={{0,7},{1,6},{2,5},{3,4},{4,3},{5,2},{6,1},{7,0},{8,15},{9,14},{10,... | collective-permute-start | bytes 208904 | tf_op jit(solution)/shard_map/ppermute | solution.py:296
  77.7 1.3 %collective-permute-start.23 = (bf16[16,1024]{1,0:T(8,128)(2,1)S(1)}, bf16[16,1024]{1,0:T(8,128)(2,1)S(1)}, u32[]{:S(2)}, u32[]{:S(2)}) collective-permute-start(bf16[16,1024]{1,0:T(8,128)(2,1)S(1)} %get-tuple-element.45), channel_id=1, source_target_pairs={{0,8},{8,0},{1,9},{9,1},{2,10},{10,2},{3,11},{11,3},{4,12},{12,4},... | collective-permute-start | bytes 98312 | tf_op jit(solution)/shard_map/ppermute | solution.py:497
  (18 other events, 291.2 us)

commit v5 on v4

--- a/solution.py
+++ b/solution.py
@@ -44,8 +44,11 @@
     return pl.ds(pl.multiple_of(index * size, size), size)
 
 
-def plan_kernel(slots, steps, map_ref, length_ref, *rest):
-    meta_ref, take_ref, give_ref, before_ref, place_ref = rest[-5:]
+def early_kernel(*refs):
+    refs[-1][...] = jnp.zeros_like(refs[-1])
+
+
+def plan_kernel(slots, steps, map_ref, length_ref, meta_ref, take_ref, give_ref, before_ref, place_ref):
     count = map_ref.shape[0]
     mine = lax.axis_index("dp")
     base = mine * slots
@@ -114,7 +117,7 @@
                 out_ref[s, half * (EXT // 2) + c] = piece
 
 
-def project_kernel(pages, per_page, width, own_ref, far_ref, take_ref, gain_ref, wq_ref, wkv_ref, out_ref, tokens):
+def project_kernel(pages, per_page, width, after_ref, own_ref, far_ref, take_ref, gain_ref, wq_ref, wkv_ref, out_ref, tokens):
     me = lax.axis_index("tensor")
     chunks, rows, depth = own_ref.shape
     total = jnp.zeros((rows, depth), jnp.float32)
@@ -147,7 +150,7 @@
         out_ref[body + v * rows : body + (v + 1) * rows] = keyval[:, v * LANES : (v + 1) * LANES]
 
 
-def attend_kernel(pages, page_rows, split, meta_ref, q_ref, k_ref, v_ref, reward_ref, *rest):
+def attend_kernel(pages, page_rows, meta_ref, q_ref, k_ref, v_ref, reward_ref, *rest):
     outs, (spread, product) = rest[:-2], rest[-2:]
     width = k_ref.shape[1]
     span = KVH * page_rows
@@ -303,14 +306,17 @@
     pair = jnp.stack([x, partner(x, chunks, 1)])
     if tie is not None:
         pair, tie = lax.optimization_barrier((pair, tie))
+        after = tie
+    else:
+        after = pair
     others = [partner(pair, chunks, bits) for bits in (2, 4, 6)]
-    return jnp.stack([pair] + others).reshape((chunks,) + x.shape), pair
+    return jnp.stack([pair] + others).reshape((chunks,) + x.shape), after
 
 
 def trade(blocks, chunks):
     if len(blocks) == 1:
         return [lax.all_to_all(blocks[0], "tensor", 0, 0, tiled=True)]
-    traded = {bits: partner(blocks[bits], chunks, bits) for bits in (4, 5, 6, 7, 2, 3, 1)}
+    traded = {bits: partner(blocks[bits], chunks, bits) for bits in (6, 1, 7, 2, 5, 3, 4)}
     return [blocks[0]] + [traded[bits] for bits in range(1, chunks)]
 
 
@@ -347,7 +353,7 @@
 
     meta, take, give = pl.pallas_call(
         functools.partial(plan_kernel, slots, STEPS),
-        in_specs=[SMEM, SMEM] + [ANY] * 3,
+        in_specs=[SMEM, SMEM],
         out_specs=[SMEM, VMEM, VMEM],
         out_shape=(
             jax.ShapeDtypeStruct((2 * pages,), jnp.int32),
@@ -358,19 +364,26 @@
             pltpu.SMEM(slot_map.shape, jnp.int32),
             pltpu.SMEM(slot_map.shape, jnp.int32),
         ],
-        compiler_params=pltpu.CompilerParams(vmem_limit_bytes=42 * MIB),
-        cost_estimate=pl.CostEstimate(flops=0, bytes_accessed=1000, transcendentals=0),
+        compiler_params=pltpu.CompilerParams(vmem_limit_bytes=MIB),
         name="plan",
-    )(slot_map, lengths, w_out, w_out, w_out)
-
-    own, _ = spread_all(decode_inputs.reshape(rows, part), chunks, index, take)
+    )(slot_map, lengths)
+
+    early = pl.pallas_call(
+        early_kernel,
+        in_specs=[ANY] * 3,
+        out_specs=VMEM,
+        out_shape=jax.ShapeDtypeStruct((EXT, LANES), jnp.float32),
+        compiler_params=pltpu.CompilerParams(vmem_limit_bytes=38 * MIB),
+        name="early",
+    )(w_out, w_out, w_out)
+    own, after = spread_all(decode_inputs.reshape(rows, part), chunks, index, early)
     far = lax.ppermute(own, "dp", swap)
 
     pieces = max(kvcols // LANES, 1)
     packed_rows = body + pieces * rows
     packed = pl.pallas_call(
         functools.partial(project_kernel, pages, per_page, depth),
-        in_specs=[VMEM] * 6,
+        in_specs=[ANY] + [VMEM] * 6,
         out_specs=VMEM,
         out_shape=jax.ShapeDtypeStruct((packed_rows, LANES), jnp.bfloat16),
         scratch_shapes=[
@@ -383,7 +396,7 @@
             transcendentals=0,
         ),
         name="project",
-    )(own, far, take, attn_gain.reshape(chunks, 1, part), w_query, w_keyval)
+    )(after, own, far, take, attn_gain.reshape(chunks, 1, part), w_query, w_keyval)
     gathered, after = spread_all(packed, chunks, index)
 
     span = reward_hidden.shape[1]
@@ -435,7 +448,7 @@
     big = pages * page_rows
     block = (big + 2 * EXT, HD)
     attended = pl.pallas_call(
-        functools.partial(attend_kernel, pages, page_rows, split),
+        functools.partial(attend_kernel, pages, page_rows),
         in_specs=[SMEM] + [VMEM] * 4,
         out_specs=[VMEM] * (KVH if direct else 1),
         out_shape=(

time: 79.9 us -> 76 us (0.951)
  local copies, waits for them, and re-layouts: 5.29 us -> 0.72 us
  starting transfers between devices: 35.1 us -> 37.1 us
  waiting for transfers between devices: 24.7 us -> 23.3 us
    unnamed x36, local copies, waits for them, and re-layouts: 4.67 us -> 0.09 us
    ppermute x22, starting transfers between devices: 35 us -> 37 us  [partner(): return lax.ppermute(x, 'tensor', [(i, i ^ bits) for i in range(chunks)])]
    ppermute x1, waiting for transfers between devices: 1.52 us -> 0.16 us  [local(): far = lax.ppermute(own, 'dp', swap)]
    pallas_call x1 -> x2, Pallas kernels: 2.92 us -> 2.89 us  [the longest x1 2.89 us: local(): pl.pallas_call(functools.partial(attend_kernel, pages, page_rows), in_spe...]
  transfers between devices with their start and end apart: 24 -> 24, of which waited for: 10 -> 12; matrix products, arithmetic and copies ran while one was open for 1% -> 1% of each run, Pallas kernels for 5% -> 5%
where the time goes in v5:
time: 76 us; the launch traced here: 75.8 us
  starting transfers between devices  37.1 us (49%)
  waiting for transfers between devices  23.3 us (31%)
  Pallas kernels  12.8 us (17%)
  between operations  0.96 us (1%)
    ppermute x22, starting transfers between devices, partner(): return lax.ppermute(x, 'tensor', [(i, i ^ bits) for i in range(chunks)])  37 us
    ppermute x22, waiting for transfers between devices, partner(): return lax.ppermute(x, 'tensor', [(i, i ^ bits) for i in range(chunks)])  22.6 us
    pallas_call x1, Pallas kernels, local(): pl.pallas_call(functools.partial(project_kernel, pages, per_page, depth),...  3.28 us
    pallas_call x1, Pallas kernels, local(): pl.pallas_call(functools.partial(merge_kernel, pages, per_page, depth, sp...  3 us
    pallas_call x1, Pallas kernels, local(): pl.pallas_call(functools.partial(attend_kernel, pages, page_rows), in_spe...  2.89 us
    pallas_call x1, Pallas kernels, local(): pl.pallas_call(reward_kernel, in_specs=[ANY, ANY, VMEM, VMEM] + [ANY] * 0...  2.31 us
  transfers between devices with their start and end apart: 24, of which 12 were waited for; matrix products, arithmetic and copies ran while one was open for 1% of the time, Pallas kernels for 5%

profile of v5, /device:TPU:0, one launch (start us, length us, event | category | flops | bytes accessed | tf_op | source)
XLA Modules:
  0.0 75.8 jit_solution(16882103058903858579)
XLA Ops:
  0.7 3.1 %collective-permute-start = (bf16[16,1024]{1,0:T(8,128)(2,1)}, bf16[16,1024]{1,0:T(8,128)(2,1)S(1)}, u32[]{:S(2)}, u32[]{:S(2)}) collective-permute-start(bf16[16,1024]{1,0:T(8,128)(2,1)} %bitcast.42), channel_id=1, source_target_pairs={{0,1},{1,0},{2,3},{3,2},{4,5},{5,4},{6,7},{7,6},{8,9},{9,8},{10,11... | collective-permute-start | bytes 98312 | tf_op jit(solution)/shard_map/ppermute | solution.py:299
  3.8 2.1 %collective-permute-done = bf16[16,1024]{1,0:T(8,128)(2,1)S(1)} collective-permute-done((bf16[16,1024]{1,0:T(8,128)(2,1)}, bf16[16,1024]{1,0:T(8,128)(2,1)S(1)}, u32[]{:S(2)}, u32[]{:S(2)}) %collective-permute-start) | collective-permute-done | bytes 32800 | tf_op jit(solution)/shard_map/ppermute | solution.py:299
  5.9 4.2 %collective-permute-start.3 = (bf16[2,16,1024]{2,1,0:T(8,128)(2,1)S(1)}, bf16[2,16,1024]{2,1,0:T(8,128)(2,1)S(1)}, u32[]{:S(2)}, u32[]{:S(2)}) collective-permute-start(bf16[2,16,1024]{2,1,0:T(8,128)(2,1)S(1)} %pad_maximum_fusion.3), channel_id=1, source_target_pairs={{0,6},{1,7},{2,4},{3,5},{4,2},{5,3},{6,0},{7,1},{8,14},{9,15},{10,... | collective-permute-start | bytes 196616 | tf_op jit(solution)/shard_map/ppermute | solution.py:299
  10.7 1.8 %collective-permute-done.3 = bf16[2,16,1024]{2,1,0:T(8,128)(2,1)S(1)} collective-permute-done((bf16[2,16,1024]{2,1,0:T(8,128)(2,1)S(1)}, bf16[2,16,1024]{2,1,0:T(8,128)(2,1)S(1)}, u32[]{:S(2)}, u32[]{:S(2)}) %collective-permute-start.3) | collective-permute-done | bytes 65568 | tf_op jit(solution)/shard_map/ppermute | solution.py:299
  12.5 2.8 %collective-permute-done.2 = bf16[2,16,1024]{2,1,0:T(8,128)(2,1)S(1)} collective-permute-done((bf16[2,16,1024]{2,1,0:T(8,128)(2,1)S(1)}, bf16[2,16,1024]{2,1,0:T(8,128)(2,1)S(1)}, u32[]{:S(2)}, u32[]{:S(2)}) %collective-permute-start.2) | collective-permute-done | bytes 65568 | tf_op jit(solution)/shard_map/ppermute | solution.py:299
  17.0 3.3 %project.1.q_ref = bf16[160,128]{1,0:T(8,128)(2,1)S(1)} custom-call(f32[8,128]{1,0:T(8,128)S(1)} %early.1.after_ref, bf16[8,16,1024]{2,1,0:T(8,128)(2,1)S(1)} %bitcast.29, bf16[8,16,1024]{2,1,0:T(8,128)(2,1)S(1)} %collective-permute-done.4.far_ref, bf16[16,32]{1,0:T(8,128)(2,1)S(1)} %get-tuple-element.27.take_ref, f32[8,1,1024]{2,1,0:T(1,128)S(1)} %bitcast.31, ...), custom_call_target="tpu_custom_call" | custom-call | flops 335544320 | bytes 20971520 | tf_op jit(solution)/shard_map/project/pallas_call | solution.py:384
  21.9 2.5 %collective-permute-done.5 = bf16[160,128]{1,0:T(8,128)(2,1)S(1)} collective-permute-done((bf16[160,128]{1,0:T(8,128)(2,1)S(1)}, bf16[160,128]{1,0:T(8,128)(2,1)S(1)}, u32[]{:S(2)}, u32[]{:S(2)}) %collective-permute-start.5) | collective-permute-done | bytes 40992 | tf_op jit(solution)/shard_map/ppermute | solution.py:299
  24.4 2.2 %collective-permute-start.8 = (bf16[2,160,128]{2,1,0:T(8,128)(2,1)S(1)}, bf16[2,160,128]{2,1,0:T(8,128)(2,1)S(1)}, u32[]{:S(2)}, u32[]{:S(2)}) collective-permute-start(bf16[2,160,128]{2,1,0:T(8,128)(2,1)S(1)} %get-tuple-element.49.after_ref), channel_id=1, source_target_pairs={{0,6},{1,7},{2,4},{3,5},{4,2},{5,3},{6,0},{7,1},{8,14},{9,15},{10,... | collective-permute-start | bytes 245768 | tf_op jit(solution)/shard_map/ppermute | solution.py:299
  26.6 2.3 %collective-permute-start.6 = (bf16[2,160,128]{2,1,0:T(8,128)(2,1)S(1)}, bf16[2,160,128]{2,1,0:T(8,128)(2,1)S(1)}, u32[]{:S(2)}, u32[]{:S(2)}) collective-permute-start(bf16[2,160,128]{2,1,0:T(8,128)(2,1)S(1)} %get-tuple-element.49.after_ref), channel_id=1, source_target_pairs={{0,2},{1,3},{2,0},{3,1},{4,6},{5,7},{6,4},{7,5},{8,10},{9,11},{10,... | collective-permute-start | bytes 245768 | tf_op jit(solution)/shard_map/ppermute | solution.py:299
  28.9 2.3 %reward.1.reward_ref = f32[8,8,128]{2,1,0:T(8,128)S(1)} custom-call(bf16[2,160,128]{2,1,0:T(8,128)(2,1)S(1)} %get-tuple-element.49.after_ref, bf16[8,256,1024]{2,1,0:T(8,128)(2,1)S(1)} %copy-done, f32[1,1024]{1,0:T(1,128)S(1)} %bitcast.32, f32[1,1024]{1,0:T(1,128)S(1)} %bitcast.33), custom_call_target="tpu_custom_call" | custom-call | flops 8388608 | bytes 4194304 | tf_op jit(solution)/shard_map/reward/pallas_call | solution.py:404
  31.3 2.8 %collective-permute-done.7 = bf16[2,160,128]{2,1,0:T(8,128)(2,1)S(1)} collective-permute-done((bf16[2,160,128]{2,1,0:T(8,128)(2,1)S(1)}, bf16[2,160,128]{2,1,0:T(8,128)(2,1)S(1)}, u32[]{:S(2)}, u32[]{:S(2)}) %collective-permute-start.7) | collective-permute-done | bytes 81952 | tf_op jit(solution)/shard_map/ppermute | solution.py:299
  34.2 2.9 %attend.1 = (f32[144,128]{1,0:T(8,128)S(1)}, f32[144,128]{1,0:T(8,128)S(1)}, f32[144,128]{1,0:T(8,128)S(1)}, f32[144,128]{1,0:T(8,128)S(1)}, f32[144,128]{1,0:T(...) custom-call(s32[8]{0:T(128)S(1)} %get-tuple-element.28.meta_ref, ...), custom_call_target="tpu_custom_call" | custom-call | flops 1073741824 | bytes 4194304 | tf_op jit(solution)/shard_map/attend/pallas_call | solution.py:450
  38.7 2.0 %collective-permute-start.11 = (f32[144,128]{1,0:T(8,128)S(1)}, f32[144,128]{1,0:T(8,128)S(1)}, u32[]{:S(2)}, u32[]{:S(2)}) collective-permute-start(f32[144,128]{1,0:T(8,128)S(1)} %get-tuple-element.32), channel_id=1, source_target_pairs={{0,3},{1,2},{2,1},{3,0},{4,7},{5,6},{6,5},{7,4},{8,11},{9,10},{10,... | collective-permute-start | bytes 221192 | tf_op jit(solution)/shard_map/ppermute | solution.py:299
  41.4 3.1 %collective-permute-start.13 = (f32[144,128]{1,0:T(8,128)S(1)}, f32[144,128]{1,0:T(8,128)S(1)}, u32[]{:S(2)}, u32[]{:S(2)}) collective-permute-start(f32[144,128]{1,0:T(8,128)S(1)} %get-tuple-element.34), channel_id=1, source_target_pairs={{0,5},{1,4},{2,7},{3,6},{4,1},{5,0},{6,3},{7,2},{8,13},{9,12},{10,... | collective-permute-start | bytes 221192 | tf_op jit(solution)/shard_map/ppermute | solution.py:299
  44.6 2.1 %collective-permute-start.14 = (f32[144,128]{1,0:T(8,128)S(1)}, f32[144,128]{1,0:T(8,128)S(1)}, u32[]{:S(2)}, u32[]{:S(2)}) collective-permute-start(f32[144,128]{1,0:T(8,128)S(1)} %get-tuple-element.35), channel_id=1, source_target_pairs={{0,6},{1,7},{2,4},{3,5},{4,2},{5,3},{6,0},{7,1},{8,14},{9,15},{10,... | collective-permute-start | bytes 221192 | tf_op jit(solution)/shard_map/ppermute | solution.py:299
  48.4 3.1 %collective-permute-done.12.rest_4_ = f32[144,128]{1,0:T(8,128)S(1)} collective-permute-done((f32[144,128]{1,0:T(8,128)S(1)}, f32[144,128]{1,0:T(8,128)S(1)}, u32[]{:S(2)}, u32[]{:S(2)}) %collective-permute-start.12) | collective-permute-done | bytes 73760 | tf_op jit(solution)/shard_map/ppermute | solution.py:299
  51.4 2.7 %collective-permute-done.13.rest_5_ = f32[144,128]{1,0:T(8,128)S(1)} collective-permute-done((f32[144,128]{1,0:T(8,128)S(1)}, f32[144,128]{1,0:T(8,128)S(1)}, u32[]{:S(2)}, u32[]{:S(2)}) %collective-permute-start.13) | collective-permute-done | bytes 73760 | tf_op jit(solution)/shard_map/ppermute | solution.py:299
  54.2 3.0 %merge.1 = (f32[136,128]{1,0:T(8,128)S(1)}, f32[136,128]{1,0:T(8,128)S(1)}, f32[136,128]{1,0:T(8,128)S(1)}, f32[136,128]{1,0:T(8,128)S(1)}, f32[136,128]{1,0:T(8...) custom-call(bf16[160,128]{1,0:T(8,128)(2,1)S(1)} %project.1.q_ref, ...), custom_call_target="tpu_custom_call" | custom-call | flops 268435456 | bytes 16777216 | tf_op jit(solution)/shard_map/merge/pallas_call | solution.py:483
  58.3 2.1 %collective-permute-start.17 = (f32[136,128]{1,0:T(8,128)S(1)}, f32[136,128]{1,0:T(8,128)S(1)}, u32[]{:S(2)}, u32[]{:S(2)}) collective-permute-start(f32[136,128]{1,0:T(8,128)S(1)} %get-tuple-element.39), channel_id=1, source_target_pairs={{0,2},{1,3},{2,0},{3,1},{4,6},{5,7},{6,4},{7,5},{8,10},{9,11},{10,... | collective-permute-start | bytes 208904 | tf_op jit(solution)/shard_map/ppermute | solution.py:299
  61.4 2.2 %collective-permute-start.19 = (f32[136,128]{1,0:T(8,128)S(1)}, f32[136,128]{1,0:T(8,128)S(1)}, u32[]{:S(2)}, u32[]{:S(2)}) collective-permute-start(f32[136,128]{1,0:T(8,128)S(1)} %get-tuple-element.41), channel_id=1, source_target_pairs={{0,4},{1,5},{2,6},{3,7},{4,0},{5,1},{6,2},{7,3},{8,12},{9,13},{10,... | collective-permute-start | bytes 208904 | tf_op jit(solution)/shard_map/ppermute | solution.py:299
  64.3 1.9 %collective-permute-start.21 = (f32[136,128]{1,0:T(8,128)S(1)}, f32[136,128]{1,0:T(8,128)S(1)}, u32[]{:S(2)}, u32[]{:S(2)}) collective-permute-start(f32[136,128]{1,0:T(8,128)S(1)} %get-tuple-element.43), channel_id=1, source_target_pairs={{0,6},{1,7},{2,4},{3,5},{4,2},{5,3},{6,0},{7,1},{8,14},{9,15},{10,... | collective-permute-start | bytes 208904 | tf_op jit(solution)/shard_map/ppermute | solution.py:299
  66.2 2.8 %collective-permute-start.22 = (f32[136,128]{1,0:T(8,128)S(1)}, f32[136,128]{1,0:T(8,128)S(1)}, u32[]{:S(2)}, u32[]{:S(2)}) collective-permute-start(f32[136,128]{1,0:T(8,128)S(1)} %get-tuple-element.44), channel_id=1, source_target_pairs={{0,7},{1,6},{2,5},{3,4},{4,3},{5,2},{6,1},{7,0},{8,15},{9,14},{10,... | collective-permute-start | bytes 208904 | tf_op jit(solution)/shard_map/ppermute | solution.py:299
  69.1 2.8 %collective-permute-done.19.refs_4_ = f32[136,128]{1,0:T(8,128)S(1)} collective-permute-done((f32[136,128]{1,0:T(8,128)S(1)}, f32[136,128]{1,0:T(8,128)S(1)}, u32[]{:S(2)}, u32[]{:S(2)}) %collective-permute-start.19) | collective-permute-done | bytes 69664 | tf_op jit(solution)/shard_map/ppermute | solution.py:299
  71.8 1.9 %collective-permute-done.20.refs_5_ = f32[136,128]{1,0:T(8,128)S(1)} collective-permute-done((f32[136,128]{1,0:T(8,128)S(1)}, f32[136,128]{1,0:T(8,128)S(1)}, u32[]{:S(2)}, u32[]{:S(2)}) %collective-permute-start.20) | collective-permute-done | bytes 69664 | tf_op jit(solution)/shard_map/ppermute | solution.py:299
  (75 shorter events, 12.9 us)
Async XLA Ops:
  0.7 5.2 %collective-permute-start = (bf16[16,1024]{1,0:T(8,128)(2,1)}, bf16[16,1024]{1,0:T(8,128)(2,1)S(1)}, u32[]{:S(2)}, u32[]{:S(2)}) collective-permute-start(bf16[16,1024]{1,0:T(8,128)(2,1)} %bitcast.42), channel_id=1, source_target_pairs={{0,1},{1,0},{2,3},{3,2},{4,5},{5,4},{6,7},{7,6},{8,9},{9,8},{10,11... | collective-permute-start | bytes 98312 | tf_op jit(solution)/shard_map/ppermute | solution.py:299
  5.9 6.6 %collective-permute-start.3 = (bf16[2,16,1024]{2,1,0:T(8,128)(2,1)S(1)}, bf16[2,16,1024]{2,1,0:T(8,128)(2,1)S(1)}, u32[]{:S(2)}, u32[]{:S(2)}) collective-permute-start(bf16[2,16,1024]{2,1,0:T(8,128)(2,1)S(1)} %pad_maximum_fusion.3), channel_id=1, source_target_pairs={{0,6},{1,7},{2,4},{3,5},{4,2},{5,3},{6,0},{7,1},{8,14},{9,15},{10,... | collective-permute-start | bytes 196616 | tf_op jit(solution)/shard_map/ppermute | solution.py:299
  10.1 5.2 %collective-permute-start.2 = (bf16[2,16,1024]{2,1,0:T(8,128)(2,1)S(1)}, bf16[2,16,1024]{2,1,0:T(8,128)(2,1)S(1)}, u32[]{:S(2)}, u32[]{:S(2)}) collective-permute-start(bf16[2,16,1024]{2,1,0:T(8,128)(2,1)S(1)} %pad_maximum_fusion.3), channel_id=1, source_target_pairs={{0,4},{1,5},{2,6},{3,7},{4,0},{5,1},{6,2},{7,3},{8,12},{9,13},{10,... | collective-permute-start | bytes 196616 | tf_op jit(solution)/shard_map/ppermute | solution.py:299
  10.1 5.2 %collective-permute-start.1 = (bf16[2,16,1024]{2,1,0:T(8,128)(2,1)S(1)}, bf16[2,16,1024]{2,1,0:T(8,128)(2,1)S(1)}, u32[]{:S(2)}, u32[]{:S(2)}) collective-permute-start(bf16[2,16,1024]{2,1,0:T(8,128)(2,1)S(1)} %pad_maximum_fusion.3), channel_id=1, source_target_pairs={{0,2},{1,3},{2,0},{3,1},{4,6},{5,7},{6,4},{7,5},{8,10},{9,11},{10,... | collective-permute-start | bytes 196616 | tf_op jit(solution)/shard_map/ppermute | solution.py:299
  15.3 1.6 %collective-permute-start.4 = (bf16[8,16,1024]{2,1,0:T(8,128)(2,1)S(1)}, bf16[8,16,1024]{2,1,0:T(8,128)(2,1)S(1)}, u32[]{:S(2)}, u32[]{:S(2)}) collective-permute-start(bf16[8,16,1024]{2,1,0:T(8,128)(2,1)S(1)} %bitcast.28), channel_id=1, source_target_pairs={{0,8},{8,0},{1,9},{9,1},{2,10},{10,2},{3,11},{11,3},{4,12},{12,4},... | collective-permute-start | bytes 786440 | tf_op jit(solution)/shard_map/ppermute | solution.py:380
  20.3 4.1 %collective-permute-start.5 = (bf16[160,128]{1,0:T(8,128)(2,1)S(1)}, bf16[160,128]{1,0:T(8,128)(2,1)S(1)}, u32[]{:S(2)}, u32[]{:S(2)}) collective-permute-start(bf16[160,128]{1,0:T(8,128)(2,1)S(1)} %project.1.q_ref), channel_id=1, source_target_pairs={{0,1},{1,0},{2,3},{3,2},{4,5},{5,4},{6,7},{7,6},{8,9},{9,8},{10,11... | collective-permute-start | bytes 122888 | tf_op jit(solution)/shard_map/ppermute | solution.py:299
  24.4 6.9 %collective-permute-start.8 = (bf16[2,160,128]{2,1,0:T(8,128)(2,1)S(1)}, bf16[2,160,128]{2,1,0:T(8,128)(2,1)S(1)}, u32[]{:S(2)}, u32[]{:S(2)}) collective-permute-start(bf16[2,160,128]{2,1,0:T(8,128)(2,1)S(1)} %get-tuple-element.49.after_ref), channel_id=1, source_target_pairs={{0,6},{1,7},{2,4},{3,5},{4,2},{5,3},{6,0},{7,1},{8,14},{9,15},{10,... | collective-permute-start | bytes 245768 | tf_op jit(solution)/shard_map/ppermute | solution.py:299
  26.6 7.6 %collective-permute-start.7 = (bf16[2,160,128]{2,1,0:T(8,128)(2,1)S(1)}, bf16[2,160,128]{2,1,0:T(8,128)(2,1)S(1)}, u32[]{:S(2)}, u32[]{:S(2)}) collective-permute-start(bf16[2,160,128]{2,1,0:T(8,128)(2,1)S(1)} %get-tuple-element.49.after_ref), channel_id=1, source_target_pairs={{0,4},{1,5},{2,6},{3,7},{4,0},{5,1},{6,2},{7,3},{8,12},{9,13},{10,... | collective-permute-start | bytes 245768 | tf_op jit(solution)/shard_map/ppermute | solution.py:299
  26.6 7.6 %collective-permute-start.6 = (bf16[2,160,128]{2,1,0:T(8,128)(2,1)S(1)}, bf16[2,160,128]{2,1,0:T(8,128)(2,1)S(1)}, u32[]{:S(2)}, u32[]{:S(2)}) collective-permute-start(bf16[2,160,128]{2,1,0:T(8,128)(2,1)S(1)} %get-tuple-element.49.after_ref), channel_id=1, source_target_pairs={{0,2},{1,3},{2,0},{3,1},{4,6},{5,7},{6,4},{7,5},{8,10},{9,11},{10,... | collective-permute-start | bytes 245768 | tf_op jit(solution)/shard_map/ppermute | solution.py:299
  37.1 7.4 %collective-permute-start.9 = (f32[144,128]{1,0:T(8,128)S(1)}, f32[144,128]{1,0:T(8,128)S(1)}, u32[]{:S(2)}, u32[]{:S(2)}) collective-permute-start(f32[144,128]{1,0:T(8,128)S(1)} %get-tuple-element.30), channel_id=1, source_target_pairs={{0,1},{1,0},{2,3},{3,2},{4,5},{5,4},{6,7},{7,6},{8,9},{9,8},{10,11... | collective-permute-start | bytes 221192 | tf_op jit(solution)/shard_map/ppermute | solution.py:299
  38.7 8.0 %collective-permute-start.10 = (f32[144,128]{1,0:T(8,128)S(1)}, f32[144,128]{1,0:T(8,128)S(1)}, u32[]{:S(2)}, u32[]{:S(2)}) collective-permute-start(f32[144,128]{1,0:T(8,128)S(1)} %get-tuple-element.31), channel_id=1, source_target_pairs={{0,2},{1,3},{2,0},{3,1},{4,6},{5,7},{6,4},{7,5},{8,10},{9,11},{10,... | collective-permute-start | bytes 221192 | tf_op jit(solution)/shard_map/ppermute | solution.py:299
  38.7 9.6 %collective-permute-start.11 = (f32[144,128]{1,0:T(8,128)S(1)}, f32[144,128]{1,0:T(8,128)S(1)}, u32[]{:S(2)}, u32[]{:S(2)}) collective-permute-start(f32[144,128]{1,0:T(8,128)S(1)} %get-tuple-element.32), channel_id=1, source_target_pairs={{0,3},{1,2},{2,1},{3,0},{4,7},{5,6},{6,5},{7,4},{8,11},{9,10},{10,... | collective-permute-start | bytes 221192 | tf_op jit(solution)/shard_map/ppermute | solution.py:299
  40.7 10.7 %collective-permute-start.12 = (f32[144,128]{1,0:T(8,128)S(1)}, f32[144,128]{1,0:T(8,128)S(1)}, u32[]{:S(2)}, u32[]{:S(2)}) collective-permute-start(f32[144,128]{1,0:T(8,128)S(1)} %get-tuple-element.33), channel_id=1, source_target_pairs={{0,4},{1,5},{2,6},{3,7},{4,0},{5,1},{6,2},{7,3},{8,12},{9,13},{10,... | collective-permute-start | bytes 221192 | tf_op jit(solution)/shard_map/ppermute | solution.py:299
  41.4 12.7 %collective-permute-start.13 = (f32[144,128]{1,0:T(8,128)S(1)}, f32[144,128]{1,0:T(8,128)S(1)}, u32[]{:S(2)}, u32[]{:S(2)}) collective-permute-start(f32[144,128]{1,0:T(8,128)S(1)} %get-tuple-element.34), channel_id=1, source_target_pairs={{0,5},{1,4},{2,7},{3,6},{4,1},{5,0},{6,3},{7,2},{8,13},{9,12},{10,... | collective-permute-start | bytes 221192 | tf_op jit(solution)/shard_map/ppermute | solution.py:299
  44.6 9.5 %collective-permute-start.14 = (f32[144,128]{1,0:T(8,128)S(1)}, f32[144,128]{1,0:T(8,128)S(1)}, u32[]{:S(2)}, u32[]{:S(2)}) collective-permute-start(f32[144,128]{1,0:T(8,128)S(1)} %get-tuple-element.35), channel_id=1, source_target_pairs={{0,6},{1,7},{2,4},{3,5},{4,2},{5,3},{6,0},{7,1},{8,14},{9,15},{10,... | collective-permute-start | bytes 221192 | tf_op jit(solution)/shard_map/ppermute | solution.py:299
  46.7 7.4 %collective-permute-start.15 = (f32[144,128]{1,0:T(8,128)S(1)}, f32[144,128]{1,0:T(8,128)S(1)}, u32[]{:S(2)}, u32[]{:S(2)}) collective-permute-start(f32[144,128]{1,0:T(8,128)S(1)} %get-tuple-element.36), channel_id=1, source_target_pairs={{0,7},{1,6},{2,5},{3,4},{4,3},{5,2},{6,1},{7,0},{8,15},{9,14},{10,... | collective-permute-start | bytes 221192 | tf_op jit(solution)/shard_map/ppermute | solution.py:299
  57.2 7.2 %collective-permute-start.16 = (f32[136,128]{1,0:T(8,128)S(1)}, f32[136,128]{1,0:T(8,128)S(1)}, u32[]{:S(2)}, u32[]{:S(2)}) collective-permute-start(f32[136,128]{1,0:T(8,128)S(1)} %get-tuple-element.38), channel_id=1, source_target_pairs={{0,1},{1,0},{2,3},{3,2},{4,5},{5,4},{6,7},{7,6},{8,9},{9,8},{10,11... | collective-permute-start | bytes 208904 | tf_op jit(solution)/shard_map/ppermute | solution.py:299
  58.3 7.9 %collective-permute-start.17 = (f32[136,128]{1,0:T(8,128)S(1)}, f32[136,128]{1,0:T(8,128)S(1)}, u32[]{:S(2)}, u32[]{:S(2)}) collective-permute-start(f32[136,128]{1,0:T(8,128)S(1)} %get-tuple-element.39), channel_id=1, source_target_pairs={{0,2},{1,3},{2,0},{3,1},{4,6},{5,7},{6,4},{7,5},{8,10},{9,11},{10,... | collective-permute-start | bytes 208904 | tf_op jit(solution)/shard_map/ppermute | solution.py:299
  60.4 8.6 %collective-permute-start.18 = (f32[136,128]{1,0:T(8,128)S(1)}, f32[136,128]{1,0:T(8,128)S(1)}, u32[]{:S(2)}, u32[]{:S(2)}) collective-permute-start(f32[136,128]{1,0:T(8,128)S(1)} %get-tuple-element.40), channel_id=1, source_target_pairs={{0,3},{1,2},{2,1},{3,0},{4,7},{5,6},{6,5},{7,4},{8,11},{9,10},{10,... | collective-permute-start | bytes 208904 | tf_op jit(solution)/shard_map/ppermute | solution.py:299
  61.4 10.4 %collective-permute-start.19 = (f32[136,128]{1,0:T(8,128)S(1)}, f32[136,128]{1,0:T(8,128)S(1)}, u32[]{:S(2)}, u32[]{:S(2)}) collective-permute-start(f32[136,128]{1,0:T(8,128)S(1)} %get-tuple-element.41), channel_id=1, source_target_pairs={{0,4},{1,5},{2,6},{3,7},{4,0},{5,1},{6,2},{7,3},{8,12},{9,13},{10,... | collective-permute-start | bytes 208904 | tf_op jit(solution)/shard_map/ppermute | solution.py:299
  63.6 10.1 %collective-permute-start.20 = (f32[136,128]{1,0:T(8,128)S(1)}, f32[136,128]{1,0:T(8,128)S(1)}, u32[]{:S(2)}, u32[]{:S(2)}) collective-permute-start(f32[136,128]{1,0:T(8,128)S(1)} %get-tuple-element.42), channel_id=1, source_target_pairs={{0,5},{1,4},{2,7},{3,6},{4,1},{5,0},{6,3},{7,2},{8,13},{9,12},{10,... | collective-permute-start | bytes 208904 | tf_op jit(solution)/shard_map/ppermute | solution.py:299
  64.3 9.4 %collective-permute-start.21 = (f32[136,128]{1,0:T(8,128)S(1)}, f32[136,128]{1,0:T(8,128)S(1)}, u32[]{:S(2)}, u32[]{:S(2)}) collective-permute-start(f32[136,128]{1,0:T(8,128)S(1)} %get-tuple-element.43), channel_id=1, source_target_pairs={{0,6},{1,7},{2,4},{3,5},{4,2},{5,3},{6,0},{7,1},{8,14},{9,15},{10,... | collective-permute-start | bytes 208904 | tf_op jit(solution)/shard_map/ppermute | solution.py:299
  66.2 7.5 %collective-permute-start.22 = (f32[136,128]{1,0:T(8,128)S(1)}, f32[136,128]{1,0:T(8,128)S(1)}, u32[]{:S(2)}, u32[]{:S(2)}) collective-permute-start(f32[136,128]{1,0:T(8,128)S(1)} %get-tuple-element.44), channel_id=1, source_target_pairs={{0,7},{1,6},{2,5},{3,4},{4,3},{5,2},{6,1},{7,0},{8,15},{9,14},{10,... | collective-permute-start | bytes 208904 | tf_op jit(solution)/shard_map/ppermute | solution.py:299
  73.8 1.3 %collective-permute-start.23 = (bf16[16,1024]{1,0:T(8,128)(2,1)S(1)}, bf16[16,1024]{1,0:T(8,128)(2,1)S(1)}, u32[]{:S(2)}, u32[]{:S(2)}) collective-permute-start(bf16[16,1024]{1,0:T(8,128)(2,1)S(1)} %get-tuple-element.47), channel_id=1, source_target_pairs={{0,8},{8,0},{1,9},{9,1},{2,10},{10,2},{3,11},{11,3},{4,12},{12,4},... | collective-permute-start | bytes 98312 | tf_op jit(solution)/shard_map/ppermute | solution.py:510
  (18 other events, 330.3 us)

commit v6 on v5

--- a/solution.py
+++ b/solution.py
@@ -6,6 +6,7 @@
 from jax.experimental import pallas as pl
 from jax.experimental.pallas import tpu as pltpu
 from jax.sharding import PartitionSpec as P
+
 
 HD = 128
 KVH = 8
@@ -295,6 +296,10 @@
     reward_ref[...] = total[total.shape[0] - EXT :]
 
 
+LINE = (6, 2, 4)
+ALL = (6, 1, 7, 2, 5, 3, 4)
+
+
 def partner(x, chunks, bits):
     return lax.ppermute(x, "tensor", [(i, i ^ bits) for i in range(chunks)])
 
@@ -309,14 +314,14 @@
         after = tie
     else:
         after = pair
-    others = [partner(pair, chunks, bits) for bits in (2, 4, 6)]
-    return jnp.stack([pair] + others).reshape((chunks,) + x.shape), after
+    others = {bits: partner(pair, chunks, bits) for bits in LINE}
+    return jnp.stack([pair] + [others[bits] for bits in sorted(LINE)]).reshape((chunks,) + x.shape), after
 
 
 def trade(blocks, chunks):
     if len(blocks) == 1:
         return [lax.all_to_all(blocks[0], "tensor", 0, 0, tiled=True)]
-    traded = {bits: partner(blocks[bits], chunks, bits) for bits in (6, 1, 7, 2, 5, 3, 4)}
+    traded = {bits: partner(blocks[bits], chunks, bits) for bits in ALL}
     return [blocks[0]] + [traded[bits] for bits in range(1, chunks)]
 
 
@@ -513,8 +518,13 @@
 
 
 def solution(mesh):
+    chunks = mesh.shape["tensor"]
+
+    def body(*arrays):
+        return local(chunks, *arrays)
+
     return jax.shard_map(
-        functools.partial(local, mesh.shape["tensor"]),
+        body,
         mesh=mesh,
         in_specs=(
             P(("groups", "dp"), None, "tensor"),

time: 76 us -> 76 us (level)
  no operation moved by 1% of the time
where the time goes in v6:
time: 76 us; the launch traced here: 75.8 us
  starting transfers between devices  37.1 us (49%)
  waiting for transfers between devices  23.3 us (31%)
  Pallas kernels  12.8 us (17%)
  between operations  0.96 us (1%)
    ppermute x22, starting transfers between devices, partner(): return lax.ppermute(x, 'tensor', [(i, i ^ bits) for i in range(chunks)])  37 us
    ppermute x22, waiting for transfers between devices, partner(): return lax.ppermute(x, 'tensor', [(i, i ^ bits) for i in range(chunks)])  22.6 us
    pallas_call x1, Pallas kernels, local(): pl.pallas_call(functools.partial(project_kernel, pages, per_page, depth),...  3.28 us
    pallas_call x1, Pallas kernels, local(): pl.pallas_call(functools.partial(merge_kernel, pages, per_page, depth, sp...  3 us
    pallas_call x1, Pallas kernels, local(): pl.pallas_call(functools.partial(attend_kernel, pages, page_rows), in_spe...  2.89 us
    pallas_call x1, Pallas kernels, local(): pl.pallas_call(reward_kernel, in_specs=[ANY, ANY, VMEM, VMEM] + [ANY] * 0...  2.31 us
  transfers between devices with their start and end apart: 24, of which 12 were waited for; matrix products, arithmetic and copies ran while one was open for 1% of the time, Pallas kernels for 5%

profile of v6, /device:TPU:0, one launch (start us, length us, event | category | flops | bytes accessed | tf_op | source)
XLA Modules:
  0.0 75.8 jit_solution(16882103058903858579)
XLA Ops:
  0.7 3.1 %collective-permute-start = (bf16[16,1024]{1,0:T(8,128)(2,1)}, bf16[16,1024]{1,0:T(8,128)(2,1)S(1)}, u32[]{:S(2)}, u32[]{:S(2)}) collective-permute-start(bf16[16,1024]{1,0:T(8,128)(2,1)} %bitcast.42), channel_id=1, source_target_pairs={{0,1},{1,0},{2,3},{3,2},{4,5},{5,4},{6,7},{7,6},{8,9},{9,8},{10,11... | collective-permute-start | bytes 98312 | tf_op jit(solution)/shard_map/ppermute | solution.py:304
  3.8 2.1 %collective-permute-done = bf16[16,1024]{1,0:T(8,128)(2,1)S(1)} collective-permute-done((bf16[16,1024]{1,0:T(8,128)(2,1)}, bf16[16,1024]{1,0:T(8,128)(2,1)S(1)}, u32[]{:S(2)}, u32[]{:S(2)}) %collective-permute-start) | collective-permute-done | bytes 32800 | tf_op jit(solution)/shard_map/ppermute | solution.py:304
  5.9 4.2 %collective-permute-start.3 = (bf16[2,16,1024]{2,1,0:T(8,128)(2,1)S(1)}, bf16[2,16,1024]{2,1,0:T(8,128)(2,1)S(1)}, u32[]{:S(2)}, u32[]{:S(2)}) collective-permute-start(bf16[2,16,1024]{2,1,0:T(8,128)(2,1)S(1)} %pad_maximum_fusion.3), channel_id=1, source_target_pairs={{0,6},{1,7},{2,4},{3,5},{4,2},{5,3},{6,0},{7,1},{8,14},{9,15},{10,... | collective-permute-start | bytes 196616 | tf_op jit(solution)/shard_map/ppermute | solution.py:304
  10.7 1.8 %collective-permute-done.3 = bf16[2,16,1024]{2,1,0:T(8,128)(2,1)S(1)} collective-permute-done((bf16[2,16,1024]{2,1,0:T(8,128)(2,1)S(1)}, bf16[2,16,1024]{2,1,0:T(8,128)(2,1)S(1)}, u32[]{:S(2)}, u32[]{:S(2)}) %collective-permute-start.3) | collective-permute-done | bytes 65568 | tf_op jit(solution)/shard_map/ppermute | solution.py:304
  12.5 2.8 %collective-permute-done.2 = bf16[2,16,1024]{2,1,0:T(8,128)(2,1)S(1)} collective-permute-done((bf16[2,16,1024]{2,1,0:T(8,128)(2,1)S(1)}, bf16[2,16,1024]{2,1,0:T(8,128)(2,1)S(1)}, u32[]{:S(2)}, u32[]{:S(2)}) %collective-permute-start.2) | collective-permute-done | bytes 65568 | tf_op jit(solution)/shard_map/ppermute | solution.py:304
  17.0 3.3 %project.1.q_ref = bf16[160,128]{1,0:T(8,128)(2,1)S(1)} custom-call(f32[8,128]{1,0:T(8,128)S(1)} %early.1.after_ref, bf16[8,16,1024]{2,1,0:T(8,128)(2,1)S(1)} %bitcast.29, bf16[8,16,1024]{2,1,0:T(8,128)(2,1)S(1)} %collective-permute-done.4.far_ref, bf16[16,32]{1,0:T(8,128)(2,1)S(1)} %get-tuple-element.27.take_ref, f32[8,1,1024]{2,1,0:T(1,128)S(1)} %bitcast.31, ...), custom_call_target="tpu_custom_call" | custom-call | flops 335544320 | bytes 20971520 | tf_op jit(solution)/shard_map/project/pallas_call | solution.py:389
  21.9 2.5 %collective-permute-done.5 = bf16[160,128]{1,0:T(8,128)(2,1)S(1)} collective-permute-done((bf16[160,128]{1,0:T(8,128)(2,1)S(1)}, bf16[160,128]{1,0:T(8,128)(2,1)S(1)}, u32[]{:S(2)}, u32[]{:S(2)}) %collective-permute-start.5) | collective-permute-done | bytes 40992 | tf_op jit(solution)/shard_map/ppermute | solution.py:304
  24.4 2.2 %collective-permute-start.8 = (bf16[2,160,128]{2,1,0:T(8,128)(2,1)S(1)}, bf16[2,160,128]{2,1,0:T(8,128)(2,1)S(1)}, u32[]{:S(2)}, u32[]{:S(2)}) collective-permute-start(bf16[2,160,128]{2,1,0:T(8,128)(2,1)S(1)} %get-tuple-element.49.after_ref), channel_id=1, source_target_pairs={{0,6},{1,7},{2,4},{3,5},{4,2},{5,3},{6,0},{7,1},{8,14},{9,15},{10,... | collective-permute-start | bytes 245768 | tf_op jit(solution)/shard_map/ppermute | solution.py:304
  26.6 2.3 %collective-permute-start.6 = (bf16[2,160,128]{2,1,0:T(8,128)(2,1)S(1)}, bf16[2,160,128]{2,1,0:T(8,128)(2,1)S(1)}, u32[]{:S(2)}, u32[]{:S(2)}) collective-permute-start(bf16[2,160,128]{2,1,0:T(8,128)(2,1)S(1)} %get-tuple-element.49.after_ref), channel_id=1, source_target_pairs={{0,2},{1,3},{2,0},{3,1},{4,6},{5,7},{6,4},{7,5},{8,10},{9,11},{10,... | collective-permute-start | bytes 245768 | tf_op jit(solution)/shard_map/ppermute | solution.py:304
  28.9 2.3 %reward.1.reward_ref = f32[8,8,128]{2,1,0:T(8,128)S(1)} custom-call(bf16[2,160,128]{2,1,0:T(8,128)(2,1)S(1)} %get-tuple-element.49.after_ref, bf16[8,256,1024]{2,1,0:T(8,128)(2,1)S(1)} %copy-done, f32[1,1024]{1,0:T(1,128)S(1)} %bitcast.32, f32[1,1024]{1,0:T(1,128)S(1)} %bitcast.33), custom_call_target="tpu_custom_call" | custom-call | flops 8388608 | bytes 4194304 | tf_op jit(solution)/shard_map/reward/pallas_call | solution.py:409
  31.3 2.8 %collective-permute-done.7 = bf16[2,160,128]{2,1,0:T(8,128)(2,1)S(1)} collective-permute-done((bf16[2,160,128]{2,1,0:T(8,128)(2,1)S(1)}, bf16[2,160,128]{2,1,0:T(8,128)(2,1)S(1)}, u32[]{:S(2)}, u32[]{:S(2)}) %collective-permute-start.7) | collective-permute-done | bytes 81952 | tf_op jit(solution)/shard_map/ppermute | solution.py:304
  34.2 2.9 %attend.1 = (f32[144,128]{1,0:T(8,128)S(1)}, f32[144,128]{1,0:T(8,128)S(1)}, f32[144,128]{1,0:T(8,128)S(1)}, f32[144,128]{1,0:T(8,128)S(1)}, f32[144,128]{1,0:T(...) custom-call(s32[8]{0:T(128)S(1)} %get-tuple-element.28.meta_ref, ...), custom_call_target="tpu_custom_call" | custom-call | flops 1073741824 | bytes 4194304 | tf_op jit(solution)/shard_map/attend/pallas_call | solution.py:455
  38.7 2.0 %collective-permute-start.11 = (f32[144,128]{1,0:T(8,128)S(1)}, f32[144,128]{1,0:T(8,128)S(1)}, u32[]{:S(2)}, u32[]{:S(2)}) collective-permute-start(f32[144,128]{1,0:T(8,128)S(1)} %get-tuple-element.32), channel_id=1, source_target_pairs={{0,3},{1,2},{2,1},{3,0},{4,7},{5,6},{6,5},{7,4},{8,11},{9,10},{10,... | collective-permute-start | bytes 221192 | tf_op jit(solution)/shard_map/ppermute | solution.py:304
  41.4 3.1 %collective-permute-start.13 = (f32[144,128]{1,0:T(8,128)S(1)}, f32[144,128]{1,0:T(8,128)S(1)}, u32[]{:S(2)}, u32[]{:S(2)}) collective-permute-start(f32[144,128]{1,0:T(8,128)S(1)} %get-tuple-element.34), channel_id=1, source_target_pairs={{0,5},{1,4},{2,7},{3,6},{4,1},{5,0},{6,3},{7,2},{8,13},{9,12},{10,... | collective-permute-start | bytes 221192 | tf_op jit(solution)/shard_map/ppermute | solution.py:304
  44.6 2.1 %collective-permute-start.14 = (f32[144,128]{1,0:T(8,128)S(1)}, f32[144,128]{1,0:T(8,128)S(1)}, u32[]{:S(2)}, u32[]{:S(2)}) collective-permute-start(f32[144,128]{1,0:T(8,128)S(1)} %get-tuple-element.35), channel_id=1, source_target_pairs={{0,6},{1,7},{2,4},{3,5},{4,2},{5,3},{6,0},{7,1},{8,14},{9,15},{10,... | collective-permute-start | bytes 221192 | tf_op jit(solution)/shard_map/ppermute | solution.py:304
  48.4 3.1 %collective-permute-done.12.rest_4_ = f32[144,128]{1,0:T(8,128)S(1)} collective-permute-done((f32[144,128]{1,0:T(8,128)S(1)}, f32[144,128]{1,0:T(8,128)S(1)}, u32[]{:S(2)}, u32[]{:S(2)}) %collective-permute-start.12) | collective-permute-done | bytes 73760 | tf_op jit(solution)/shard_map/ppermute | solution.py:304
  51.4 2.7 %collective-permute-done.13.rest_5_ = f32[144,128]{1,0:T(8,128)S(1)} collective-permute-done((f32[144,128]{1,0:T(8,128)S(1)}, f32[144,128]{1,0:T(8,128)S(1)}, u32[]{:S(2)}, u32[]{:S(2)}) %collective-permute-start.13) | collective-permute-done | bytes 73760 | tf_op jit(solution)/shard_map/ppermute | solution.py:304
  54.2 3.0 %merge.1 = (f32[136,128]{1,0:T(8,128)S(1)}, f32[136,128]{1,0:T(8,128)S(1)}, f32[136,128]{1,0:T(8,128)S(1)}, f32[136,128]{1,0:T(8,128)S(1)}, f32[136,128]{1,0:T(8...) custom-call(bf16[160,128]{1,0:T(8,128)(2,1)S(1)} %project.1.q_ref, ...), custom_call_target="tpu_custom_call" | custom-call | flops 268435456 | bytes 16777216 | tf_op jit(solution)/shard_map/merge/pallas_call | solution.py:488
  58.3 2.1 %collective-permute-start.17 = (f32[136,128]{1,0:T(8,128)S(1)}, f32[136,128]{1,0:T(8,128)S(1)}, u32[]{:S(2)}, u32[]{:S(2)}) collective-permute-start(f32[136,128]{1,0:T(8,128)S(1)} %get-tuple-element.39), channel_id=1, source_target_pairs={{0,2},{1,3},{2,0},{3,1},{4,6},{5,7},{6,4},{7,5},{8,10},{9,11},{10,... | collective-permute-start | bytes 208904 | tf_op jit(solution)/shard_map/ppermute | solution.py:304
  61.4 2.2 %collective-permute-start.19 = (f32[136,128]{1,0:T(8,128)S(1)}, f32[136,128]{1,0:T(8,128)S(1)}, u32[]{:S(2)}, u32[]{:S(2)}) collective-permute-start(f32[136,128]{1,0:T(8,128)S(1)} %get-tuple-element.41), channel_id=1, source_target_pairs={{0,4},{1,5},{2,6},{3,7},{4,0},{5,1},{6,2},{7,3},{8,12},{9,13},{10,... | collective-permute-start | bytes 208904 | tf_op jit(solution)/shard_map/ppermute | solution.py:304
  64.3 1.9 %collective-permute-start.21 = (f32[136,128]{1,0:T(8,128)S(1)}, f32[136,128]{1,0:T(8,128)S(1)}, u32[]{:S(2)}, u32[]{:S(2)}) collective-permute-start(f32[136,128]{1,0:T(8,128)S(1)} %get-tuple-element.43), channel_id=1, source_target_pairs={{0,6},{1,7},{2,4},{3,5},{4,2},{5,3},{6,0},{7,1},{8,14},{9,15},{10,... | collective-permute-start | bytes 208904 | tf_op jit(solution)/shard_map/ppermute | solution.py:304
  66.2 2.8 %collective-permute-start.22 = (f32[136,128]{1,0:T(8,128)S(1)}, f32[136,128]{1,0:T(8,128)S(1)}, u32[]{:S(2)}, u32[]{:S(2)}) collective-permute-start(f32[136,128]{1,0:T(8,128)S(1)} %get-tuple-element.44), channel_id=1, source_target_pairs={{0,7},{1,6},{2,5},{3,4},{4,3},{5,2},{6,1},{7,0},{8,15},{9,14},{10,... | collective-permute-start | bytes 208904 | tf_op jit(solution)/shard_map/ppermute | solution.py:304
  69.1 2.8 %collective-permute-done.19.refs_4_ = f32[136,128]{1,0:T(8,128)S(1)} collective-permute-done((f32[136,128]{1,0:T(8,128)S(1)}, f32[136,128]{1,0:T(8,128)S(1)}, u32[]{:S(2)}, u32[]{:S(2)}) %collective-permute-start.19) | collective-permute-done | bytes 69664 | tf_op jit(solution)/shard_map/ppermute | solution.py:304
  71.8 1.9 %collective-permute-done.20.refs_5_ = f32[136,128]{1,0:T(8,128)S(1)} collective-permute-done((f32[136,128]{1,0:T(8,128)S(1)}, f32[136,128]{1,0:T(8,128)S(1)}, u32[]{:S(2)}, u32[]{:S(2)}) %collective-permute-start.20) | collective-permute-done | bytes 69664 | tf_op jit(solution)/shard_map/ppermute | solution.py:304
  (75 shorter events, 12.9 us)
Async XLA Ops:
  0.7 5.2 %collective-permute-start = (bf16[16,1024]{1,0:T(8,128)(2,1)}, bf16[16,1024]{1,0:T(8,128)(2,1)S(1)}, u32[]{:S(2)}, u32[]{:S(2)}) collective-permute-start(bf16[16,1024]{1,0:T(8,128)(2,1)} %bitcast.42), channel_id=1, source_target_pairs={{0,1},{1,0},{2,3},{3,2},{4,5},{5,4},{6,7},{7,6},{8,9},{9,8},{10,11... | collective-permute-start | bytes 98312 | tf_op jit(solution)/shard_map/ppermute | solution.py:304
  5.9 6.6 %collective-permute-start.3 = (bf16[2,16,1024]{2,1,0:T(8,128)(2,1)S(1)}, bf16[2,16,1024]{2,1,0:T(8,128)(2,1)S(1)}, u32[]{:S(2)}, u32[]{:S(2)}) collective-permute-start(bf16[2,16,1024]{2,1,0:T(8,128)(2,1)S(1)} %pad_maximum_fusion.3), channel_id=1, source_target_pairs={{0,6},{1,7},{2,4},{3,5},{4,2},{5,3},{6,0},{7,1},{8,14},{9,15},{10,... | collective-permute-start | bytes 196616 | tf_op jit(solution)/shard_map/ppermute | solution.py:304
  10.1 5.2 %collective-permute-start.2 = (bf16[2,16,1024]{2,1,0:T(8,128)(2,1)S(1)}, bf16[2,16,1024]{2,1,0:T(8,128)(2,1)S(1)}, u32[]{:S(2)}, u32[]{:S(2)}) collective-permute-start(bf16[2,16,1024]{2,1,0:T(8,128)(2,1)S(1)} %pad_maximum_fusion.3), channel_id=1, source_target_pairs={{0,4},{1,5},{2,6},{3,7},{4,0},{5,1},{6,2},{7,3},{8,12},{9,13},{10,... | collective-permute-start | bytes 196616 | tf_op jit(solution)/shard_map/ppermute | solution.py:304
  10.1 5.2 %collective-permute-start.1 = (bf16[2,16,1024]{2,1,0:T(8,128)(2,1)S(1)}, bf16[2,16,1024]{2,1,0:T(8,128)(2,1)S(1)}, u32[]{:S(2)}, u32[]{:S(2)}) collective-permute-start(bf16[2,16,1024]{2,1,0:T(8,128)(2,1)S(1)} %pad_maximum_fusion.3), channel_id=1, source_target_pairs={{0,2},{1,3},{2,0},{3,1},{4,6},{5,7},{6,4},{7,5},{8,10},{9,11},{10,... | collective-permute-start | bytes 196616 | tf_op jit(solution)/shard_map/ppermute | solution.py:304
  15.3 1.6 %collective-permute-start.4 = (bf16[8,16,1024]{2,1,0:T(8,128)(2,1)S(1)}, bf16[8,16,1024]{2,1,0:T(8,128)(2,1)S(1)}, u32[]{:S(2)}, u32[]{:S(2)}) collective-permute-start(bf16[8,16,1024]{2,1,0:T(8,128)(2,1)S(1)} %bitcast.28), channel_id=1, source_target_pairs={{0,8},{8,0},{1,9},{9,1},{2,10},{10,2},{3,11},{11,3},{4,12},{12,4},... | collective-permute-start | bytes 786440 | tf_op jit(solution)/shard_map/ppermute | solution.py:385
  20.3 4.1 %collective-permute-start.5 = (bf16[160,128]{1,0:T(8,128)(2,1)S(1)}, bf16[160,128]{1,0:T(8,128)(2,1)S(1)}, u32[]{:S(2)}, u32[]{:S(2)}) collective-permute-start(bf16[160,128]{1,0:T(8,128)(2,1)S(1)} %project.1.q_ref), channel_id=1, source_target_pairs={{0,1},{1,0},{2,3},{3,2},{4,5},{5,4},{6,7},{7,6},{8,9},{9,8},{10,11... | collective-permute-start | bytes 122888 | tf_op jit(solution)/shard_map/ppermute | solution.py:304
  24.4 6.9 %collective-permute-start.8 = (bf16[2,160,128]{2,1,0:T(8,128)(2,1)S(1)}, bf16[2,160,128]{2,1,0:T(8,128)(2,1)S(1)}, u32[]{:S(2)}, u32[]{:S(2)}) collective-permute-start(bf16[2,160,128]{2,1,0:T(8,128)(2,1)S(1)} %get-tuple-element.49.after_ref), channel_id=1, source_target_pairs={{0,6},{1,7},{2,4},{3,5},{4,2},{5,3},{6,0},{7,1},{8,14},{9,15},{10,... | collective-permute-start | bytes 245768 | tf_op jit(solution)/shard_map/ppermute | solution.py:304
  26.6 7.6 %collective-permute-start.7 = (bf16[2,160,128]{2,1,0:T(8,128)(2,1)S(1)}, bf16[2,160,128]{2,1,0:T(8,128)(2,1)S(1)}, u32[]{:S(2)}, u32[]{:S(2)}) collective-permute-start(bf16[2,160,128]{2,1,0:T(8,128)(2,1)S(1)} %get-tuple-element.49.after_ref), channel_id=1, source_target_pairs={{0,4},{1,5},{2,6},{3,7},{4,0},{5,1},{6,2},{7,3},{8,12},{9,13},{10,... | collective-permute-start | bytes 245768 | tf_op jit(solution)/shard_map/ppermute | solution.py:304
  26.6 7.6 %collective-permute-start.6 = (bf16[2,160,128]{2,1,0:T(8,128)(2,1)S(1)}, bf16[2,160,128]{2,1,0:T(8,128)(2,1)S(1)}, u32[]{:S(2)}, u32[]{:S(2)}) collective-permute-start(bf16[2,160,128]{2,1,0:T(8,128)(2,1)S(1)} %get-tuple-element.49.after_ref), channel_id=1, source_target_pairs={{0,2},{1,3},{2,0},{3,1},{4,6},{5,7},{6,4},{7,5},{8,10},{9,11},{10,... | collective-permute-start | bytes 245768 | tf_op jit(solution)/shard_map/ppermute | solution.py:304
  37.1 7.4 %collective-permute-start.9 = (f32[144,128]{1,0:T(8,128)S(1)}, f32[144,128]{1,0:T(8,128)S(1)}, u32[]{:S(2)}, u32[]{:S(2)}) collective-permute-start(f32[144,128]{1,0:T(8,128)S(1)} %get-tuple-element.30), channel_id=1, source_target_pairs={{0,1},{1,0},{2,3},{3,2},{4,5},{5,4},{6,7},{7,6},{8,9},{9,8},{10,11... | collective-permute-start | bytes 221192 | tf_op jit(solution)/shard_map/ppermute | solution.py:304
  38.7 8.0 %collective-permute-start.10 = (f32[144,128]{1,0:T(8,128)S(1)}, f32[144,128]{1,0:T(8,128)S(1)}, u32[]{:S(2)}, u32[]{:S(2)}) collective-permute-start(f32[144,128]{1,0:T(8,128)S(1)} %get-tuple-element.31), channel_id=1, source_target_pairs={{0,2},{1,3},{2,0},{3,1},{4,6},{5,7},{6,4},{7,5},{8,10},{9,11},{10,... | collective-permute-start | bytes 221192 | tf_op jit(solution)/shard_map/ppermute | solution.py:304
  38.7 9.6 %collective-permute-start.11 = (f32[144,128]{1,0:T(8,128)S(1)}, f32[144,128]{1,0:T(8,128)S(1)}, u32[]{:S(2)}, u32[]{:S(2)}) collective-permute-start(f32[144,128]{1,0:T(8,128)S(1)} %get-tuple-element.32), channel_id=1, source_target_pairs={{0,3},{1,2},{2,1},{3,0},{4,7},{5,6},{6,5},{7,4},{8,11},{9,10},{10,... | collective-permute-start | bytes 221192 | tf_op jit(solution)/shard_map/ppermute | solution.py:304
  40.7 10.7 %collective-permute-start.12 = (f32[144,128]{1,0:T(8,128)S(1)}, f32[144,128]{1,0:T(8,128)S(1)}, u32[]{:S(2)}, u32[]{:S(2)}) collective-permute-start(f32[144,128]{1,0:T(8,128)S(1)} %get-tuple-element.33), channel_id=1, source_target_pairs={{0,4},{1,5},{2,6},{3,7},{4,0},{5,1},{6,2},{7,3},{8,12},{9,13},{10,... | collective-permute-start | bytes 221192 | tf_op jit(solution)/shard_map/ppermute | solution.py:304
  41.4 12.7 %collective-permute-start.13 = (f32[144,128]{1,0:T(8,128)S(1)}, f32[144,128]{1,0:T(8,128)S(1)}, u32[]{:S(2)}, u32[]{:S(2)}) collective-permute-start(f32[144,128]{1,0:T(8,128)S(1)} %get-tuple-element.34), channel_id=1, source_target_pairs={{0,5},{1,4},{2,7},{3,6},{4,1},{5,0},{6,3},{7,2},{8,13},{9,12},{10,... | collective-permute-start | bytes 221192 | tf_op jit(solution)/shard_map/ppermute | solution.py:304
  44.6 9.5 %collective-permute-start.14 = (f32[144,128]{1,0:T(8,128)S(1)}, f32[144,128]{1,0:T(8,128)S(1)}, u32[]{:S(2)}, u32[]{:S(2)}) collective-permute-start(f32[144,128]{1,0:T(8,128)S(1)} %get-tuple-element.35), channel_id=1, source_target_pairs={{0,6},{1,7},{2,4},{3,5},{4,2},{5,3},{6,0},{7,1},{8,14},{9,15},{10,... | collective-permute-start | bytes 221192 | tf_op jit(solution)/shard_map/ppermute | solution.py:304
  46.7 7.4 %collective-permute-start.15 = (f32[144,128]{1,0:T(8,128)S(1)}, f32[144,128]{1,0:T(8,128)S(1)}, u32[]{:S(2)}, u32[]{:S(2)}) collective-permute-start(f32[144,128]{1,0:T(8,128)S(1)} %get-tuple-element.36), channel_id=1, source_target_pairs={{0,7},{1,6},{2,5},{3,4},{4,3},{5,2},{6,1},{7,0},{8,15},{9,14},{10,... | collective-permute-start | bytes 221192 | tf_op jit(solution)/shard_map/ppermute | solution.py:304
  57.2 7.2 %collective-permute-start.16 = (f32[136,128]{1,0:T(8,128)S(1)}, f32[136,128]{1,0:T(8,128)S(1)}, u32[]{:S(2)}, u32[]{:S(2)}) collective-permute-start(f32[136,128]{1,0:T(8,128)S(1)} %get-tuple-element.38), channel_id=1, source_target_pairs={{0,1},{1,0},{2,3},{3,2},{4,5},{5,4},{6,7},{7,6},{8,9},{9,8},{10,11... | collective-permute-start | bytes 208904 | tf_op jit(solution)/shard_map/ppermute | solution.py:304
  58.3 7.9 %collective-permute-start.17 = (f32[136,128]{1,0:T(8,128)S(1)}, f32[136,128]{1,0:T(8,128)S(1)}, u32[]{:S(2)}, u32[]{:S(2)}) collective-permute-start(f32[136,128]{1,0:T(8,128)S(1)} %get-tuple-element.39), channel_id=1, source_target_pairs={{0,2},{1,3},{2,0},{3,1},{4,6},{5,7},{6,4},{7,5},{8,10},{9,11},{10,... | collective-permute-start | bytes 208904 | tf_op jit(solution)/shard_map/ppermute | solution.py:304
  60.4 8.6 %collective-permute-start.18 = (f32[136,128]{1,0:T(8,128)S(1)}, f32[136,128]{1,0:T(8,128)S(1)}, u32[]{:S(2)}, u32[]{:S(2)}) collective-permute-start(f32[136,128]{1,0:T(8,128)S(1)} %get-tuple-element.40), channel_id=1, source_target_pairs={{0,3},{1,2},{2,1},{3,0},{4,7},{5,6},{6,5},{7,4},{8,11},{9,10},{10,... | collective-permute-start | bytes 208904 | tf_op jit(solution)/shard_map/ppermute | solution.py:304
  61.4 10.4 %collective-permute-start.19 = (f32[136,128]{1,0:T(8,128)S(1)}, f32[136,128]{1,0:T(8,128)S(1)}, u32[]{:S(2)}, u32[]{:S(2)}) collective-permute-start(f32[136,128]{1,0:T(8,128)S(1)} %get-tuple-element.41), channel_id=1, source_target_pairs={{0,4},{1,5},{2,6},{3,7},{4,0},{5,1},{6,2},{7,3},{8,12},{9,13},{10,... | collective-permute-start | bytes 208904 | tf_op jit(solution)/shard_map/ppermute | solution.py:304
  63.6 10.1 %collective-permute-start.20 = (f32[136,128]{1,0:T(8,128)S(1)}, f32[136,128]{1,0:T(8,128)S(1)}, u32[]{:S(2)}, u32[]{:S(2)}) collective-permute-start(f32[136,128]{1,0:T(8,128)S(1)} %get-tuple-element.42), channel_id=1, source_target_pairs={{0,5},{1,4},{2,7},{3,6},{4,1},{5,0},{6,3},{7,2},{8,13},{9,12},{10,... | collective-permute-start | bytes 208904 | tf_op jit(solution)/shard_map/ppermute | solution.py:304
  64.3 9.4 %collective-permute-start.21 = (f32[136,128]{1,0:T(8,128)S(1)}, f32[136,128]{1,0:T(8,128)S(1)}, u32[]{:S(2)}, u32[]{:S(2)}) collective-permute-start(f32[136,128]{1,0:T(8,128)S(1)} %get-tuple-element.43), channel_id=1, source_target_pairs={{0,6},{1,7},{2,4},{3,5},{4,2},{5,3},{6,0},{7,1},{8,14},{9,15},{10,... | collective-permute-start | bytes 208904 | tf_op jit(solution)/shard_map/ppermute | solution.py:304
  66.2 7.5 %collective-permute-start.22 = (f32[136,128]{1,0:T(8,128)S(1)}, f32[136,128]{1,0:T(8,128)S(1)}, u32[]{:S(2)}, u32[]{:S(2)}) collective-permute-start(f32[136,128]{1,0:T(8,128)S(1)} %get-tuple-element.44), channel_id=1, source_target_pairs={{0,7},{1,6},{2,5},{3,4},{4,3},{5,2},{6,1},{7,0},{8,15},{9,14},{10,... | collective-permute-start | bytes 208904 | tf_op jit(solution)/shard_map/ppermute | solution.py:304
  73.8 1.3 %collective-permute-start.23 = (bf16[16,1024]{1,0:T(8,128)(2,1)S(1)}, bf16[16,1024]{1,0:T(8,128)(2,1)S(1)}, u32[]{:S(2)}, u32[]{:S(2)}) collective-permute-start(bf16[16,1024]{1,0:T(8,128)(2,1)S(1)} %get-tuple-element.47), channel_id=1, source_target_pairs={{0,8},{8,0},{1,9},{9,1},{2,10},{10,2},{3,11},{11,3},{4,12},{12,4},... | collective-permute-start | bytes 98312 | tf_op jit(solution)/shard_map/ppermute | solution.py:515
  (18 other events, 330.3 us)

commit v7 on v6

--- a/solution.py
+++ b/solution.py
@@ -111,11 +111,11 @@
             if len(out_ref.shape) == 2:
                 out_ref[half * slots + s] = sums
                 continue
-            for c in range(EXT // 2):
+            for c in range(EXT // 4):
                 piece = jnp.zeros((LANES,), jnp.float32)
                 if c < sums.shape[0] // LANES:
                     piece = sums[c * LANES : (c + 1) * LANES]
-                out_ref[s, half * (EXT // 2) + c] = piece
+                out_ref[s, half * (EXT // 4) + c] = piece
 
 
 def project_kernel(pages, per_page, width, after_ref, own_ref, far_ref, take_ref, gain_ref, wq_ref, wkv_ref, out_ref, tokens):
@@ -159,6 +159,7 @@
     first = lax.axis_index("tensor") * width
     me = lax.axis_index("tensor") if len(outs) > 1 else 0
     spread[...] = jnp.zeros_like(spread)
+    stats = [[jnp.zeros((1, LANES), jnp.float32)] * 2 for _ in range(KVH)]
     for i in range(pages):
         for r in range(KVH):
             spread[r * page_rows : (r + 1) * page_rows, aligned(me ^ r, HD)] = q_ref[
@@ -170,20 +171,35 @@
         top = jnp.max(scores, axis=0, keepdims=True)
         expo = jnp.where(valid, jnp.exp(scores - top), 0.0)
         total = jnp.sum(expo, axis=0, keepdims=True)
-        product[...] = dot(expo.astype(jnp.bfloat16), v_ref[meta_ref[i]], TN)
+        weights = expo.astype(jnp.bfloat16)
+        rows = 2 * page_rows
+        for pair in range(KVH // 2):
+            values = v_ref[meta_ref[i], :, aligned(pair ^ lax.div(me, 2), 2 * HD)]
+            product[pair * rows : (pair + 1) * rows] = dot(
+                weights[:, pair * rows : (pair + 1) * rows], values, TN
+            )
         for r in range(KVH):
             out = outs[r] if len(outs) > 1 else outs[0].at[r]
             out[i * page_rows : (i + 1) * page_rows, :] = product[
-                r * page_rows : (r + 1) * page_rows, aligned(me ^ r, HD)
+                r * page_rows : (r + 1) * page_rows, aligned((me ^ r) & 1, HD)
             ]
-            lane = (r * page_rows) // LANES * LANES
-            out[body + i : body + i + 1, :] = top[:, lane : lane + LANES]
-            out[body + pages + i : body + pages + i + 1, :] = total[:, lane : lane + LANES]
+            start = r * page_rows
+            lane = start // LANES * LANES
+            shift = (i * page_rows - start) % LANES
+            mask = iota((1, LANES), 1) // page_rows == i
+            for k, packed in enumerate((top, total)):
+                packed = packed[:, lane : lane + LANES]
+                if shift:
+                    packed = pltpu.roll(packed, shift, 1)
+                stats[r][k] = jnp.where(mask, packed, stats[r][k])
     for r in range(KVH):
+        out = outs[r] if len(outs) > 1 else outs[0].at[r]
+        out[body : body + 2, :] = jnp.concatenate(stats[r], axis=0)
         if len(outs) > 1:
-            outs[r][body + EXT :, :] = reward_ref[me ^ r]
+            out[body + 2 : body + 4, :] = jnp.zeros((2, LANES), jnp.float32)
+            out[body + 4 :, :] = reward_ref[me ^ r]
         else:
-            outs[0][r, body + EXT :, :] = jnp.zeros((EXT, LANES), jnp.float32)
+            out[body + 2 :, :] = jnp.zeros((EXT - 2, LANES), jnp.float32)
 
 
 def merge_kernel(pages, per_page, width, span, slots, chunks, q_ref, gathered_ref, w_ref, *rest):
@@ -192,7 +208,7 @@
     parts = rest[:chunks] if split else [rest[0].at[b] for b in range(chunks)]
     outs = rest[chunks:-1] if split else rest[1:-1]
     me = lax.axis_index("tensor")
-    body = parts[0].shape[0] - 2 * EXT
+    body = parts[0].shape[0] - EXT
     page_rows = body // pages
     heads = page_rows // per_page
     rows = pages * per_page
@@ -221,35 +237,17 @@
     recent_total = jnp.sum(recent_exp, axis=-1, keepdims=True)
     recent_acc = dot(recent_exp.astype(jnp.bfloat16), fresh_v)
 
-    extras = []
-    for b in range(chunks):
-        extra = parts[b][body : body + EXT, :]
-        if split:
-            shift = -(b * page_rows) % LANES
-            extras.append(pltpu.roll(extra, shift, 1) if shift else extra)
-        else:
-            shift = lax.rem(LANES - lax.rem(me * page_rows, LANES), LANES)
-            extras.append(pltpu.roll(extra, shift, 1))
-    maxima = [extra[:pages] for extra in extras]
-    totals = [extra[pages : 2 * pages] for extra in extras]
+    maxima = [parts[b][body : body + 1, :] for b in range(chunks)]
+    totals = [parts[b][body + 1 : body + 2, :] for b in range(chunks)]
     top = functools.reduce(jnp.maximum, maxima)
     factors = [jnp.exp(m - top) for m in maxima]
     total = functools.reduce(jnp.add, [f * t for f, t in zip(factors, totals)])
 
-    pick = iota((page_rows, LANES), 0) == iota((page_rows, LANES), 1)
+    pick = iota((body, LANES), 0) == iota((body, LANES), 1)
 
     def column(packed):
-        return jnp.concatenate(
-            [
-                jnp.sum(
-                    jnp.where(pick, jnp.broadcast_to(packed[i : i + 1], pick.shape), 0.0),
-                    axis=-1,
-                    keepdims=True,
-                )
-                for i in range(pages)
-            ],
-            axis=0,
-        )
+        wide = jnp.where(pick, jnp.broadcast_to(packed, pick.shape), 0.0)
+        return jnp.sum(wide, axis=-1, keepdims=True)
 
     acc = jnp.zeros((body, HD), jnp.float32)
     for b in range(chunks):
@@ -266,8 +264,8 @@
     for h in range(heads):
         att[:, h * HD : (h + 1) * HD] = attended[h * rows : (h + 1) * rows]
 
-    tile = functools.reduce(jnp.add, [parts[b][body + EXT :, :] for b in range(chunks)])
-    used = EXT // 2
+    tile = functools.reduce(jnp.add, [parts[b][body + EXT // 2 :, :] for b in range(chunks)])
+    used = EXT // 4
     value = tile[used:] * lax.rsqrt(tile[:used] / width + EPS)
     mean = jnp.sum(value, keepdims=True) / span
     own = lax.div(me * (slots * span // chunks), span)
@@ -405,13 +403,13 @@
     gathered, after = spread_all(packed, chunks, index)
 
     span = reward_hidden.shape[1]
-    tiled = direct and slots == chunks
+    tiled = direct and slots == chunks and span <= EXT // 4 * LANES
     reward_parts = pl.pallas_call(
         reward_kernel,
         in_specs=[ANY, ANY, VMEM, VMEM] + [ANY] * 0,
         out_specs=VMEM,
         out_shape=jax.ShapeDtypeStruct(
-            (slots, EXT, LANES) if tiled else (2 * slots, span), jnp.float32
+            (slots, EXT // 2, LANES) if tiled else (2 * slots, span), jnp.float32
         ),
         scratch_shapes=[
             pltpu.VMEM(reward_hidden.shape, reward_hidden.dtype),
@@ -428,9 +426,9 @@
 
     def tile(values):
         values = values.reshape(chunks, -1)
-        size = EXT // 2 * LANES
+        size = EXT // 4 * LANES
         return jnp.pad(values, ((0, 0), (0, size - values.shape[1]))).reshape(
-            chunks, EXT // 2, LANES
+            chunks, EXT // 4, LANES
         )
 
     if not tiled:
@@ -451,7 +449,7 @@
         )
 
     big = pages * page_rows
-    block = (big + 2 * EXT, HD)
+    block = (big + EXT, HD)
     attended = pl.pallas_call(
         functools.partial(attend_kernel, pages, page_rows),
         in_specs=[SMEM] + [VMEM] * 4,
@@ -463,7 +461,7 @@
         ),
         scratch_shapes=[
             pltpu.VMEM((KVH * page_rows, KVH * HD), jnp.bfloat16),
-            pltpu.VMEM((KVH * page_rows, KVH * HD), jnp.float32),
+            pltpu.VMEM((KVH * page_rows, 2 * HD), jnp.float32),
         ],
         compiler_params=pltpu.CompilerParams(vmem_limit_bytes=6 * MIB),
         cost_estimate=pl.CostEstimate(
@@ -480,7 +478,9 @@
             .transpose(0, 2, 1, 3, 4)
             .reshape(chunks, body, HD)
         )
-        extra = jnp.repeat(attended[0][:, big : big + EXT], split, axis=0)
+        extra = attended[0][:, big : big + 2].reshape(KVH, 2, pages, split, heads * per_page)
+        extra = extra.transpose(0, 3, 1, 2, 4).reshape(chunks, 2, body)
+        extra = jnp.pad(extra, ((0, 0), (0, 2), (0, LANES - body)))
         attended = [jnp.concatenate([acc, extra, reward_parts], axis=1)]
     parts = trade(attended, chunks)
 

time: 76 us -> 75.4 us (level)
  transfers between devices with their start and end apart: 24 -> 24, of which waited for: 12 -> 13; matrix products, arithmetic and copies ran while one was open for 1% -> 1% of each run, Pallas kernels for 5% -> 5%
where the time goes in v7:
time: 75.4 us; the launch traced here: 75.2 us
  starting transfers between devices  36.7 us (49%)
  waiting for transfers between devices  23 us (31%)
  Pallas kernels  12.9 us (17%)
  between operations  0.94 us (1%)
    ppermute x22, starting transfers between devices, partner(): return lax.ppermute(x, 'tensor', [(i, i ^ bits) for i in range(chunks)])  36.6 us
    ppermute x22, waiting for transfers between devices, partner(): return lax.ppermute(x, 'tensor', [(i, i ^ bits) for i in range(chunks)])  22.3 us
    pallas_call x1, Pallas kernels, local(): pl.pallas_call(functools.partial(project_kernel, pages, per_page, depth),...  3.28 us
    pallas_call x1, Pallas kernels, local(): pl.pallas_call(functools.partial(attend_kernel, pages, page_rows), in_spe...  3.21 us
    pallas_call x1, Pallas kernels, local(): pl.pallas_call(functools.partial(merge_kernel, pages, per_page, depth, sp...  2.76 us
    pallas_call x1, Pallas kernels, local(): pl.pallas_call(reward_kernel, in_specs=[ANY, ANY, VMEM, VMEM] + [ANY] * 0...  2.31 us
  transfers between devices with their start and end apart: 24, of which 13 were waited for; matrix products, arithmetic and copies ran while one was open for 1% of the time, Pallas kernels for 5%

profile of v7, /device:TPU:0, one launch (start us, length us, event | category | flops | bytes accessed | tf_op | source)
XLA Modules:
  0.0 75.2 jit_solution(11495510394640940477)
XLA Ops:
  0.7 3.1 %collective-permute-start = (bf16[16,1024]{1,0:T(8,128)(2,1)}, bf16[16,1024]{1,0:T(8,128)(2,1)S(1)}, u32[]{:S(2)}, u32[]{:S(2)}) collective-permute-start(bf16[16,1024]{1,0:T(8,128)(2,1)} %bitcast.42), channel_id=1, source_target_pairs={{0,1},{1,0},{2,3},{3,2},{4,5},{5,4},{6,7},{7,6},{8,9},{9,8},{10,11... | collective-permute-start | bytes 98312 | tf_op jit(solution)/shard_map/ppermute | solution.py:302
  3.8 2.1 %collective-permute-done = bf16[16,1024]{1,0:T(8,128)(2,1)S(1)} collective-permute-done((bf16[16,1024]{1,0:T(8,128)(2,1)}, bf16[16,1024]{1,0:T(8,128)(2,1)S(1)}, u32[]{:S(2)}, u32[]{:S(2)}) %collective-permute-start) | collective-permute-done | bytes 32800 | tf_op jit(solution)/shard_map/ppermute | solution.py:302
  5.9 4.2 %collective-permute-start.3 = (bf16[2,16,1024]{2,1,0:T(8,128)(2,1)S(1)}, bf16[2,16,1024]{2,1,0:T(8,128)(2,1)S(1)}, u32[]{:S(2)}, u32[]{:S(2)}) collective-permute-start(bf16[2,16,1024]{2,1,0:T(8,128)(2,1)S(1)} %pad_maximum_fusion.3), channel_id=1, source_target_pairs={{0,6},{1,7},{2,4},{3,5},{4,2},{5,3},{6,0},{7,1},{8,14},{9,15},{10,... | collective-permute-start | bytes 196616 | tf_op jit(solution)/shard_map/ppermute | solution.py:302
  10.7 1.8 %collective-permute-done.3 = bf16[2,16,1024]{2,1,0:T(8,128)(2,1)S(1)} collective-permute-done((bf16[2,16,1024]{2,1,0:T(8,128)(2,1)S(1)}, bf16[2,16,1024]{2,1,0:T(8,128)(2,1)S(1)}, u32[]{:S(2)}, u32[]{:S(2)}) %collective-permute-start.3) | collective-permute-done | bytes 65568 | tf_op jit(solution)/shard_map/ppermute | solution.py:302
  12.5 2.8 %collective-permute-done.2 = bf16[2,16,1024]{2,1,0:T(8,128)(2,1)S(1)} collective-permute-done((bf16[2,16,1024]{2,1,0:T(8,128)(2,1)S(1)}, bf16[2,16,1024]{2,1,0:T(8,128)(2,1)S(1)}, u32[]{:S(2)}, u32[]{:S(2)}) %collective-permute-start.2) | collective-permute-done | bytes 65568 | tf_op jit(solution)/shard_map/ppermute | solution.py:302
  17.0 3.3 %project.1.q_ref = bf16[160,128]{1,0:T(8,128)(2,1)S(1)} custom-call(f32[8,128]{1,0:T(8,128)S(1)} %early.1.after_ref, bf16[8,16,1024]{2,1,0:T(8,128)(2,1)S(1)} %bitcast.29, bf16[8,16,1024]{2,1,0:T(8,128)(2,1)S(1)} %collective-permute-done.4.far_ref, bf16[16,32]{1,0:T(8,128)(2,1)S(1)} %get-tuple-element.27.take_ref, f32[8,1,1024]{2,1,0:T(1,128)S(1)} %bitcast.31, ...), custom_call_target="tpu_custom_call" | custom-call | flops 335544320 | bytes 20971520 | tf_op jit(solution)/shard_map/project/pallas_call | solution.py:387
  21.9 2.5 %collective-permute-done.5 = bf16[160,128]{1,0:T(8,128)(2,1)S(1)} collective-permute-done((bf16[160,128]{1,0:T(8,128)(2,1)S(1)}, bf16[160,128]{1,0:T(8,128)(2,1)S(1)}, u32[]{:S(2)}, u32[]{:S(2)}) %collective-permute-start.5) | collective-permute-done | bytes 40992 | tf_op jit(solution)/shard_map/ppermute | solution.py:302
  24.4 2.2 %collective-permute-start.8 = (bf16[2,160,128]{2,1,0:T(8,128)(2,1)S(1)}, bf16[2,160,128]{2,1,0:T(8,128)(2,1)S(1)}, u32[]{:S(2)}, u32[]{:S(2)}) collective-permute-start(bf16[2,160,128]{2,1,0:T(8,128)(2,1)S(1)} %get-tuple-element.49.after_ref), channel_id=1, source_target_pairs={{0,6},{1,7},{2,4},{3,5},{4,2},{5,3},{6,0},{7,1},{8,14},{9,15},{10,... | collective-permute-start | bytes 245768 | tf_op jit(solution)/shard_map/ppermute | solution.py:302
  26.6 2.3 %collective-permute-start.6 = (bf16[2,160,128]{2,1,0:T(8,128)(2,1)S(1)}, bf16[2,160,128]{2,1,0:T(8,128)(2,1)S(1)}, u32[]{:S(2)}, u32[]{:S(2)}) collective-permute-start(bf16[2,160,128]{2,1,0:T(8,128)(2,1)S(1)} %get-tuple-element.49.after_ref), channel_id=1, source_target_pairs={{0,2},{1,3},{2,0},{3,1},{4,6},{5,7},{6,4},{7,5},{8,10},{9,11},{10,... | collective-permute-start | bytes 245768 | tf_op jit(solution)/shard_map/ppermute | solution.py:302
  28.9 2.3 %reward.1.reward_ref = f32[8,4,128]{2,1,0:T(4,128)S(1)} custom-call(bf16[2,160,128]{2,1,0:T(8,128)(2,1)S(1)} %get-tuple-element.49.after_ref, bf16[8,256,1024]{2,1,0:T(8,128)(2,1)S(1)} %copy-done, f32[1,1024]{1,0:T(1,128)S(1)} %bitcast.32, f32[1,1024]{1,0:T(1,128)S(1)} %bitcast.33), custom_call_target="tpu_custom_call" | custom-call | flops 8388608 | bytes 4194304 | tf_op jit(solution)/shard_map/reward/pallas_call | solution.py:407
  31.3 2.8 %collective-permute-done.7 = bf16[2,160,128]{2,1,0:T(8,128)(2,1)S(1)} collective-permute-done((bf16[2,160,128]{2,1,0:T(8,128)(2,1)S(1)}, bf16[2,160,128]{2,1,0:T(8,128)(2,1)S(1)}, u32[]{:S(2)}, u32[]{:S(2)}) %collective-permute-start.7) | collective-permute-done | bytes 81952 | tf_op jit(solution)/shard_map/ppermute | solution.py:302
  34.2 3.2 %attend.1 = (f32[136,128]{1,0:T(8,128)S(1)}, f32[136,128]{1,0:T(8,128)S(1)}, f32[136,128]{1,0:T(8,128)S(1)}, f32[136,128]{1,0:T(8,128)S(1)}, f32[136,128]{1,0:T(...) custom-call(s32[8]{0:T(128)S(1)} %get-tuple-element.28.meta_ref, ...), custom_call_target="tpu_custom_call" | custom-call | flops 1073741824 | bytes 4194304 | tf_op jit(solution)/shard_map/attend/pallas_call | solution.py:453
  39.0 2.0 %collective-permute-start.11 = (f32[136,128]{1,0:T(8,128)S(1)}, f32[136,128]{1,0:T(8,128)S(1)}, u32[]{:S(2)}, u32[]{:S(2)}) collective-permute-start(f32[136,128]{1,0:T(8,128)S(1)} %get-tuple-element.32), channel_id=1, source_target_pairs={{0,3},{1,2},{2,1},{3,0},{4,7},{5,6},{6,5},{7,4},{8,11},{9,10},{10,... | collective-permute-start | bytes 208904 | tf_op jit(solution)/shard_map/ppermute | solution.py:302
  41.7 3.1 %collective-permute-start.13 = (f32[136,128]{1,0:T(8,128)S(1)}, f32[136,128]{1,0:T(8,128)S(1)}, u32[]{:S(2)}, u32[]{:S(2)}) collective-permute-start(f32[136,128]{1,0:T(8,128)S(1)} %get-tuple-element.34), channel_id=1, source_target_pairs={{0,5},{1,4},{2,7},{3,6},{4,1},{5,0},{6,3},{7,2},{8,13},{9,12},{10,... | collective-permute-start | bytes 208904 | tf_op jit(solution)/shard_map/ppermute | solution.py:302
  44.9 2.1 %collective-permute-start.14 = (f32[136,128]{1,0:T(8,128)S(1)}, f32[136,128]{1,0:T(8,128)S(1)}, u32[]{:S(2)}, u32[]{:S(2)}) collective-permute-start(f32[136,128]{1,0:T(8,128)S(1)} %get-tuple-element.35), channel_id=1, source_target_pairs={{0,6},{1,7},{2,4},{3,5},{4,2},{5,3},{6,0},{7,1},{8,14},{9,15},{10,... | collective-permute-start | bytes 208904 | tf_op jit(solution)/shard_map/ppermute | solution.py:302
  48.7 2.7 %collective-permute-done.12.rest_4_ = f32[136,128]{1,0:T(8,128)S(1)} collective-permute-done((f32[136,128]{1,0:T(8,128)S(1)}, f32[136,128]{1,0:T(8,128)S(1)}, u32[]{:S(2)}, u32[]{:S(2)}) %collective-permute-start.12) | collective-permute-done | bytes 69664 | tf_op jit(solution)/shard_map/ppermute | solution.py:302
  51.4 1.8 %collective-permute-done.13.rest_5_ = f32[136,128]{1,0:T(8,128)S(1)} collective-permute-done((f32[136,128]{1,0:T(8,128)S(1)}, f32[136,128]{1,0:T(8,128)S(1)}, u32[]{:S(2)}, u32[]{:S(2)}) %collective-permute-start.13) | collective-permute-done | bytes 69664 | tf_op jit(solution)/shard_map/ppermute | solution.py:302
  54.2 2.8 %merge.1 = (f32[136,128]{1,0:T(8,128)S(1)}, f32[136,128]{1,0:T(8,128)S(1)}, f32[136,128]{1,0:T(8,128)S(1)}, f32[136,128]{1,0:T(8,128)S(1)}, f32[136,128]{1,0:T(8...) custom-call(bf16[160,128]{1,0:T(8,128)(2,1)S(1)} %project.1.q_ref, ...), custom_call_target="tpu_custom_call" | custom-call | flops 268435456 | bytes 16777216 | tf_op jit(solution)/shard_map/merge/pallas_call | solution.py:488
  57.7 2.0 %collective-permute-start.17 = (f32[136,128]{1,0:T(8,128)S(1)}, f32[136,128]{1,0:T(8,128)S(1)}, u32[]{:S(2)}, u32[]{:S(2)}) collective-permute-start(f32[136,128]{1,0:T(8,128)S(1)} %get-tuple-element.39), channel_id=1, source_target_pairs={{0,2},{1,3},{2,0},{3,1},{4,6},{5,7},{6,4},{7,5},{8,10},{9,11},{10,... | collective-permute-start | bytes 208904 | tf_op jit(solution)/shard_map/ppermute | solution.py:302
  60.8 2.2 %collective-permute-start.19 = (f32[136,128]{1,0:T(8,128)S(1)}, f32[136,128]{1,0:T(8,128)S(1)}, u32[]{:S(2)}, u32[]{:S(2)}) collective-permute-start(f32[136,128]{1,0:T(8,128)S(1)} %get-tuple-element.41), channel_id=1, source_target_pairs={{0,4},{1,5},{2,6},{3,7},{4,0},{5,1},{6,2},{7,3},{8,12},{9,13},{10,... | collective-permute-start | bytes 208904 | tf_op jit(solution)/shard_map/ppermute | solution.py:302
  63.7 1.9 %collective-permute-start.21 = (f32[136,128]{1,0:T(8,128)S(1)}, f32[136,128]{1,0:T(8,128)S(1)}, u32[]{:S(2)}, u32[]{:S(2)}) collective-permute-start(f32[136,128]{1,0:T(8,128)S(1)} %get-tuple-element.43), channel_id=1, source_target_pairs={{0,6},{1,7},{2,4},{3,5},{4,2},{5,3},{6,0},{7,1},{8,14},{9,15},{10,... | collective-permute-start | bytes 208904 | tf_op jit(solution)/shard_map/ppermute | solution.py:302
  65.6 2.9 %collective-permute-start.22 = (f32[136,128]{1,0:T(8,128)S(1)}, f32[136,128]{1,0:T(8,128)S(1)}, u32[]{:S(2)}, u32[]{:S(2)}) collective-permute-start(f32[136,128]{1,0:T(8,128)S(1)} %get-tuple-element.44), channel_id=1, source_target_pairs={{0,7},{1,6},{2,5},{3,4},{4,3},{5,2},{6,1},{7,0},{8,15},{9,14},{10,... | collective-permute-start | bytes 208904 | tf_op jit(solution)/shard_map/ppermute | solution.py:302
  68.4 2.8 %collective-permute-done.19.refs_4_ = f32[136,128]{1,0:T(8,128)S(1)} collective-permute-done((f32[136,128]{1,0:T(8,128)S(1)}, f32[136,128]{1,0:T(8,128)S(1)}, u32[]{:S(2)}, u32[]{:S(2)}) %collective-permute-start.19) | collective-permute-done | bytes 69664 | tf_op jit(solution)/shard_map/ppermute | solution.py:302
  71.2 1.9 %collective-permute-done.20.refs_5_ = f32[136,128]{1,0:T(8,128)S(1)} collective-permute-done((f32[136,128]{1,0:T(8,128)S(1)}, f32[136,128]{1,0:T(8,128)S(1)}, u32[]{:S(2)}, u32[]{:S(2)}) %collective-permute-start.20) | collective-permute-done | bytes 69664 | tf_op jit(solution)/shard_map/ppermute | solution.py:302
  (75 shorter events, 13.6 us)
Async XLA Ops:
  0.7 5.2 %collective-permute-start = (bf16[16,1024]{1,0:T(8,128)(2,1)}, bf16[16,1024]{1,0:T(8,128)(2,1)S(1)}, u32[]{:S(2)}, u32[]{:S(2)}) collective-permute-start(bf16[16,1024]{1,0:T(8,128)(2,1)} %bitcast.42), channel_id=1, source_target_pairs={{0,1},{1,0},{2,3},{3,2},{4,5},{5,4},{6,7},{7,6},{8,9},{9,8},{10,11... | collective-permute-start | bytes 98312 | tf_op jit(solution)/shard_map/ppermute | solution.py:302
  5.9 6.6 %collective-permute-start.3 = (bf16[2,16,1024]{2,1,0:T(8,128)(2,1)S(1)}, bf16[2,16,1024]{2,1,0:T(8,128)(2,1)S(1)}, u32[]{:S(2)}, u32[]{:S(2)}) collective-permute-start(bf16[2,16,1024]{2,1,0:T(8,128)(2,1)S(1)} %pad_maximum_fusion.3), channel_id=1, source_target_pairs={{0,6},{1,7},{2,4},{3,5},{4,2},{5,3},{6,0},{7,1},{8,14},{9,15},{10,... | collective-permute-start | bytes 196616 | tf_op jit(solution)/shard_map/ppermute | solution.py:302
  10.1 5.2 %collective-permute-start.2 = (bf16[2,16,1024]{2,1,0:T(8,128)(2,1)S(1)}, bf16[2,16,1024]{2,1,0:T(8,128)(2,1)S(1)}, u32[]{:S(2)}, u32[]{:S(2)}) collective-permute-start(bf16[2,16,1024]{2,1,0:T(8,128)(2,1)S(1)} %pad_maximum_fusion.3), channel_id=1, source_target_pairs={{0,4},{1,5},{2,6},{3,7},{4,0},{5,1},{6,2},{7,3},{8,12},{9,13},{10,... | collective-permute-start | bytes 196616 | tf_op jit(solution)/shard_map/ppermute | solution.py:302
  10.1 5.2 %collective-permute-start.1 = (bf16[2,16,1024]{2,1,0:T(8,128)(2,1)S(1)}, bf16[2,16,1024]{2,1,0:T(8,128)(2,1)S(1)}, u32[]{:S(2)}, u32[]{:S(2)}) collective-permute-start(bf16[2,16,1024]{2,1,0:T(8,128)(2,1)S(1)} %pad_maximum_fusion.3), channel_id=1, source_target_pairs={{0,2},{1,3},{2,0},{3,1},{4,6},{5,7},{6,4},{7,5},{8,10},{9,11},{10,... | collective-permute-start | bytes 196616 | tf_op jit(solution)/shard_map/ppermute | solution.py:302
  15.3 1.6 %collective-permute-start.4 = (bf16[8,16,1024]{2,1,0:T(8,128)(2,1)S(1)}, bf16[8,16,1024]{2,1,0:T(8,128)(2,1)S(1)}, u32[]{:S(2)}, u32[]{:S(2)}) collective-permute-start(bf16[8,16,1024]{2,1,0:T(8,128)(2,1)S(1)} %bitcast.28), channel_id=1, source_target_pairs={{0,8},{8,0},{1,9},{9,1},{2,10},{10,2},{3,11},{11,3},{4,12},{12,4},... | collective-permute-start | bytes 786440 | tf_op jit(solution)/shard_map/ppermute | solution.py:383
  20.3 4.1 %collective-permute-start.5 = (bf16[160,128]{1,0:T(8,128)(2,1)S(1)}, bf16[160,128]{1,0:T(8,128)(2,1)S(1)}, u32[]{:S(2)}, u32[]{:S(2)}) collective-permute-start(bf16[160,128]{1,0:T(8,128)(2,1)S(1)} %project.1.q_ref), channel_id=1, source_target_pairs={{0,1},{1,0},{2,3},{3,2},{4,5},{5,4},{6,7},{7,6},{8,9},{9,8},{10,11... | collective-permute-start | bytes 122888 | tf_op jit(solution)/shard_map/ppermute | solution.py:302
  24.4 6.9 %collective-permute-start.8 = (bf16[2,160,128]{2,1,0:T(8,128)(2,1)S(1)}, bf16[2,160,128]{2,1,0:T(8,128)(2,1)S(1)}, u32[]{:S(2)}, u32[]{:S(2)}) collective-permute-start(bf16[2,160,128]{2,1,0:T(8,128)(2,1)S(1)} %get-tuple-element.49.after_ref), channel_id=1, source_target_pairs={{0,6},{1,7},{2,4},{3,5},{4,2},{5,3},{6,0},{7,1},{8,14},{9,15},{10,... | collective-permute-start | bytes 245768 | tf_op jit(solution)/shard_map/ppermute | solution.py:302
  26.6 7.6 %collective-permute-start.7 = (bf16[2,160,128]{2,1,0:T(8,128)(2,1)S(1)}, bf16[2,160,128]{2,1,0:T(8,128)(2,1)S(1)}, u32[]{:S(2)}, u32[]{:S(2)}) collective-permute-start(bf16[2,160,128]{2,1,0:T(8,128)(2,1)S(1)} %get-tuple-element.49.after_ref), channel_id=1, source_target_pairs={{0,4},{1,5},{2,6},{3,7},{4,0},{5,1},{6,2},{7,3},{8,12},{9,13},{10,... | collective-permute-start | bytes 245768 | tf_op jit(solution)/shard_map/ppermute | solution.py:302
  26.6 7.6 %collective-permute-start.6 = (bf16[2,160,128]{2,1,0:T(8,128)(2,1)S(1)}, bf16[2,160,128]{2,1,0:T(8,128)(2,1)S(1)}, u32[]{:S(2)}, u32[]{:S(2)}) collective-permute-start(bf16[2,160,128]{2,1,0:T(8,128)(2,1)S(1)} %get-tuple-element.49.after_ref), channel_id=1, source_target_pairs={{0,2},{1,3},{2,0},{3,1},{4,6},{5,7},{6,4},{7,5},{8,10},{9,11},{10,... | collective-permute-start | bytes 245768 | tf_op jit(solution)/shard_map/ppermute | solution.py:302
  37.5 7.4 %collective-permute-start.9 = (f32[136,128]{1,0:T(8,128)S(1)}, f32[136,128]{1,0:T(8,128)S(1)}, u32[]{:S(2)}, u32[]{:S(2)}) collective-permute-start(f32[136,128]{1,0:T(8,128)S(1)} %get-tuple-element.30), channel_id=1, source_target_pairs={{0,1},{1,0},{2,3},{3,2},{4,5},{5,4},{6,7},{7,6},{8,9},{9,8},{10,11... | collective-permute-start | bytes 208904 | tf_op jit(solution)/shard_map/ppermute | solution.py:302
  39.0 8.0 %collective-permute-start.10 = (f32[136,128]{1,0:T(8,128)S(1)}, f32[136,128]{1,0:T(8,128)S(1)}, u32[]{:S(2)}, u32[]{:S(2)}) collective-permute-start(f32[136,128]{1,0:T(8,128)S(1)} %get-tuple-element.31), channel_id=1, source_target_pairs={{0,2},{1,3},{2,0},{3,1},{4,6},{5,7},{6,4},{7,5},{8,10},{9,11},{10,... | collective-permute-start | bytes 208904 | tf_op jit(solution)/shard_map/ppermute | solution.py:302
  39.0 9.6 %collective-permute-start.11 = (f32[136,128]{1,0:T(8,128)S(1)}, f32[136,128]{1,0:T(8,128)S(1)}, u32[]{:S(2)}, u32[]{:S(2)}) collective-permute-start(f32[136,128]{1,0:T(8,128)S(1)} %get-tuple-element.32), channel_id=1, source_target_pairs={{0,3},{1,2},{2,1},{3,0},{4,7},{5,6},{6,5},{7,4},{8,11},{9,10},{10,... | collective-permute-start | bytes 208904 | tf_op jit(solution)/shard_map/ppermute | solution.py:302
  41.0 10.4 %collective-permute-start.12 = (f32[136,128]{1,0:T(8,128)S(1)}, f32[136,128]{1,0:T(8,128)S(1)}, u32[]{:S(2)}, u32[]{:S(2)}) collective-permute-start(f32[136,128]{1,0:T(8,128)S(1)} %get-tuple-element.33), channel_id=1, source_target_pairs={{0,4},{1,5},{2,6},{3,7},{4,0},{5,1},{6,2},{7,3},{8,12},{9,13},{10,... | collective-permute-start | bytes 208904 | tf_op jit(solution)/shard_map/ppermute | solution.py:302
  41.7 11.5 %collective-permute-start.13 = (f32[136,128]{1,0:T(8,128)S(1)}, f32[136,128]{1,0:T(8,128)S(1)}, u32[]{:S(2)}, u32[]{:S(2)}) collective-permute-start(f32[136,128]{1,0:T(8,128)S(1)} %get-tuple-element.34), channel_id=1, source_target_pairs={{0,5},{1,4},{2,7},{3,6},{4,1},{5,0},{6,3},{7,2},{8,13},{9,12},{10,... | collective-permute-start | bytes 208904 | tf_op jit(solution)/shard_map/ppermute | solution.py:302
  44.9 8.3 %collective-permute-start.14 = (f32[136,128]{1,0:T(8,128)S(1)}, f32[136,128]{1,0:T(8,128)S(1)}, u32[]{:S(2)}, u32[]{:S(2)}) collective-permute-start(f32[136,128]{1,0:T(8,128)S(1)} %get-tuple-element.35), channel_id=1, source_target_pairs={{0,6},{1,7},{2,4},{3,5},{4,2},{5,3},{6,0},{7,1},{8,14},{9,15},{10,... | collective-permute-start | bytes 208904 | tf_op jit(solution)/shard_map/ppermute | solution.py:302
  47.0 7.1 %collective-permute-start.15 = (f32[136,128]{1,0:T(8,128)S(1)}, f32[136,128]{1,0:T(8,128)S(1)}, u32[]{:S(2)}, u32[]{:S(2)}) collective-permute-start(f32[136,128]{1,0:T(8,128)S(1)} %get-tuple-element.36), channel_id=1, source_target_pairs={{0,7},{1,6},{2,5},{3,4},{4,3},{5,2},{6,1},{7,0},{8,15},{9,14},{10,... | collective-permute-start | bytes 208904 | tf_op jit(solution)/shard_map/ppermute | solution.py:302
  56.9 6.8 %collective-permute-start.16 = (f32[136,128]{1,0:T(8,128)S(1)}, f32[136,128]{1,0:T(8,128)S(1)}, u32[]{:S(2)}, u32[]{:S(2)}) collective-permute-start(f32[136,128]{1,0:T(8,128)S(1)} %get-tuple-element.38), channel_id=1, source_target_pairs={{0,1},{1,0},{2,3},{3,2},{4,5},{5,4},{6,7},{7,6},{8,9},{9,8},{10,11... | collective-permute-start | bytes 208904 | tf_op jit(solution)/shard_map/ppermute | solution.py:302
  57.7 7.8 %collective-permute-start.17 = (f32[136,128]{1,0:T(8,128)S(1)}, f32[136,128]{1,0:T(8,128)S(1)}, u32[]{:S(2)}, u32[]{:S(2)}) collective-permute-start(f32[136,128]{1,0:T(8,128)S(1)} %get-tuple-element.39), channel_id=1, source_target_pairs={{0,2},{1,3},{2,0},{3,1},{4,6},{5,7},{6,4},{7,5},{8,10},{9,11},{10,... | collective-permute-start | bytes 208904 | tf_op jit(solution)/shard_map/ppermute | solution.py:302
  59.8 8.7 %collective-permute-start.18 = (f32[136,128]{1,0:T(8,128)S(1)}, f32[136,128]{1,0:T(8,128)S(1)}, u32[]{:S(2)}, u32[]{:S(2)}) collective-permute-start(f32[136,128]{1,0:T(8,128)S(1)} %get-tuple-element.40), channel_id=1, source_target_pairs={{0,3},{1,2},{2,1},{3,0},{4,7},{5,6},{6,5},{7,4},{8,11},{9,10},{10,... | collective-permute-start | bytes 208904 | tf_op jit(solution)/shard_map/ppermute | solution.py:302
  60.8 10.4 %collective-permute-start.19 = (f32[136,128]{1,0:T(8,128)S(1)}, f32[136,128]{1,0:T(8,128)S(1)}, u32[]{:S(2)}, u32[]{:S(2)}) collective-permute-start(f32[136,128]{1,0:T(8,128)S(1)} %get-tuple-element.41), channel_id=1, source_target_pairs={{0,4},{1,5},{2,6},{3,7},{4,0},{5,1},{6,2},{7,3},{8,12},{9,13},{10,... | collective-permute-start | bytes 208904 | tf_op jit(solution)/shard_map/ppermute | solution.py:302
  63.0 10.1 %collective-permute-start.20 = (f32[136,128]{1,0:T(8,128)S(1)}, f32[136,128]{1,0:T(8,128)S(1)}, u32[]{:S(2)}, u32[]{:S(2)}) collective-permute-start(f32[136,128]{1,0:T(8,128)S(1)} %get-tuple-element.42), channel_id=1, source_target_pairs={{0,5},{1,4},{2,7},{3,6},{4,1},{5,0},{6,3},{7,2},{8,13},{9,12},{10,... | collective-permute-start | bytes 208904 | tf_op jit(solution)/shard_map/ppermute | solution.py:302
  63.7 9.4 %collective-permute-start.21 = (f32[136,128]{1,0:T(8,128)S(1)}, f32[136,128]{1,0:T(8,128)S(1)}, u32[]{:S(2)}, u32[]{:S(2)}) collective-permute-start(f32[136,128]{1,0:T(8,128)S(1)} %get-tuple-element.43), channel_id=1, source_target_pairs={{0,6},{1,7},{2,4},{3,5},{4,2},{5,3},{6,0},{7,1},{8,14},{9,15},{10,... | collective-permute-start | bytes 208904 | tf_op jit(solution)/shard_map/ppermute | solution.py:302
  65.6 7.6 %collective-permute-start.22 = (f32[136,128]{1,0:T(8,128)S(1)}, f32[136,128]{1,0:T(8,128)S(1)}, u32[]{:S(2)}, u32[]{:S(2)}) collective-permute-start(f32[136,128]{1,0:T(8,128)S(1)} %get-tuple-element.44), channel_id=1, source_target_pairs={{0,7},{1,6},{2,5},{3,4},{4,3},{5,2},{6,1},{7,0},{8,15},{9,14},{10,... | collective-permute-start | bytes 208904 | tf_op jit(solution)/shard_map/ppermute | solution.py:302
  73.2 1.3 %collective-permute-start.23 = (bf16[16,1024]{1,0:T(8,128)(2,1)S(1)}, bf16[16,1024]{1,0:T(8,128)(2,1)S(1)}, u32[]{:S(2)}, u32[]{:S(2)}) collective-permute-start(bf16[16,1024]{1,0:T(8,128)(2,1)S(1)} %get-tuple-element.47), channel_id=1, source_target_pairs={{0,8},{8,0},{1,9},{9,1},{2,10},{10,2},{3,11},{11,3},{4,12},{12,4},... | collective-permute-start | bytes 98312 | tf_op jit(solution)/shard_map/ppermute | solution.py:515
  (18 other events, 330.4 us)
